TPU v7x, 32 devices: a whole 2x2x4 slice. The times are simulated.
32 devices in a mesh: dp: 2 (over core), seq: 16 (over z, y, x).
Axes of the slice: x: 2, y: 2, z: 4, core: 2. Of those that a mesh axis runs over, the one named last changes fastest.
Arguments:
- tokens: bfloat16 [32768, 768], P(('dp', 'seq')), may hold values from -6 to 6
- cotangent: bfloat16 [16384, 768], P(('dp', 'seq')), may hold values from -6 to 6
- lengths: int32 [256], replicated, may hold values from 1 to 256, 16384 in all
- w_query: float32 [768, 768], P('seq'), may hold values from -0.4375 to 0.4375
- b_query: float32 [768], P('seq'), may hold values from -3 to 3
- w_key: float32 [768, 768], P('seq'), may hold values from -0.21875 to 0.21875
- w_value: float32 [768, 768], P('seq'), may hold values from -0.21875 to 0.21875
- b_value: float32 [768], P('seq'), may hold values from -3 to 3
- w_output: float32 [768, 768], P('seq'), may hold values from -1.75 to 1.75
- b_output: float32 [768], P('seq'), may hold values from -3 to 3
- gain_attn: float32 [768], P('seq'), may hold values from 0.1 to 1.9
- shift_attn: float32 [768], P('seq'), may hold values from -3 to 3
- w_up: float32 [768, 3072], P('seq'), may hold values from -0.21875 to 0.21875
- b_up: float32 [3072], P('seq'), may hold values from -3 to 3
- w_down: float32 [3072, 768], P('seq'), may hold values from -0.109375 to 0.109375
- b_down: float32 [768], P('seq'), may hold values from -3 to 3
- gain_ffn: float32 [768], P('seq'), may hold values from 0.1 to 1.9
- shift_ffn: float32 [768], P('seq'), may hold values from -3 to 3
- distance_slope: float32 [12], replicated, may hold values from 0.004 to 0.08
Outputs:
- pooled_out: bfloat16 [16384, 768], P(('dp', 'seq'))
- grad_tokens: float32 [32768, 768], P(('dp', 'seq'))
- grad_w_query: float32 [768, 768], P('seq')
- grad_b_query: float32 [768], P('seq')
- grad_w_key: float32 [768, 768], P('seq')
- grad_w_value: float32 [768, 768], P('seq')
- grad_b_value: float32 [768], P('seq')
- grad_w_output: float32 [768, 768], P('seq')
- grad_b_output: float32 [768], P('seq')
- grad_gain_attn: float32 [768], P('seq')
- grad_shift_attn: float32 [768], P('seq')
- grad_w_up: float32 [768, 3072], P('seq')
- grad_b_up: float32 [3072], P('seq')
- grad_w_down: float32 [3072, 768], P('seq')
- grad_b_down: float32 [768], P('seq')
- grad_gain_ffn: float32 [768], P('seq')
- grad_shift_ffn: float32 [768], P('seq')
- grad_distance_slope: float32 [12], replicated
Inputs may be any that keep to these rules, and one draw needn't show every extreme that they name: Lengths count token pairs; all 256 lengths sum to 16384, so the rows fill the pack exactly.
All inputs are finite; a program needn't handle non-finite values.
Results may differ from a plain program's by a relative error of at most 0.015.
The roundings to bfloat16 on the way count: a program that leaves them out, or rounds other values in their place, can miss the bound.
Values may be sent and summed in bfloat16 or wider, within the bound.
No kernel may reach another device: no remote copies, remote signals or barrier semaphores. Data moves between devices by JAX's collectives and lax.ppermute only.
A program may use at most 384 MiB of HBM per device.

v0:
```python
import functools

import jax
import jax.numpy as jnp
from jax import lax
from jax.experimental import pallas as pl
from jax.experimental.pallas import tpu as pltpu
from jax.sharding import PartitionSpec as P

HD = 64
NB = 16
QB = 128
KC = 256
EPS = 1e-05
FAR = 1e12
BF = jnp.bfloat16
FL = jnp.float32


def rel_a(p):
    return (p & 1) * 8 + ((p >> 1) & 1) * 4 + ((p >> 2) & 1) * 2 + ((p >> 3) & 1)


def rel_b(p):
    return (p & 1) * 4 + ((p >> 1) & 1) * 8 + ((p >> 2) & 1) + ((p >> 3) & 1) * 2


def dot(a, b):
    return jnp.dot(a, b, preferred_element_type=FL)


def dot_t(a, b):
    return lax.dot_general(a, b, (((1,), (1,)), ((), ())), preferred_element_type=FL)


def t_dot(a, b):
    return lax.dot_general(a, b, (((0,), (0,)), ((), ())), preferred_element_type=FL)


def exchange(x, stride_a, stride_b):
    n = lax.axis_size("seq")
    pairs = [(s, s ^ stride_a) for s in range(n)] + [(n + s, n + (s ^ stride_b)) for s in range(n)]
    return lax.ppermute(x, ("dp", "seq"), pairs)


def swap_core(x):
    return lax.ppermute(x, "dp", [(0, 1), (1, 0)])


def add(*xs):
    total = xs[0].astype(FL)
    for x in xs[1:]:
        total = total + x.astype(FL)
    return total


def params(**kw):
    return pltpu.CompilerParams(vmem_limit_bytes=58 * 1024 * 1024, **kw)


def takes(us):
    return pl.CostEstimate(flops=us * 1150 * 10**6, transcendentals=0, bytes_accessed=us * 3600 * 10**3)


ANY = pl.BlockSpec(memory_space=pl.ANY)


def load_sets(ids, low, high, olow, ohigh, copies_a, copies_b):
    def start(a_refs, b_refs):
        for p in range(NB):
            copies_a(a_refs[p // 8].at[p % 8], ids[0] ^ rel_a(p), p)
            copies_b(b_refs[p // 8].at[p % 8], ids[0] ^ rel_b(p), p)

    @pl.when(ids[1] == 0)
    def _():
        start((low, high), (olow, ohigh))

    @pl.when(ids[1] != 0)
    def _():
        start((olow, ohigh), (low, high))


def wait_all(ref, sem):
    pltpu.make_async_copy(ref, ref, sem).wait()


def spread_matrix(rows, cols, rb):
    lanes = lax.broadcasted_iota(jnp.int32, (rows, cols), 1)
    return (lax.broadcasted_iota(jnp.int32, (rows, cols), 0) == lanes - rb * div_rb(lanes)).astype(FL).astype(BF)


def div_rb(x):
    return (x * 21846) >> 20


def qkv_kernel(
    ids, tok, low, high, olow, ohigh, q_out, k_out, v_out, kt_out, vt_out, pool_out, wq, wk, wv, vec_out, up_out, bias, x32, sems
):
    width = tok.shape[1]
    rb = width // NB

    @pl.when(pl.program_id(0) == 0)
    def _():
        def rows(r, n):
            return pl.ds(pl.multiple_of(r, 16), n)

        def copies_a(block, s, p):
            pltpu.make_async_copy(block.at[pl.ds(0, 48)], wq.at[rows(s * rb, 48)], sems.at[0]).start()
            pltpu.make_async_copy(block.at[pl.ds(48, 32)], wk.at[rows(s * rb, 32)], sems.at[1]).start()

        def copies_b(block, s, p):
            pltpu.make_async_copy(block.at[pl.ds(0, 16)], wk.at[rows(s * rb + 32, 16)], sems.at[1]).start()
            pltpu.make_async_copy(block.at[pl.ds(16, 48)], wv.at[rows(s * rb, 48)], sems.at[2]).start()
            pltpu.make_async_copy(block.at[pl.ds(64, 16)], bias.at[pl.ds(16 * p, 16)], sems.at[3]).start()

        load_sets(ids, low, high, olow, ohigh, copies_a, copies_b)
        wait_all(wq, sems.at[0])
        wait_all(wk, sems.at[1])
        wait_all(wv, sems.at[2])
        wait_all(bias, sems.at[3])
        parts = bias[:, 0:128]
        wide = dot(parts, spread_matrix(128, width, rb))
        block_of = div_rb(lax.broadcasted_iota(jnp.int32, (16, width), 1))
        total = jnp.zeros((16, width), FL)
        for p in range(NB):
            total = total + jnp.where(block_of == (ids[0] ^ rel_b(p)), wide[16 * p : 16 * p + 16], 0.0)
        vec_out[...] = total
        ff = up_out.shape[1]
        wide = dot(parts, spread_matrix(128, ff, rb))
        block_of = div_rb(lax.broadcasted_iota(jnp.int32, (16, ff), 1))
        row = lax.broadcasted_iota(jnp.int32, (16, ff), 0)
        block_of = jnp.where((row >= 8) & (row < 12), block_of - row + 8, -1)
        total = jnp.zeros((16, ff), FL)
        for p in range(NB):
            total = total + jnp.where(block_of == 4 * (ids[0] ^ rel_b(p)), wide[16 * p : 16 * p + 16], 0.0)
        up_out[...] = jnp.broadcast_to(jnp.sum(total, 0, keepdims=True), up_out.shape)

    pool_out[...] = project(tok[...], wq, wk, wv, vec_out, q_out, k_out, v_out, kt_out, vt_out, x32)


def project(x, wq, wk, wv, vec, q_out, k_out, v_out, kt_out, vt_out, x32):
    width = x.shape[1]
    half = x.shape[0] // 2
    k_out[...] = dot(x, wk[...]).astype(BF)
    v_out[...] = (dot(x, wv[...]) + vec[1:2]).astype(BF)
    for c in range(x.shape[0] // KC):
        kt_out[c] = k_out[KC * c : KC * c + KC].T
        vt_out[c] = v_out[KC * c : KC * c + KC].T
    pooled = []
    for j in range(width // 128):
        x32[j] = x[:, 128 * j : 128 * j + 128].astype(FL)
        pooled.append((x32[j, pl.ds(0, half, stride=2)] + x32[j, pl.ds(1, half, stride=2)]) * 0.5)
    pooled = jnp.concatenate(pooled, 1)
    q = (dot(pooled.astype(BF), wq[...]) + vec[0:1]).astype(BF)
    q_out[...] = (q.astype(FL) * HD**-0.5).astype(BF)
    return pooled


def qkv(ids, tokens, sets, ff):
    rows, width = tokens.shape
    step = 512
    whole = lambda i, *_: (0, 0)
    square = jax.ShapeDtypeStruct((width, width), BF)
    thin = pl.BlockSpec((step // 2, width), lambda i, *_: (i, 0))
    block = pl.BlockSpec((step, width), lambda i, *_: (i, 0))
    inner = pl.BlockSpec((step, width), lambda i, *_: (i + 1, 0))
    tall = pl.BlockSpec((step // KC, width, KC), lambda i, *_: (i + 1, 0, 0))
    return pl.pallas_call(
        qkv_kernel,
        name="qkv",
        cost_estimate=takes(9),
        grid_spec=pltpu.PrefetchScalarGridSpec(
            num_scalar_prefetch=1,
            grid=(rows // step,),
            in_specs=[block, ANY, ANY, ANY, ANY],
            out_specs=[thin, inner, inner, tall, tall, thin]
            + [pl.BlockSpec((width, width), whole)] * 3
            + [pl.BlockSpec((16, width), whole), pl.BlockSpec((8, ff), whole)],
            scratch_shapes=[
                pltpu.VMEM((16 * NB, width), BF),
                pltpu.VMEM((width // 128, step, 128), FL),
                pltpu.SemaphoreType.DMA((4,)),
            ],
        ),
        out_shape=[
            jax.ShapeDtypeStruct((rows // 2, width), BF),
            jax.ShapeDtypeStruct((2 * rows, width), BF),
            jax.ShapeDtypeStruct((2 * rows, width), BF),
            jax.ShapeDtypeStruct((2 * rows // KC, width, KC), BF),
            jax.ShapeDtypeStruct((2 * rows // KC, width, KC), BF),
            jax.ShapeDtypeStruct((rows // 2, width), FL),
            square,
            square,
            square,
            jax.ShapeDtypeStruct((16, width), FL),
            jax.ShapeDtypeStruct((8, ff), FL),
        ],
        compiler_params=params(),
    )(ids, tokens, *sets)


def halo_qkv_kernel(
    low_a, low_b, high_a, high_b, wq, wk, wv, vec, k, v, kt, vt, q_out, k_out, v_out, kt_out, vt_out, x32
):
    low = pl.program_id(0) == 0
    parts = [jnp.where(low, a[...], b[...]) for a, b in ((low_a, high_a), (low_b, high_b))]
    project(jnp.concatenate(parts, 0), wq, wk, wv, vec, q_out, k_out, v_out, kt_out, vt_out, x32)


def halo_qkv(low_a, low_b, high_a, high_b, wq, wk, wv, vec, k, v, kt, vt):
    rows, width = low_a.shape
    rows = 2 * rows
    full = lambda x: pl.BlockSpec(x.shape, lambda i: (0,) * len(x.shape))
    args = (low_a, low_b, high_a, high_b, wq, wk, wv, vec)
    edge = pl.BlockSpec((rows, width), lambda i: (3 * i, 0))
    tall = pl.BlockSpec((rows // KC, width, KC), lambda i: (3 * i, 0, 0))
    return pl.pallas_call(
        halo_qkv_kernel,
        name="halo_qkv",
        cost_estimate=takes(7),
        grid=(2,),
        in_specs=[full(x) for x in args] + [ANY] * 4,
        out_specs=[pl.BlockSpec((None, rows // 2, width), lambda i: (i, 0, 0)), edge, edge, tall, tall],
        out_shape=[jax.ShapeDtypeStruct((2, rows // 2, width), BF)]
        + [jax.ShapeDtypeStruct(x.shape, x.dtype) for x in (k, v, kt, vt)],
        input_output_aliases={8: 1, 9: 2, 10: 3, 11: 4},
        scratch_shapes=[pltpu.VMEM((width // 128, rows, 128), FL)],
        compiler_params=params(),
    )(*args, k, v, kt, vt)


def two_heads(x):
    lane = lax.broadcasted_iota(jnp.int32, x.shape, 1)
    zero = jnp.zeros_like(x)
    return jnp.concatenate([jnp.where(lane < HD, x, zero), jnp.where(lane < HD, zero, x)], 0)


def one_block(x):
    r = x.shape[1] // 2
    line = lax.broadcasted_iota(jnp.int32, (128, r), 0)
    return jnp.where(line < HD, x[:, :r], x[:, r:]).T


def distances(bounds, row, c):
    low = bounds[0:1, pl.ds(row, QB)]
    high = bounds[1:2, pl.ds(row, QB)]
    query = (2 * (row + lax.broadcasted_iota(jnp.int32, (KC, QB), 1))).astype(FL) + 0.5
    key = (c * KC + lax.broadcasted_iota(jnp.int32, (KC, QB), 0)).astype(FL)
    far = jnp.where((key >= low) & (key < high), jnp.abs(query - key), FAR)
    return jnp.concatenate([far, far], 1)


def fold(x, f):
    n = x.shape[0] // 8
    parts = [x[8 * i : 8 * i + 8] for i in range(n)]
    while len(parts) > 1:
        parts = [f(parts[2 * i], parts[2 * i + 1]) for i in range(len(parts) // 2)]
    return parts[0]


def slope_line(slopes, head):
    lane = lax.broadcasted_iota(jnp.int32, (1, 2 * QB), 1)
    return jnp.where(lane < QB, slopes[head], slopes[head + 1])


def forward_kernel(
    spans, slopes, q, k, vt, bounds, o_out, exact_out, lse_out, s_scr, q2, top, total, acc, rest
):
    pairs = q.shape[1] // 128
    head0 = pl.program_id(0) * 2 * pairs
    q_first = q.shape[0] // 2
    slope = [slope_line(slopes, head0 + 2 * j) for j in range(pairs)]

    def query_block(b, _):
        row = pl.multiple_of(q_first + b * QB, QB)
        out_rows = pl.ds(pl.multiple_of(b * QB, QB), QB)
        block = row // QB
        c0 = spans[block]
        c1 = spans[spans.shape[0] // 2 + block]
        for j in range(pairs):
            q2[j] = two_heads(q[out_rows, 128 * j : 128 * j + 128])
        top[...] = jnp.full(top.shape, -3e38, FL)
        total[...] = jnp.zeros(total.shape, FL)
        acc[...] = jnp.zeros(acc.shape, FL)
        rest[...] = jnp.zeros(rest.shape, FL)

        def score(c, _):
            far = distances(bounds, row, c)
            keys = pl.ds(pl.multiple_of(c * KC, KC), KC)
            for j in range(pairs):
                s = dot_t(k[keys, 128 * j : 128 * j + 128], q2[j]) - slope[j] * far
                s_scr[c - c0, j] = s
                top[j] = jnp.maximum(top[j], fold(s, jnp.maximum))
            return 0

        lax.fori_loop(c0, c1, score, 0)
        peak = [jnp.max(top[j], 0, keepdims=True) for j in range(pairs)]

        def exponent(c, _):
            for j in range(pairs):
                e = jnp.exp(s_scr[c - c0, j] - peak[j])
                s_scr[c - c0, j] = e
                total[j] = total[j] + fold(e, jnp.add)
            return 0

        lax.fori_loop(c0, c1, exponent, 0)
        inverse = []
        for j in range(pairs):
            l = jnp.sum(total[j], 0, keepdims=True)
            t = peak[j] + jnp.log(l)
            inverse.append(1.0 / l)
            lse_out[2 * j : 2 * j + 1, out_rows] = t[:, :QB]
            lse_out[2 * j + 1 : 2 * j + 2, out_rows] = t[:, QB:]

        def attend(c, _):
            for j in range(pairs):
                p = s_scr[c - c0, j] * inverse[j]
                high = p.astype(BF)
                low = (p - high.astype(FL)).astype(BF)
                values = vt[c, 128 * j : 128 * j + 128]
                acc[j] = acc[j] + dot(values, high)
                rest[j] = rest[j] + dot(values, low)
            return 0

        lax.fori_loop(c0, c1, attend, 0)
        for j in range(pairs):
            cols = slice(128 * j, 128 * j + 128)
            o_out[out_rows, cols] = one_block(acc[j]).astype(BF)
            exact_out[out_rows, cols] = one_block(acc[j] + rest[j])
        return 0

    lse_out[...] = jnp.zeros(lse_out.shape, FL)
    lax.fori_loop(0, o_out.shape[0] // QB, query_block, 0)


def attend_forward(spans, slopes, q, k, vt, bounds):
    own, width = q.shape
    wide = width // 2
    pairs = wide // 128
    keys = k.shape[0]
    chunks = keys // KC
    col = lambda i, *_: (0, i)
    return pl.pallas_call(
        forward_kernel,
        name="attend_forward",
        cost_estimate=takes(30),
        grid_spec=pltpu.PrefetchScalarGridSpec(
            num_scalar_prefetch=2,
            grid=(2,),
            in_specs=[
                pl.BlockSpec((own, wide), col),
                pl.BlockSpec((keys, wide), col),
                pl.BlockSpec((chunks, wide, KC), lambda i, *_: (0, i, 0)),
                pl.BlockSpec(bounds.shape, lambda i, *_: (0, 0)),
            ],
            out_specs=[
                pl.BlockSpec((own, wide), col),
                pl.BlockSpec((own, wide), col),
                pl.BlockSpec((8, own), lambda i, *_: (i, 0)),
            ],
            scratch_shapes=[
                pltpu.VMEM((chunks, pairs, KC, 2 * QB), FL),
                pltpu.VMEM((pairs, 2 * QB, 128), BF),
                pltpu.VMEM((pairs, 8, 2 * QB), FL),
                pltpu.VMEM((pairs, 8, 2 * QB), FL),
                pltpu.VMEM((pairs, 128, 2 * QB), FL),
                pltpu.VMEM((pairs, 128, 2 * QB), FL),
            ],
        ),
        out_shape=[
            jax.ShapeDtypeStruct((own, width), BF),
            jax.ShapeDtypeStruct((own, width), FL),
            jax.ShapeDtypeStruct((16, own), FL),
        ],
        compiler_params=params(),
    )(spans, slopes, q, k, vt, bounds)


def pieces(x):
    out = []
    for _ in range(3):
        y = x.astype(BF).astype(FL)
        out.append(y)
        x = x - y
    return out


def key_lines(side, kind):
    lane = lax.broadcasted_iota(jnp.int32, (KC, 128), 1)
    key = lax.broadcasted_iota(jnp.int32, (KC, 128), 0).astype(FL)
    x = jnp.where(lane < 3, 1.0, jnp.where(lane < 6, -side, jnp.where(lane < 9, side * key, 0.0)))
    return jnp.where(lane == kind, 1.0, x) if kind else x


def chunk_lines(base, away, side, limit):
    lane = lax.broadcasted_iota(jnp.int32, (KC, 128), 1)
    key = lax.broadcasted_iota(jnp.int32, (KC, 128), 0).astype(FL) + KC * away
    other = jnp.where(side * key < side * limit, 1.0, 0.0)
    x = base + jnp.where((lane >= 9) & (lane < 12), side * KC * away, 0.0)
    return jnp.where(lane == 12, other, x).astype(BF)


def value_lines():
    lane = lax.broadcasted_iota(jnp.int32, (KC, 128), 1)
    return (lane < 3).astype(FL).astype(BF)


def query_rows(lse, slope, spots, out_left, out_right):
    one = jnp.ones_like(lse)
    rows = pieces(-lse) + pieces(slope * spots) + pieces(slope * one) * 2
    rows += [-FAR * one, -FAR * out_left, -FAR * out_right, 0.0 * one]
    return jnp.concatenate(rows, 0).astype(BF)


def two_heads_t(x):
    line = lax.broadcasted_iota(jnp.int32, x.shape, 0)
    zero = jnp.zeros_like(x)
    return jnp.concatenate([jnp.where(line < HD, x, zero), jnp.where(line < HD, zero, x)], 1)


def block_setup(bounds, row):
    low = bounds[0:1, pl.ds(row, QB)]
    high = bounds[1:2, pl.ds(row, QB)]
    first = low[:, 0:1]
    last = high[:, QB - 1 : QB]
    base = (2 * row).astype(FL) if hasattr(row, "astype") else float(2 * row)
    out_left = jnp.where(low == first, 0.0, 1.0)
    out_right = jnp.where(high == last, 0.0, 1.0)
    spots = 2.0 * lax.broadcasted_iota(jnp.int32, (1, QB), 1).astype(FL) + 0.5
    return low - base, high - base, first - base, last - base - 0.5, twice(out_left), twice(out_right), twice(spots)


def twice(x):
    return jnp.concatenate([x, x], 1)


def fill_queries(j, q, da, lse, delta, slope, setup, q2, da2, qt, dat):
    out_left, out_right, spots = setup[4:]
    q2[j] = two_heads(q)
    da2[j] = two_heads(da)
    qt[j, 0:128] = two_heads_t(q.T)
    dat[j, 0:128] = two_heads_t(da.T)
    qt[j, 128:144] = query_rows(lse, slope, spots, out_left, out_right)
    rows = pieces(-delta) + [jnp.zeros((13, 2 * QB), FL)]
    dat[j, 128:144] = jnp.concatenate(rows, 0).astype(BF)


def own_kernel(
    spans, slopes, q, k, v, kt, da, stats, bounds, dq_out, dk, dv, slope_out, q2, da2, qt, dat, dq2, sl, base
):
    pairs = q.shape[1] // 128
    head0 = pl.program_id(0) * 2 * pairs
    total_blocks = bounds.shape[1] // QB
    quarter = k.shape[0] // KC // 4
    first = total_blocks // 4
    slope = [slope_line(slopes, head0 + 2 * j) for j in range(pairs)]
    dk[...] = jnp.zeros(dk.shape, FL)
    dv[...] = jnp.zeros(dv.shape, FL)
    sl[...] = jnp.zeros(sl.shape, FL)
    qt[...] = jnp.zeros(qt.shape, BF)
    dat[...] = jnp.zeros(dat.shape, BF)
    line = lax.broadcasted_iota(jnp.int32, (16, KC), 0)
    spot = lax.broadcasted_iota(jnp.int32, (16, KC), 1).astype(FL)
    extra = jnp.where(line == 0, 1.0, jnp.where(line == 1, spot, 0.0)).astype(BF)
    base[0] = key_lines(1.0, 13)
    base[1] = key_lines(-1.0, 14)
    own_lines = key_lines(1.0, 0).astype(BF)
    ones = value_lines()

    def query_block(b, _):
        block = first + b
        row = pl.multiple_of(block * QB, QB)
        rows = pl.ds(pl.multiple_of(b * QB, QB), QB)
        c0 = spans[block]
        c1 = spans[total_blocks + block]
        setup = block_setup(bounds, row)
        low, high, limit_left, limit_right = setup[:4]
        spots = setup[6]
        for j in range(pairs):
            cols = slice(128 * j, 128 * j + 128)
            h = 2 * j
            lse = jnp.concatenate([stats[h : h + 1, rows], stats[h + 1 : h + 2, rows]], 1)
            delta = jnp.concatenate([stats[8 + h : 9 + h, rows], stats[9 + h : 10 + h, rows]], 1)
            fill_queries(j, q[rows, cols], da[rows, cols], lse, delta, slope[j], setup, q2, da2, qt, dat)
        dq2[...] = jnp.zeros(dq2.shape, FL)

        def step(c, lines, side, away, grads, wide):
            keys = pl.ds(pl.multiple_of(c * KC, KC), KC)
            col = [slice(128 * j, 128 * j + 128) for j in range(pairs)]
            s = [dot(jnp.concatenate([k[keys, col[j]], lines], 1), qt[j]) for j in range(pairs)]
            dp = [dot(jnp.concatenate([v[keys, col[j]], ones], 1), dat[j]) for j in range(pairs)]
            if wide is not None:
                s = [s[j] - slope[j] * wide for j in range(pairs)]
            p = [jnp.exp(x) for x in s]
            ds = [(p[j] * dp[j]).astype(BF) for j in range(pairs)]
            if grads:
                mine = pl.ds(pl.multiple_of((c - quarter) * KC, KC), KC)
                new_v = [dot(p[j].astype(BF), da2[j]) for j in range(pairs)]
                new_k = [dot(ds[j], q2[j]) for j in range(pairs)]
            r = [dot(jnp.concatenate([kt[c, col[j]], extra], 0), ds[j]) for j in range(pairs)]
            for j in range(pairs):
                if grads:
                    dv[mine, col[j]] = dv[mine, col[j]] + new_v[j]
                    dk[mine, col[j]] = dk[mine, col[j]] + new_k[j]
                dq2[j] = dq2[j] + r[j][0:128]
                part = side * ((spots - KC * away) * r[j][128:129] - r[j][129:130])
                if wide is not None:
                    part = part + jnp.sum(ds[j].astype(FL) * wide, 0, keepdims=True)
                sl[j] = sl[j] + part

        key = lax.broadcasted_iota(jnp.int32, (KC, QB), 0).astype(FL)
        over = 2.0 * jnp.maximum(key - spots[:, :QB], 0.0)
        wide = twice(jnp.where((key >= low) & (key < high), over, FAR))
        step(block, own_lines, 1.0, 0.0, True, wide)

        def other(c, grads):
            before = c < block
            side = jnp.where(before, 1.0, -1.0)
            away = (c - block).astype(FL)
            limit = jnp.where(before, limit_left, limit_right)
            step(c, chunk_lines(base[jnp.where(before, 0, 1)], away, side, limit), side, away, grads, None)

        def inside(i, _):
            other(jnp.where(i < block, i, i + 1), True)
            return 0

        left = jnp.maximum(jnp.minimum(c1, quarter) - c0, 0)
        right0 = jnp.maximum(c0, 3 * quarter)

        def outside(i, _):
            other(jnp.where(i < left, c0 + i, right0 + i - left), False)
            return 0

        lax.fori_loop(jnp.maximum(c0, quarter), jnp.minimum(c1, 3 * quarter) - 1, inside, 0)
        lax.fori_loop(0, left + jnp.maximum(c1 - right0, 0), outside, 0)
        for j in range(pairs):
            dq_out[rows, 128 * j : 128 * j + 128] = (one_block(dq2[j]) * HD**-0.5).astype(BF)
        return 0

    lax.fori_loop(0, da.shape[0] // QB, query_block, 0)
    slope_out[...] = jnp.zeros(slope_out.shape, FL)
    for j in range(pairs):
        slope_out[8 * j : 8 * j + 1] = sl[j]


def attend_own(spans, slopes, q, k, v, kt, da, stats, bounds):
    own, width = q.shape
    wide = width // 2
    pairs = wide // 128
    keys = k.shape[0]
    chunks = keys // KC
    col = lambda i, *_: (0, i)
    zero = lambda i, *_: (0, 0)
    return pl.pallas_call(
        own_kernel,
        name="attend_own",
        cost_estimate=takes(30),
        grid_spec=pltpu.PrefetchScalarGridSpec(
            num_scalar_prefetch=2,
            grid=(2,),
            in_specs=[
                pl.BlockSpec((own, wide), col),
                pl.BlockSpec((keys, wide), col),
                pl.BlockSpec((keys, wide), col),
                pl.BlockSpec((chunks, wide, KC), lambda i, *_: (0, i, 0)),
                pl.BlockSpec((own, wide), col),
                pl.BlockSpec((16, own), lambda i, *_: (i, 0)),
                pl.BlockSpec(bounds.shape, zero),
            ],
            out_specs=[
                pl.BlockSpec((own, wide), col),
                pl.BlockSpec((keys // 2, wide), col),
                pl.BlockSpec((keys // 2, wide), col),
                pl.BlockSpec((8 * pairs, 2 * QB), lambda i, *_: (i, 0)),
            ],
            scratch_shapes=[
                pltpu.VMEM((pairs, 2 * QB, 128), BF),
                pltpu.VMEM((pairs, 2 * QB, 128), BF),
                pltpu.VMEM((pairs, 256, 2 * QB), BF),
                pltpu.VMEM((pairs, 256, 2 * QB), BF),
                pltpu.VMEM((pairs, 128, 2 * QB), FL),
                pltpu.VMEM((pairs, 1, 2 * QB), FL),
                pltpu.VMEM((2, KC, 128), FL),
            ],
        ),
        out_shape=[
            jax.ShapeDtypeStruct((own, width), BF),
            jax.ShapeDtypeStruct((keys // 2, width), FL),
            jax.ShapeDtypeStruct((keys // 2, width), FL),
            jax.ShapeDtypeStruct((16 * pairs, 2 * QB), FL),
        ],
        compiler_params=params(),
    )(spans, slopes, q, k, v, kt, da, stats, bounds)


def halo_kernel(
    spans, slopes, q, k, v, low_pay, high_pay, bounds, dk0, dv0, dk_out, dv_out, q2, da2, qt, dat, st, dk, dv
):
    width = q.shape[2]
    pairs = width // 128
    total_blocks = bounds.shape[1] // QB
    quarter = k.shape[0] // KC // 4
    count = low_pay.shape[0] // QB
    dk[...] = dk0[...]
    dv[...] = dv0[...]
    qt[...] = jnp.zeros(qt.shape, BF)
    dat[...] = jnp.zeros(dat.shape, BF)
    ones = value_lines()
    for side, pay in enumerate((low_pay, high_pay)):
        x = pay[:, width : width + 128].astype(FL)
        st[side] = (x + pltpu.roll(x, 96, 1) + pltpu.roll(x, 64, 1)).T

    def query_block(i, _):
        side = i // count
        nth = i - side * count
        block = jnp.where(side == 0, i, total_blocks - 2 * count + i)
        row = pl.multiple_of(block * QB, QB)
        rows = pl.ds(pl.multiple_of(nth * QB, QB), QB)
        c0 = spans[block]
        c1 = spans[total_blocks + block]

        @pl.when(c0 < c1)
        def _():
            setup = block_setup(bounds, row)
            limit = jnp.where(side == 0, setup[3], setup[2])
            sign = jnp.where(side == 0, -1.0, 1.0)
            base = jnp.where(side == 0, key_lines(-1.0, 14), key_lines(1.0, 13))
            for j in range(pairs):
                cols = slice(128 * j, 128 * j + 128)
                h = 2 * j
                at = 16 * (h // (width // 128)) + h % (width // 128)
                lse = jnp.concatenate([st[side, at : at + 1, rows], st[side, at + 1 : at + 2, rows]], 1)
                delta = jnp.concatenate([st[side, at + 8 : at + 9, rows], st[side, at + 9 : at + 10, rows]], 1)
                d = jnp.where(side == 0, low_pay[rows, cols], high_pay[rows, cols])
                fill_queries(
                    j, q[side, rows, cols], d, lse, delta, slope_line(slopes, h), setup, q2, da2, qt, dat
                )

            def step(c, _):
                keys = pl.ds(pl.multiple_of(c * KC, KC), KC)
                mine = pl.ds(pl.multiple_of((c - quarter) * KC, KC), KC)
                lines = chunk_lines(base, (c - block).astype(FL), sign, limit)
                for g in range(0, pairs, 3):
                    js = range(g, g + 3)
                    col = {j: slice(128 * j, 128 * j + 128) for j in js}
                    p = [jnp.exp(dot(jnp.concatenate([k[keys, col[j]], lines], 1), qt[j])) for j in js]
                    dp = [dot(jnp.concatenate([v[keys, col[j]], ones], 1), dat[j]) for j in js]
                    new_v = [dot(x.astype(BF), da2[j]) for x, j in zip(p, js)]
                    new_k = [dot((x * y).astype(BF), q2[j]) for x, y, j in zip(p, dp, js)]
                    for j, x, y in zip(js, new_v, new_k):
                        dv[mine, col[j]] = dv[mine, col[j]] + x
                        dk[mine, col[j]] = dk[mine, col[j]] + y
                return 0

            lax.fori_loop(c0, c1, step, 0)

        return 0

    lax.fori_loop(0, 2 * count, query_block, 0)
    dk_out[...] = dk[...].astype(BF)
    dv_out[...] = dv[...].astype(BF)


def attend_halo(spans, slopes, q, k, v, low_pay, high_pay, bounds, dk0, dv0):
    width = q.shape[2]
    pairs = width // 128
    keys = dk0.shape[0]
    full = lambda x: pl.BlockSpec(x.shape, lambda i, *_: (0,) * len(x.shape))
    shape = jax.ShapeDtypeStruct((keys, width), BF)
    return pl.pallas_call(
        halo_kernel,
        name="attend_halo",
        cost_estimate=takes(12),
        grid_spec=pltpu.PrefetchScalarGridSpec(
            num_scalar_prefetch=2,
            grid=(1,),
            in_specs=[full(x) for x in (q, k, v, low_pay, high_pay, bounds, dk0, dv0)],
            out_specs=[full(shape), full(shape)],
            scratch_shapes=[
                pltpu.VMEM((pairs, 2 * QB, 128), BF),
                pltpu.VMEM((pairs, 2 * QB, 128), BF),
                pltpu.VMEM((pairs, 256, 2 * QB), BF),
                pltpu.VMEM((pairs, 256, 2 * QB), BF),
                pltpu.VMEM((2, 128, low_pay.shape[0]), FL),
                pltpu.VMEM((keys, width), FL),
                pltpu.VMEM((keys, width), FL),
            ],
        ),
        out_shape=[shape, shape],
        compiler_params=params(),
    )(spans, slopes, q, k, v, low_pay, high_pay, bounds, dk0, dv0)


def normalize(z):
    centred = z - jnp.mean(z, -1, keepdims=True)
    scale = lax.rsqrt(jnp.mean(centred * centred, -1, keepdims=True) + EPS)
    return centred * scale, scale


def normalize_back(d, unit, scale):
    return scale * (d - jnp.mean(d, -1, keepdims=True) - unit * jnp.mean(d * unit, -1, keepdims=True))


def rows_sum(x):
    return jnp.sum(x, 0, keepdims=True)


def middle_kernel(
    ids,
    pool,
    att,
    exact,
    lse,
    cot,
    vec,
    upb,
    low,
    high,
    olow,
    ohigh,
    out,
    pay,
    stats,
    mixed,
    gvec,
    gup,
    keep,
    send,
    wo,
    w1,
    w2,
    active,
    slope,
    unit1,
    hid,
    hid_low,
    z,
    d2,
    dw1,
    dw2,
    dwo,
    sems,
):
    n, width = att.shape
    rb = width // NB
    fb = w2.shape[0] // NB
    parts = w1.shape[0]

    def rows(r, size):
        return pl.ds(pl.multiple_of(r, 16), size)

    def copies_a(block, s, p):
        pltpu.make_async_copy(block.at[pl.ds(192, 32)], wo.at[rows(s * rb, 32)], sems.at[0]).start()
        pltpu.make_async_copy(block.at[pl.ds(0, 192)], w2.at[rows(s * fb, 192)], sems.at[2]).start()

    def copies_b(block, s, p):
        pltpu.make_async_copy(block.at[pl.ds(192, 16)], wo.at[rows(s * rb + 32, 16)], sems.at[0]).start()
        for c in range(parts):
            pltpu.make_async_copy(block.at[pl.ds(48 * c, 48)], w1.at[c, rows(s * rb, 48)], sems.at[1]).start()

    load_sets(ids, low, high, olow, ohigh, copies_a, copies_b)
    wait_all(wo, sems.at[0])
    z[...] = dot(att[...], wo[...])
    rc = 128

    def row_loop(f):
        def body(i, _):
            f(pl.ds(pl.multiple_of(i * rc, rc), rc), i)
            return 0

        lax.fori_loop(0, n // rc, body, 0)

    def first_norm(r, i):
        unit, scale = normalize(pool[r, :] + z[r, :] + vec[2:3])
        h = unit * vec[3:4] + vec[4:5]
        unit1[r, :] = unit
        d2[r, 0:128] = jnp.broadcast_to(scale, (rc, 128))
        hid[r, :] = h
        hid_low[r, :] = h.astype(BF)

    row_loop(first_norm)
    wait_all(w1, sems.at[1])
    wait_all(w2, sems.at[2])
    c0 = 0.7978845608028654

    def up(c, _):
        inner = dot(hid_low[...], w1[c]) + upb[pl.ds(0, 1), pl.ds(pl.multiple_of(c * width, 128), width)]
        sq = inner * inner
        t = jnp.tanh(c0 * (inner + 0.044715 * (inner * sq)))
        cdf = 0.5 * (1.0 + t)
        active[c] = (inner * cdf).astype(BF)
        slope[c] = cdf + inner * (0.5 * (1.0 - t * t)) * (c0 + (3 * 0.044715 * c0) * sq)
        part = dot(active[c], w2[pl.ds(pl.multiple_of(c * width, 128), width), :])
        z[...] = jnp.where(c == 0, part, z[...] + part)
        return 0

    lax.fori_loop(0, parts, up, 0)
    gvec[...] = jnp.zeros(gvec.shape, FL)

    def second_norm(r, i):
        unit, scale = normalize(hid[r, :] + (z[r, :] + vec[5:6]))
        out[r, :] = (unit * vec[6:7] + vec[7:8]).astype(BF)
        dy = cot[r, :].astype(FL)
        gvec[6:7] = gvec[6:7] + rows_sum(dy * unit)
        gvec[7:8] = gvec[7:8] + rows_sum(dy)
        d = normalize_back(dy * vec[6:7], unit, scale)
        hid[r, :] = d
        d_low = d.astype(BF)
        att_like[r, :] = d_low
        gvec[5:6] = gvec[5:6] + rows_sum(d_low.astype(FL))

    att_like = pay.at[:, 0:width]
    scale1 = d2[:, 0:1]
    row_loop(second_norm)
    z[...] = jnp.zeros(z.shape, FL)

    def down(c, _):
        ffn = pay[:, 0:width]
        far = pl.ds(pl.multiple_of(c * width, 128), width)
        d_inner = (dot_t(ffn, w2[far, :]) * slope[c]).astype(BF)
        gup[:, far] = jnp.broadcast_to(rows_sum(d_inner.astype(FL)), (8, width))
        dw2[far, :] = t_dot(active[c], ffn).astype(BF)
        dw1[c] = t_dot(hid_low[...], d_inner).astype(BF)
        z[...] = z[...] + dot_t(d_inner, w1[c])
        return 0

    lax.fori_loop(0, parts, down, 0)

    def store_sets(a_ref, b_ref):
        for p in range(NB):
            s = ids[0] ^ rel_a(p)
            pltpu.make_async_copy(dw2.at[rows(s * fb, 192)], a_ref.at[p, pl.ds(0, 192)], sems.at[3]).start()
            s = ids[0] ^ rel_b(p)
            for c in range(parts):
                pltpu.make_async_copy(
                    dw1.at[c, rows(s * rb, 48)], b_ref.at[p, pl.ds(48 * c, 48)], sems.at[3]
                ).start()

    @pl.when(ids[1] == 0)
    def _():
        store_sets(keep, send)

    @pl.when(ids[1] != 0)
    def _():
        store_sets(send, keep)

    def first_back(r, i):
        unit = unit1[r, :]
        d = hid[r, :] + z[r, :]
        gvec[3:4] = gvec[3:4] + rows_sum(d * unit)
        gvec[4:5] = gvec[4:5] + rows_sum(d)
        d = normalize_back(d * vec[3:4], unit, d2[r, 0:1])
        mixed[r, :] = d
        d_low = d.astype(BF)
        hid_low[r, :] = d_low
        gvec[2:3] = gvec[2:3] + rows_sum(d_low.astype(FL))

    row_loop(first_back)
    dwo[...] = t_dot(att[...], hid_low[...]).astype(BF)

    def store_wo(a_ref, b_ref):
        for p in range(NB):
            s = ids[0] ^ rel_a(p)
            pltpu.make_async_copy(dwo.at[rows(s * rb, 32)], a_ref.at[p, pl.ds(192, 32)], sems.at[3]).start()
            s = ids[0] ^ rel_b(p)
            pltpu.make_async_copy(dwo.at[rows(s * rb + 32, 16)], b_ref.at[p, pl.ds(192, 16)], sems.at[3]).start()
            pltpu.make_async_copy(dwo.at[rows(s * rb + 32, 16)], b_ref.at[p, pl.ds(208, 16)], sems.at[3]).start()

    @pl.when(ids[1] == 0)
    def _():
        store_wo(keep, send)

    @pl.when(ids[1] != 0)
    def _():
        store_wo(send, keep)

    z[...] = dot_t(hid_low[...], wo[...])
    heads = width // HD
    head_of = lax.broadcasted_iota(jnp.int32, (16, width), 1) // HD
    head_of = jnp.where(head_of < heads // 2, head_of, head_of - heads // 2 + 8)
    pick = (head_of == lax.broadcasted_iota(jnp.int32, (16, width), 0)).astype(FL).astype(BF)
    stats[0:8, :] = lse[0:8, :]
    stats[16:24, :] = lse[8:16, :]

    def last(r, i):
        d_low = z[r, :].astype(BF)
        pay[r, 0:width] = d_low
        prod = d_low.astype(FL) * exact[r, :]
        delta = jnp.zeros((16, rc), FL)
        for _ in range(3):
            piece = prod.astype(BF)
            delta = delta + dot_t(pick, piece)
            prod = prod - piece.astype(FL)
        stats[8:16, r] = delta[0:8]
        stats[24:32, r] = delta[8:16]

    row_loop(last)
    st = stats[...].T
    pieces = []
    for _ in range(3):
        piece = st.astype(BF).astype(FL)
        pieces.append(piece)
        st = st - piece
    pieces.append(jnp.zeros_like(st))
    pay[:, width:] = jnp.concatenate(pieces, 1).astype(BF)
    wait_all(keep, sems.at[3])
    wait_all(send, sems.at[3])


def middle(ids, pool, att, exact, lse, cot, vec, upb, sets, set_rows):
    n, width = pool.shape
    ff = upb.shape[1]
    parts = ff // width
    whole = lambda i, *_: (0, 0)
    full = lambda x: pl.BlockSpec(x.shape, whole)
    shapes = [
        jax.ShapeDtypeStruct((n, width), BF),
        jax.ShapeDtypeStruct((n, width + 128), BF),
        jax.ShapeDtypeStruct((32, n), FL),
        jax.ShapeDtypeStruct((n, width), FL),
        jax.ShapeDtypeStruct((8, width), FL),
        jax.ShapeDtypeStruct((8, ff), FL),
    ]
    big = jax.ShapeDtypeStruct((NB, set_rows, width), BF)
    return pl.pallas_call(
        middle_kernel,
        name="middle",
        cost_estimate=takes(36),
        grid_spec=pltpu.PrefetchScalarGridSpec(
            num_scalar_prefetch=1,
            grid=(1,),
            in_specs=[full(pool)]
            + [full(x) for x in (att, exact, lse, cot, vec, upb)]
            + [ANY] * 4,
            out_specs=[full(x) for x in shapes] + [ANY, ANY],
            scratch_shapes=[
                pltpu.VMEM((width, width), BF),
                pltpu.VMEM((parts, width, width), BF),
                pltpu.VMEM((ff, width), BF),
                pltpu.VMEM((parts, n, width), BF),
                pltpu.VMEM((parts, n, width), FL),
                pltpu.VMEM((n, width), FL),
                pltpu.VMEM((n, width), FL),
                pltpu.VMEM((n, width), BF),
                pltpu.VMEM((n, width), FL),
                pltpu.VMEM((n, 128), FL),
                pltpu.VMEM((parts, width, width), BF),
                pltpu.VMEM((ff, width), BF),
                pltpu.VMEM((width, width), BF),
                pltpu.SemaphoreType.DMA((4,)),
            ],
        ),
        out_shape=shapes + [big, big],
        compiler_params=params(),
    )(ids, pool, att, exact, lse, cot, vec, upb, *sets)


def weights_kernel(ids, pool, tok, dq, dk, dv, gvec, gup, sl, keep, send, dwq, dwk, dwv, bias, tt, sems):
    width = tok.shape[1]
    ff = gup.shape[1]
    rb = width // NB
    tt[...] = tok[...].T
    dwq[...] = t_dot(pool[...].astype(BF), dq[...]).astype(BF)

    def columns(c, _):
        cols = pl.ds(pl.multiple_of(c * 256, 256), 256)
        dwk[:, cols] = dot(tt[...], dk[:, cols]).astype(BF)
        dwv[:, cols] = dot(tt[...], dv[:, cols]).astype(BF)
        return 0

    lax.fori_loop(0, width // 256, columns, 0)

    def rows(r, size):
        return pl.ds(pl.multiple_of(r, 16), size)

    def go(src, dst):
        pltpu.make_async_copy(src, dst, sems.at[0]).start()

    def store_sets(a_ref, b_ref):
        for p in range(NB):
            s = ids[0] ^ rel_a(p)
            go(dwq.at[rows(s * rb, 48)], a_ref.at[p, pl.ds(0, 48)])
            go(dwk.at[rows(s * rb, 32)], a_ref.at[p, pl.ds(48, 32)])
            s = ids[0] ^ rel_b(p)
            go(dwk.at[rows(s * rb + 32, 16)], b_ref.at[p, pl.ds(0, 16)])
            go(dwv.at[rows(s * rb, 48)], b_ref.at[p, pl.ds(16, 48)])

    @pl.when(ids[1] == 0)
    def _():
        store_sets(keep, send)

    @pl.when(ids[1] != 0)
    def _():
        store_sets(send, keep)

    row = lax.broadcasted_iota(jnp.int32, (16, width), 0)
    g = jnp.concatenate([gvec[...], jnp.zeros((8, width), FL)], 0)
    g = jnp.where(row == 0, rows_sum(dq[...].astype(FL)), g)
    g = jnp.where(row == 1, rows_sum(dv[...].astype(FL)), g)
    block_of = div_rb(lax.broadcasted_iota(jnp.int32, (16, width), 1))
    parts = []
    for p in range(NB):
        parts.append(jnp.where(block_of == (ids[0] ^ rel_b(p)), g, 0.0).astype(BF))
    total = dot_t(jnp.concatenate(parts, 0), spread_matrix(128, width, rb))
    row = lax.broadcasted_iota(jnp.int32, (16, ff), 0)
    block_of = div_rb(lax.broadcasted_iota(jnp.int32, (16, ff), 1))
    block_of = jnp.where((row >= 8) & (row < 12), block_of - row + 8, -1)
    up = jnp.concatenate([gup[...], gup[...]], 0)
    parts = []
    for p in range(NB):
        parts.append(jnp.where(block_of == 4 * (ids[0] ^ rel_b(p)), up, 0.0).astype(BF))
    total = total + dot_t(jnp.concatenate(parts, 0), spread_matrix(128, ff, rb))
    line = jnp.zeros((1, 128), FL)
    lane = lax.broadcasted_iota(jnp.int32, (1, 128), 1)
    for j in range(sl.shape[0] // 8):
        for i in range(2):
            value = jnp.sum(sl[8 * j : 8 * j + 1, QB * i : QB * i + QB], 1, keepdims=True)
            line = jnp.where(lane == 2 * j + i, -value, line)
    row = lax.broadcasted_iota(jnp.int32, (16 * NB, 128), 0)
    total = jnp.where((row & 15) == 12, line, total)
    bias[...] = jnp.zeros(bias.shape, BF)
    bias[:, 0:128] = total.astype(BF)

    def store_bias(b_ref):
        for p in range(NB):
            go(bias.at[pl.ds(16 * p, 16)], b_ref.at[p, pl.ds(64, 16)])

    @pl.when(ids[1] == 0)
    def _():
        store_bias(send)

    @pl.when(ids[1] != 0)
    def _():
        store_bias(keep)

    wait_all(keep, sems.at[0])
    wait_all(send, sems.at[0])


def weight_grads(ids, pool, tok, dq, dk, dv, gvec, gup, sl, set_rows):
    width = tok.shape[1]
    full = lambda x: pl.BlockSpec(x.shape, lambda i, *_: (0, 0))
    big = jax.ShapeDtypeStruct((NB, set_rows, width), BF)
    square = pltpu.VMEM((width, width), BF)
    return pl.pallas_call(
        weights_kernel,
        name="weight_grads",
        cost_estimate=takes(9),
        grid_spec=pltpu.PrefetchScalarGridSpec(
            num_scalar_prefetch=1,
            grid=(1,),
            in_specs=[full(x) for x in (pool, tok, dq, dk, dv, gvec, gup, sl)],
            out_specs=[ANY, ANY],
            scratch_shapes=[
                square,
                square,
                square,
                pltpu.VMEM((16 * NB, width), BF),
                pltpu.VMEM((width, tok.shape[0]), BF),
                pltpu.SemaphoreType.DMA((1,)),
            ],
        ),
        out_shape=[big, big],
        compiler_params=params(),
    )(ids, pool, tok, dq, dk, dv, gvec, gup, sl)


def tokens_kernel(mixed, dq, dk, dv, wq, wk, wv, out, acc):
    half = mixed.shape[0]
    up = 0.5 * (mixed[...] + dot_t(dq[...], wq[...]))
    down = dot_t(dk[...], wk[...]) + dot_t(dv[...], wv[...])
    for j in range(mixed.shape[1] // 128):
        cols = slice(128 * j, 128 * j + 128)
        for i in range(2):
            acc[j, pl.ds(i, half, stride=2)] = up[:, cols]
        out[:, cols] = acc[j] + down[:, cols]


def token_grads(mixed, dq, dk, dv, wq, wk, wv):
    rows, width = dk.shape
    step = 512
    half = pl.BlockSpec((step // 2, width), lambda i: (i, 0))
    block = pl.BlockSpec((step, width), lambda i: (i, 0))
    whole = pl.BlockSpec((width, width), lambda i: (0, 0))
    return pl.pallas_call(
        tokens_kernel,
        name="token_grads",
        cost_estimate=takes(8),
        grid=(rows // step,),
        in_specs=[half, half, block, block, whole, whole, whole],
        out_specs=block,
        out_shape=jax.ShapeDtypeStruct((rows, width), FL),
        scratch_shapes=[pltpu.VMEM((width // 128, step, 128), FL)],
        compiler_params=params(),
    )(mixed, dq, dk, dv, wq, wk, wv)


def blocks_of(x):
    return x.reshape(NB, x.shape[0] // NB, x.shape[1])


def column_parts(x, width):
    return jnp.concatenate([x[..., width * c : width * c + width] for c in range(x.shape[-1] // width)], -2)


def bias_block(small, up, width):
    rb = small[0].shape[-1]
    rows = jnp.stack(list(small) + [up[..., rb * c : rb * c + rb] for c in range(4)], -2)
    pad = [(0, 0)] * (rows.ndim - 2) + [(0, 4), (0, width - rb)]
    return jnp.pad(rows, pad)


def pack(wq, wk, wv, wo, w1, w2, bias, width):
    a1 = jnp.concatenate([wq, wk[..., :32, :]], -2)
    b1 = jnp.concatenate([wk[..., 32:, :], wv, bias], -2)
    a2 = jnp.concatenate([w2, wo[..., :32, :]], -2)
    b2 = jnp.concatenate([column_parts(w1, width), wo[..., 32:, :], wo[..., 32:, :]], -2)
    return a1, b1, a2, b2


def unpack(a1, b1, a2, b2, width):
    wq = a1[..., :48, :]
    wk = jnp.concatenate([a1[..., 48:, :], b1[..., :16, :]], -2)
    wv = b1[..., 16:64, :]
    bias = b1[..., 64:, :]
    wo = jnp.concatenate([a2[..., 192:, :], b2[..., 192:208, :]], -2)
    w2 = a2[..., :192, :]
    parts = 4
    w1 = jnp.concatenate([b2[..., 48 * c : 48 * c + 48, :] for c in range(parts)], -1)
    return wq, wk, wv, wo, w1, w2, bias


def pack_kernel(ids, wq, wk, wv, wo, w1, w2, b_up, *refs):
    vectors, (out, bias) = refs[:8], refs[8:]
    first = out.at[:, 0:80]
    second = out.at[:, 80:304]
    rb, width = wq.shape

    @pl.when(ids[1] == 0)
    def _():
        first[0, 0:48] = wq[...].astype(BF)
        first[0, 48:80] = wk[0:32].astype(BF)
        second[0, 0:192] = w2[...].astype(BF)
        second[0, 192:224] = wo[0:32].astype(BF)

    @pl.when(ids[1] != 0)
    def _():
        bias[...] = jnp.zeros(bias.shape, FL)
        for i, x in enumerate(vectors):
            bias[i : i + 1, 0:rb] = x[...]
        for c in range(4):
            bias[8 + c : 9 + c, 0:rb] = b_up[:, rb * c : rb * c + rb]
        first[0, 0:16] = wk[32:48].astype(BF)
        first[0, 16:64] = wv[...].astype(BF)
        first[0, 64:80] = bias[...].astype(BF)
        for c in range(4):
            second[0, 48 * c : 48 * c + 48] = w1[:, width * c : width * c + width].astype(BF)
        second[0, 192:208] = wo[32:48].astype(BF)
        second[0, 208:224] = wo[32:48].astype(BF)


def pack_own(ids, masters, b_up, vectors):
    width = masters[0].shape[1]
    args = list(masters) + [b_up[None]] + [x[None] for x in vectors]
    full = lambda x: pl.BlockSpec(x.shape, lambda i, *_: (0,) * len(x.shape))
    shape = jax.ShapeDtypeStruct((1, 304, width), BF)
    return pl.pallas_call(
        pack_kernel,
        name="pack",
        cost_estimate=takes(3),
        grid_spec=pltpu.PrefetchScalarGridSpec(
            num_scalar_prefetch=1,
            grid=(1,),
            in_specs=[full(x) for x in args],
            out_specs=full(shape),
            scratch_shapes=[pltpu.VMEM((16, width), FL)],
        ),
        out_shape=shape,
        compiler_params=params(),
    )(ids, *args)


def unpack_kernel(ids, mine1, other1, mine2, other2, wq, wk, wv, wo, w1, w2, *vectors):
    width = wq.shape[1]
    rb = wq.shape[0]

    def store(a1, b1, a2, b2):
        wq[...] = a1[0:48]
        wk[0:32] = a1[48:80]
        wk[32:48] = b1[0:16]
        wv[...] = b1[16:64]
        for i in range(8):
            vectors[i][...] = b1[64 + i : 65 + i, 0:rb]
        for c in range(4):
            vectors[8][:, rb * c : rb * c + rb] = b1[72 + c : 73 + c, 0:rb]
            w1[:, width * c : width * c + width] = b2[48 * c : 48 * c + 48]
        vectors[9][...] = b1[76:77, 0:128]
        w2[...] = a2[0:192]
        wo[0:32] = a2[192:224]
        wo[32:48] = b2[192:208]

    @pl.when(ids[1] == 0)
    def _():
        store(mine1, other1, mine2, other2)

    @pl.when(ids[1] != 0)
    def _():
        store(other1, mine1, other2, mine2)


def unpack_own(ids, args, ff):
    width = args[0].shape[1]
    rb = width // NB
    dims = [(rb, width)] * 4 + [(rb, ff), (ff // NB, width)] + [(1, rb)] * 8 + [(1, ff // NB), (1, 128)]
    shapes = [jax.ShapeDtypeStruct(d, FL) for d in dims]
    full = lambda x: pl.BlockSpec(x.shape, lambda i, *_: (0, 0))
    return pl.pallas_call(
        unpack_kernel,
        name="unpack",
        cost_estimate=takes(3),
        grid_spec=pltpu.PrefetchScalarGridSpec(
            num_scalar_prefetch=1,
            grid=(1,),
            in_specs=[full(x) for x in args],
            out_specs=[full(x) for x in shapes],
        ),
        out_shape=shapes,
        compiler_params=params(),
    )(ids, *args)


def after(x, *done):
    return lax.optimization_barrier((x,) + done)[0]


def local(
    tokens,
    cotangent,
    lengths,
    w_query,
    b_query,
    w_key,
    w_value,
    b_value,
    w_output,
    b_output,
    gain_attn,
    shift_attn,
    w_up,
    b_up,
    w_down,
    b_down,
    gain_ffn,
    shift_ffn,
    distance_slope,
):
    rows_here, width = tokens.shape
    ff = w_up.shape[1]
    own = rows_here // 2
    halo = rows_here // 2
    seq = lax.axis_size("seq")
    devices = seq * lax.axis_size("dp")
    direct = seq == NB
    order = ("dp", "seq")
    up_pairs = [(i, i + 1) for i in range(devices - 1)]
    down_pairs = [(i + 1, i) for i in range(devices - 1)]

    masters = (w_query, w_key, w_value, w_output, w_up, w_down)
    vectors = (b_query, b_value, b_output, gain_attn, shift_attn, b_down, gain_ffn, shift_ffn)
    if direct:
        core = lax.axis_index("dp")
        ids = jnp.stack([lax.axis_index("seq"), core]).astype(jnp.int32)
        x = pack_own(ids, masters, b_up, vectors)
        y = x[:, 80:]
        x = x[:, :80]
        x = jnp.concatenate([x, exchange(x, 8, 4)], 0)
        x1, low_a = lax.optimization_barrier(
            (exchange(x, 4, 8), lax.ppermute(tokens[rows_here - halo : rows_here - halo // 2], order, up_pairs))
        )
        x = jnp.concatenate([x, x1], 0)
        y, part = lax.optimization_barrier((y, tokens[rows_here - halo // 2 :], x1))[:2]
        x1, y1, low_b = lax.optimization_barrier(
            (exchange(x, 2, 1), exchange(y, 8, 4), lax.ppermute(part, order, up_pairs))
        )
        low1 = jnp.concatenate([x, x1], 0)
        y = jnp.concatenate([y, y1], 0)
        high1, olow1, y1, high_a = lax.optimization_barrier(
            (
                exchange(low1, 1, 2),
                swap_core(low1),
                exchange(y, 4, 8),
                lax.ppermute(after(tokens[: halo // 2], x1), order, down_pairs),
            )
        )
        y = jnp.concatenate([y, y1], 0)
        sets1 = (low1, high1, olow1, swap_core(high1))
        y1 = exchange(y, 2, 1)
        high_b = lax.ppermute(after(tokens[halo // 2 : halo], high1), order, down_pairs)
    else:
        ids = jnp.zeros((2,), jnp.int32)
        gather = lambda x: lax.all_gather(x.astype(BF), "seq", axis=0, tiled=True)
        full = [blocks_of(gather(x)) for x in masters]
        small = [gather(x).reshape(NB, -1) for x in vectors]
        bias = bias_block(small, gather(b_up).reshape(NB, -1), width)
        a1, b1, a2, b2 = pack(*full, bias, width)
        at_a = jnp.array([rel_a(p) for p in range(NB)])
        at_b = jnp.array([rel_b(p) for p in range(NB)])
        sets1 = (a1[at_a[:8]], a1[at_a[8:]], b1[at_b[:8]], b1[at_b[8:]])
        sets2 = (a2[at_a[:8]], a2[at_a[8:]], b2[at_b[:8]], b2[at_b[8:]])
        low_a = lax.ppermute(tokens[rows_here - halo : rows_here - halo // 2], order, up_pairs)
        low_b = lax.ppermute(tokens[rows_here - halo // 2 :], order, up_pairs)
        high_a = lax.ppermute(tokens[: halo // 2], order, down_pairs)
        high_b = lax.ppermute(tokens[halo // 2 : halo], order, down_pairs)

    first_row = lax.axis_index(order) * rows_here
    total = devices * rows_here
    starts = 2 * (jnp.cumsum(lengths) - lengths)
    place = first_row - halo + 2 * jnp.arange(2 * own, dtype=jnp.int32)
    before = starts[None, :] <= place[:, None]
    begin = jnp.max(jnp.where(before, starts[None, :], 0), 1)
    end = jnp.min(jnp.where(before, total, starts[None, :]), 1)
    inside = (place >= 0) & (place < total)
    shift = first_row - halo
    begin = jnp.where(inside, begin - shift, 0)
    end = jnp.where(inside, end - shift, 0)
    bounds = jnp.pad(jnp.stack([begin, end], 0).astype(FL), ((0, 6), (0, 0)))
    blocks = 2 * own // QB
    chunks = (rows_here + 2 * halo) // KC
    low_chunk = jnp.min(jnp.where(inside, begin, 4 * total).reshape(blocks, QB), 1) // KC
    high_chunk = (jnp.max(end.reshape(blocks, QB), 1) + KC - 1) // KC
    index = jnp.arange(blocks)
    away = (index < blocks // 4) | (index >= blocks - blocks // 4)
    low_chunk = jnp.clip(low_chunk, jnp.where(away, chunks // 4, 0), chunks)
    high_chunk = jnp.clip(high_chunk, 0, jnp.where(away, chunks - chunks // 4, chunks))
    spans = jnp.concatenate([low_chunk, high_chunk]).astype(jnp.int32)

    slopes = distance_slope
    q, k, v, kt, vt, pool, wq, wk, wv, vec, upb = qkv(ids, tokens, sets1, ff)
    if direct:
        k, high_b = lax.optimization_barrier((k, high_b))
    qh, k, v, kt, vt = halo_qkv(low_a, low_b, high_a, high_b, wq, wk, wv, vec, k, v, kt, vt)
    if direct:
        y1, qh = lax.optimization_barrier((y1, qh))
        low2 = jnp.concatenate([y, y1], 0)
        bounds = after(bounds, low2)
    att, exact, lse = attend_forward(spans, slopes, q, k, vt, bounds)
    if direct:
        high2, lse = lax.optimization_barrier((exchange(low2, 1, 2), lse))
        sets2 = (low2, high2, swap_core(low2), swap_core(high2))
    out, pay, stats, mixed, gvec, gup, keep2, send2 = middle(
        ids, pool, att, exact, lse, cotangent, vec, upb, sets2, 224
    )
    low_pay = lax.ppermute(pay[own // 2 :], order, up_pairs)
    high_pay = lax.ppermute(pay[: own // 2], order, down_pairs)
    if direct:
        got = swap_core(send2)
        up = add(keep2[8:], got[8:]).astype(BF)
        bounds = after(bounds, up)
    dq, dk, dv, sl = attend_own(spans, slopes, q, k, v, kt, pay, stats, bounds)
    if direct:
        got1, dq, low_pay, high_pay = lax.optimization_barrier((exchange(up, 1, 2), dq, low_pay, high_pay))
        up = add(keep2[4:8], got[4:8], got1[4:]).astype(BF)
        bounds = after(bounds, up)
    dk, dv = attend_halo(spans, slopes, qh, k, v, low_pay, high_pay, bounds, dk, dv)
    keep1, send1 = weight_grads(ids, pool, tokens, dq, dk, dv, gvec, gup, sl, 80)
    if direct:
        got2, keep1, send1 = lax.optimization_barrier((exchange(up, 2, 1), keep1, send1))
        low = add(keep2[:4], got[:4], got1[:4])
        up = (low[2:] + got2[2:].astype(FL)).astype(BF)
        low = low[:2] + got2[:2].astype(FL)
        got, up = lax.optimization_barrier((swap_core(send1), up))
        part = add(keep1[8:], got[8:]).astype(BF)
        mixed = after(mixed, part)
    grad_tokens = token_grads(mixed, dq, dk, dv, wq, wk, wv)

    if direct:
        got3, got1, grad_tokens = lax.optimization_barrier((exchange(up, 4, 8), exchange(part, 1, 2), grad_tokens))
        part = add(keep1[4:8], got[4:8], got1[4:]).astype(BF)
        up = (low[1:] + got3[1:].astype(FL)).astype(BF)
        low = low[:1] + got3[:1].astype(FL)
        got4, got2 = lax.optimization_barrier((exchange(up, 8, 4), exchange(part, 2, 1)))
        mine = (low + got4.astype(FL))[0]
        low = add(keep1[:4], got[:4], got1[:4])
        part = (low[2:] + got2[2:].astype(FL)).astype(BF)
        low = low[:2] + got2[:2].astype(FL)
        got3, other = lax.optimization_barrier((exchange(part, 4, 8), swap_core(mine)))
        second = (mine, other)
        part = (low[1:] + got3[1:].astype(FL)).astype(BF)
        low = low[:1] + got3[:1].astype(FL)
        mine = (low + exchange(part, 8, 4).astype(FL))[0]
        other = swap_core(mine)
        gq, gk, gv, go, g1, g2, *small = unpack_own(ids, (mine, other) + second, ff)
        g_up, g_slope = small[8][0], small[9][0, : distance_slope.shape[0]]
        small = [x[0] for x in small[:8]]
    else:
        inv_a = [0] * NB
        inv_b = [0] * NB
        for p in range(NB):
            inv_a[rel_a(p)] = p
            inv_b[rel_b(p)] = p
        inv_a = jnp.array(inv_a)
        inv_b = jnp.array(inv_b)
        gq, gk, gv, go, g1, g2, gb = unpack(keep1[inv_a], send1[inv_b], keep2[inv_a], send2[inv_b], width)
        rb = width // NB

        def share(x):
            x = lax.psum(x.astype(FL), "dp")
            return lax.psum_scatter(x, "seq", scatter_dimension=0, tiled=True)

        gq, gk, gv, go, g1, g2 = [share(x.reshape(-1, x.shape[-1])) for x in (gq, gk, gv, go, g1, g2)]
        small = [share(gb[:, i, :rb].reshape(-1)) for i in range(8)]
        g_up = share(gb[:, 8:12, :rb].reshape(-1))
        g_slope = lax.psum(gb[0, 12, : distance_slope.shape[0]].astype(FL), order)
    return (
        out,
        grad_tokens,
        gq,
        small[0],
        gk,
        gv,
        small[1],
        go,
        small[2],
        small[3],
        small[4],
        g1,
        g_up,
        g2,
        small[5],
        small[6],
        small[7],
        g_slope,
    )


def solution(mesh):
    tall = P(("dp", "seq"), None)
    mat = P("seq", None)
    vec = P("seq")
    return jax.shard_map(
        local,
        mesh=mesh,
        in_specs=(tall, tall, P(), mat, vec, mat, mat, vec, mat, vec, vec, vec, mat, vec, mat, vec, vec, vec, P()),
        out_specs=(tall, tall, mat, vec, mat, mat, vec, mat, vec, vec, vec, mat, vec, mat, vec, vec, vec, P()),
        check_vma=False,
    )
```

profile of v0, /device:TPU:0, one launch (start us, length us, event | category | flops | bytes accessed | tf_op | source)
XLA Modules:
  0.0 325.5 jit_solution(14233040505492159597)
XLA Ops:
  1.3 3.2 pack.1
  5.4 4.1 %collective-permute-start = (bf16[1,80,768]{2,1,0:T(8,128)(2,1)S(1)}, bf16[1,80,768]{2,1,0:T(8,128)(2,1)S(1)}, u32[]{:S(2)}, u32[]{:S(2)}) collective-permute-start(bf16[1,80,768]{2,1,0:T(8,128)(2,1)S(1)} %slice.173), channel_id=1, source_target_pairs={{0,8},{1,9},{2,10},{3,11},{4,12},{5,13},{6,14},{7,15},{8,0},{9,1},... | collective-permute-start | bytes 368648 | tf_op jit(solution)/shard_map/ppermute | solution.py:43
  10.5 4.1 %collective-permute-start.2 = (bf16[256,768]{1,0:T(8,128)(2,1)S(1)}, bf16[256,768]{1,0:T(8,128)(2,1)}, u32[]{:S(2)}, u32[]{:S(2)}) collective-permute-start(bf16[256,768]{1,0:T(8,128)(2,1)S(1)} %get-tuple-element.213), channel_id=1, source_target_pairs={{0,1},{1,2},{2,3},{3,4},{4,5},{5,6},{6,7},{7,8},{8,9},{9,10},{10,1... | collective-permute-start | bytes 1179656 | tf_op jit(solution)/shard_map/ppermute | solution.py:1278
  15.6 7.9 %collective-permute-done.1 = bf16[2,80,768]{2,1,0:T(8,128)(2,1)S(1)} collective-permute-done((bf16[2,80,768]{2,1,0:T(8,128)(2,1)S(1)}, bf16[2,80,768]{2,1,0:T(8,128)(2,1)S(1)}, u32[]{:S(2)}, u32[]{:S(2)}) %collective-permute-start.1) | collective-permute-done | bytes 245792 | tf_op jit(solution)/shard_map/ppermute | solution.py:43
  24.7 6.1 %collective-permute-start.5 = (bf16[256,768]{1,0:T(8,128)(2,1)}, bf16[256,768]{1,0:T(8,128)(2,1)S(1)}, u32[]{:S(2)}, u32[]{:S(2)}) collective-permute-start(bf16[256,768]{1,0:T(8,128)(2,1)} %get-tuple-element.110), channel_id=1, source_target_pairs={{0,1},{1,2},{2,3},{3,4},{4,5},{5,6},{6,7},{7,8},{8,9},{9,10},{10,1... | collective-permute-start | bytes 1179656 | tf_op jit(solution)/shard_map/ppermute | solution.py:1283
  30.7 1.6 collective-permute-start.4
  33.0 9.7 %collective-permute-done.4 = bf16[1,224,768]{2,1,0:T(8,128)(2,1)S(1)} collective-permute-done((bf16[1,224,768]{2,1,0:T(8,128)(2,1)S(1)}, bf16[1,224,768]{2,1,0:T(8,128)(2,1)S(1)}, u32[]{:S(2)}, u32[]{:S(2)}) %collective-permute-start.4) | collective-permute-done | bytes 344096 | tf_op jit(solution)/shard_map/ppermute | solution.py:43
  43.6 2.0 collective-permute-start.6
  46.4 1.3 collective-permute-start.9
  48.4 17.7 %collective-permute-done.9.high_a = bf16[256,768]{1,0:T(8,128)(2,1)S(1)} collective-permute-done((bf16[256,768]{1,0:T(8,128)(2,1)}, bf16[256,768]{1,0:T(8,128)(2,1)S(1)}, u32[]{:S(2)}, u32[]{:S(2)}) %collective-permute-start.9) | collective-permute-done | bytes 393248 | tf_op jit(solution)/shard_map/ppermute | solution.py:1292
  66.9 2.0 collective-permute-start.10
  69.6 1.3 collective-permute-start.11
  71.0 4.2 %collective-permute-start.12 = (bf16[4,224,768]{2,1,0:T(8,128)(2,1)S(1)}, bf16[4,224,768]{2,1,0:T(8,128)(2,1)S(1)}, u32[]{:S(2)}, u32[]{:S(2)}) collective-permute-start(bf16[4,224,768]{2,1,0:T(8,128)(2,1)S(1)} %pad_maximum_fusion), channel_id=1, source_target_pairs={{0,2},{1,3},{2,0},{3,1},{4,6},{5,7},{6,4},{7,5},{8,10},{9,11},{10,... | collective-permute-start | bytes 4128776 | tf_op jit(solution)/shard_map/ppermute | solution.py:43
  75.3 1.5 copy-done.9
  77.8 10.4 %qkv.1 = (bf16[512,768]{1,0:T(8,128)(2,1)}, bf16[2048,768]{1,0:T(8,128)(2,1)}, bf16[2048,768]{1,0:T(8,128)(2,1)}, bf16[8,768,256]{2,1,0:T(8,128)(2,1)}, bf16[8,7...) custom-call(s32[2]{0:T(128)} %pad_add_fusion.ids, ...), custom_call_target="tpu_custom_call" | custom-call | flops 10350000128 | bytes 32400000 | tf_op jit(solution)/shard_map/qkv/pallas_call | solution.py:168
  88.2 7.1 %halo_qkv.1 = (bf16[2,256,768]{2,1,0:T(8,128)(2,1)}, bf16[2048,768]{1,0:T(8,128)(2,1)}, bf16[2048,768]{1,0:T(8,128)(2,1)}, bf16[8,768,256]{2,1,0:T(8,128)(2,1)}, bf16[8,768,256]{2,1,0:T(8,128)(2,1)}) custom-call(bf16[256,768]{1,0:T(8,128)(2,1)} %collective-permute-done.2.low_a, ...), custom_call_target="tpu_custom_call", output_to_operand_aliasing={{1}: (8, {}), {2}: (9, {}), {3}: (10, {}), {4}: (11, {})} | custom-call | flops 8049999872 | bytes 25200000 | tf_op jit(solution)/shard_map/halo_qkv/pallas_call | solution.py:217
  95.5 6.2 %collective-permute-start.14 = (bf16[8,224,768]{2,1,0:T(8,128)(2,1)S(1)}, bf16[8,224,768]{2,1,0:T(8,128)(2,1)S(1)}, u32[]{:S(2)}, u32[]{:S(2)}) collective-permute-start(bf16[8,224,768]{2,1,0:T(8,128)(2,1)S(1)} %constant_dynamic-update-slice_fusion.low), channel_id=1, source_target_pairs={{0,16},{16,0},{1,17},{17,1},{2,18},{18,2},{3,19},{19,3},{4,20},{20... | collective-permute-start | bytes 8257544 | tf_op jit(solution)/shard_map/ppermute | solution.py:47
  101.7 2.2 collective-permute-start.13
  103.8 23.6 %attend_forward.1 = (bf16[512,768]{1,0:T(8,128)(2,1)}, f32[512,768]{1,0:T(8,128)}, f32[16,512]{1,0:T(8,128)}) custom-call(s32[16]{0:T(128)} %pad_add_fusion.1.spans, f32[12]{0:T(128)} %slopes.5, bf16[512,768]{1,0:T(8,128)(2,1)} %get-tuple-element.117.q, bf16[2048,768]{1,0:T(8,128)(2,1)} %get-tuple-element.132.k, bf16[8,768,256]{2,1,0:T(8,128)(2,1)} %get-tuple-element.133.vt, ...), custom_call_target="tpu_custom_call" | custom-call | flops 34500001792 | bytes 108000000 | tf_op jit(solution)/shard_map/attend_forward/pallas_call | solution.py:343
  127.4 7.5 %collective-permute-done.13.high = bf16[8,224,768]{2,1,0:T(8,128)(2,1)} collective-permute-done((bf16[8,224,768]{2,1,0:T(8,128)(2,1)S(1)}, bf16[8,224,768]{2,1,0:T(8,128)(2,1)}, u32[]{:S(2)}, u32[]{:S(2)}) %collective-permute-start.13) | collective-permute-done | bytes 2752544 | tf_op jit(solution)/shard_map/ppermute | solution.py:43
  135.0 5.4 %collective-permute-done.15.ohigh = bf16[8,224,768]{2,1,0:T(8,128)(2,1)} collective-permute-done((bf16[8,224,768]{2,1,0:T(8,128)(2,1)}, bf16[8,224,768]{2,1,0:T(8,128)(2,1)}, u32[]{:S(2)}, u32[]{:S(2)}) %collective-permute-start.15) | collective-permute-done | bytes 2752544 | tf_op jit(solution)/shard_map/ppermute | solution.py:47
  140.4 36.3 %middle.1 = (bf16[512,768]{1,0:T(8,128)(2,1)}, bf16[512,896]{1,0:T(8,128)(2,1)}, f32[32,512]{1,0:T(8,128)}, f32[512,768]{1,0:T(8,128)}, f32[8,768]{1,0:T(8,128)}...) custom-call(s32[2]{0:T(128)} %pad_add_fusion.ids, ...), custom_call_target="tpu_custom_call" | custom-call | flops 41400000512 | bytes 129600000 | tf_op jit(solution)/shard_map/middle/pallas_call | solution.py:925
  176.9 2.0 fusion.17
  178.9 1.3 collective-permute-start.19
  180.2 5.4 %collective-permute-start.18 = (bf16[256,896]{1,0:T(8,128)(2,1)S(1)}, bf16[256,896]{1,0:T(8,128)(2,1)}, u32[]{:S(2)}, u32[]{:S(2)}) collective-permute-start(bf16[256,896]{1,0:T(8,128)(2,1)S(1)} %get-tuple-element.217), channel_id=1, source_target_pairs={{0,1},{1,2},{2,3},{3,4},{4,5},{5,6},{6,7},{7,8},{8,9},{9,10},{10,1... | collective-permute-start | bytes 1376264 | tf_op jit(solution)/shard_map/ppermute | solution.py:1353
  186.0 4.5 %add_convert_fusion = bf16[8,224,768]{2,1,0:T(8,128)(2,1)S(1)} fusion(bf16[16,224,768]{2,1,0:T(8,128)(2,1)S(1)} %collective-permute-done.16, bf16[16,224,768]{2,1,0:T(8,128)(2,1)} %get-tuple-element.145), kind=kLoop, calls=%fused_computation | loop fusion | flops 5505024 | bytes 8257536 | tf_op jit(solution)/shard_map/convert_element_type | solution.py:1357
  190.6 2.1 collective-permute-start.17
  192.7 25.7 %attend_own.1 = (bf16[512,768]{1,0:T(8,128)(2,1)}, f32[1024,768]{1,0:T(8,128)}, f32[1024,768]{1,0:T(8,128)}, f32[48,256]{1,0:T(8,128)}) custom-call(s32[16]{0:T(128)} %pad_add_fusion.1.spans, f32[12]{0:T(128)} %slopes.5, bf16[512,768]{1,0:T(8,128)(2,1)} %get-tuple-element.117.q, bf16[2048,768]{1,0:T(8,128)(2,1)} %get-tuple-element.132.k, ...), custom_call_target="tpu_custom_call" | custom-call | flops 34500001792 | bytes 108000000 | tf_op jit(solution)/shard_map/attend_own/pallas_call | solution.py:554
  218.4 16.6 %collective-permute-done.17 = bf16[8,224,768]{2,1,0:T(8,128)(2,1)S(1)} collective-permute-done((bf16[8,224,768]{2,1,0:T(8,128)(2,1)S(1)}, bf16[8,224,768]{2,1,0:T(8,128)(2,1)S(1)}, u32[]{:S(2)}, u32[]{:S(2)}) %collective-permute-start.17) | collective-permute-done | bytes 2752544 | tf_op jit(solution)/shard_map/ppermute | solution.py:43
  235.0 4.7 %convert_add_fusion = (f32[4,224,768]{2,1,0:T(8,128)S(1)}, bf16[4,224,768]{2,1,0:T(8,128)(2,1)}) fusion(bf16[16,224,768]{2,1,0:T(8,128)(2,1)} %copy-done, bf16[8,224,768]{2,1,0:T(8,128)(2,1)S(1)} %collective-permute-done.17, bf16[16,224,768]{2,1,0:T(8,128)(2,1)} %get-tuple-element.145), kind=kLoop, calls=%fused_computation.1 | loop fusion | flops 7569408 | bytes 12386304 | tf_op jit(solution)/shard_map/add | solution.py:53
  239.8 9.8 %attend_halo.1 = (bf16[1024,768]{1,0:T(8,128)(2,1)}, bf16[1024,768]{1,0:T(8,128)(2,1)}) custom-call(s32[16]{0:T(128)} %pad_add_fusion.1.spans, f32[12]{0:T(128)} %slopes.5, bf16[2,256,768]{2,1,0:T(8,128)(2,1)} %get-tuple-element.155.q, bf16[2048,768]{1,0:T(8,128)(2,1)} %get-tuple-element.132.k, bf16[2048,768]{1,0:T(8,128)(2,1)} %get-tuple-element.147.v, ...), custom_call_target="tpu_custom_call" | custom-call | flops 13799999488 | bytes 43200000 | tf_op jit(solution)/shard_map/attend_halo/pallas_call | solution.py:670
  249.6 9.6 %weight_grads.1 = (bf16[16,80,768]{2,1,0:T(8,128)(2,1)}, bf16[16,80,768]{2,1,0:T(8,128)(2,1)}) custom-call(s32[2]{0:T(128)} %pad_add_fusion.ids, f32[512,768]{1,0:T(8,128)} %get-tuple-element.116.pool, bf16[1024,768]{1,0:T(8,128)(2,1)} %tok.3, bf16[512,768]{1,0:T(8,128)(2,1)} %get-tuple-element.154.dq, bf16[1024,768]{1,0:T(8,128)(2,1)} %get-tuple-element.161.dk, ...), custom_call_target="tpu_custom_call" | custom-call | flops 10350000128 | bytes 32400000 | tf_op jit(solution)/shard_map/weight_grads/pallas_call | solution.py:1045
  259.3 2.6 slice_add_fusion
  261.8 1.6 collective-permute-done.21
  263.4 1.3 copy-done.2
  264.8 1.2 add_convert_fusion.2
  266.0 3.9 %collective-permute-start.23 = (bf16[8,80,768]{2,1,0:T(8,128)(2,1)}, bf16[8,80,768]{2,1,0:T(8,128)(2,1)}, u32[]{:S(2)}, u32[]{:S(2)}) collective-permute-start(bf16[8,80,768]{2,1,0:T(8,128)(2,1)} %add_convert_fusion.2), channel_id=1, source_target_pairs={{0,1},{1,0},{2,3},{3,2},{4,5},{5,4},{6,7},{7,6},{8,9},{9,8},{10,11... | collective-permute-start | bytes 2949128 | tf_op jit(solution)/shard_map/ppermute | solution.py:43
  269.8 2.8 collective-permute-start.22
  272.6 7.7 %token_grads.1 = f32[1024,768]{1,0:T(8,128)} custom-call(f32[512,768]{1,0:T(8,128)} %get-tuple-element.174.mixed, bf16[512,768]{1,0:T(8,128)(2,1)} %get-tuple-element.154.dq, bf16[1024,768]{1,0:T(8,128)(2,1)} %get-tuple-element.161.dk, bf16[1024,768]{1,0:T(8,128)(2,1)} %get-tuple-element.162.dv, bf16[768,768]{1,0:T(8,128)(2,1)} %get-tuple-element.124.wq, ...), custom_call_target="tpu_custom_call" | custom-call | flops 9200000000 | bytes 28800000 | tf_op jit(solution)/shard_map/token_grads/pallas_call | solution.py:1085
  280.4 8.1 %collective-permute-done.22 = bf16[2,224,768]{2,1,0:T(8,128)(2,1)S(1)} collective-permute-done((bf16[2,224,768]{2,1,0:T(8,128)(2,1)}, bf16[2,224,768]{2,1,0:T(8,128)(2,1)S(1)}, u32[]{:S(2)}, u32[]{:S(2)}) %collective-permute-start.22) | collective-permute-done | bytes 688160 | tf_op jit(solution)/shard_map/ppermute | solution.py:43
  288.5 1.5 add_convert_fusion.3
  290.7 1.4 collective-permute-start.24
  292.1 9.9 %collective-permute-done.24 = bf16[1,224,768]{2,1,0:T(8,128)(2,1)S(1)} collective-permute-done((bf16[1,224,768]{2,1,0:T(8,128)(2,1)S(1)}, bf16[1,224,768]{2,1,0:T(8,128)(2,1)S(1)}, u32[]{:S(2)}, u32[]{:S(2)}) %collective-permute-start.24) | collective-permute-done | bytes 344096 | tf_op jit(solution)/shard_map/ppermute | solution.py:43
  302.3 1.4 collective-permute-start.26
  303.7 7.5 %collective-permute-done.26 = bf16[2,80,768]{2,1,0:T(8,128)(2,1)S(1)} collective-permute-done((bf16[2,80,768]{2,1,0:T(8,128)(2,1)S(1)}, bf16[2,80,768]{2,1,0:T(8,128)(2,1)S(1)}, u32[]{:S(2)}, u32[]{:S(2)}) %collective-permute-start.26) | collective-permute-done | bytes 245792 | tf_op jit(solution)/shard_map/ppermute | solution.py:43
  312.3 6.0 %collective-permute-done.28 = bf16[1,80,768]{2,1,0:T(8,128)(2,1)S(1)} collective-permute-done((bf16[1,80,768]{2,1,0:T(8,128)(2,1)S(1)}, bf16[1,80,768]{2,1,0:T(8,128)(2,1)S(1)}, u32[]{:S(2)}, u32[]{:S(2)}) %collective-permute-start.28) | collective-permute-done | bytes 122912 | tf_op jit(solution)/shard_map/ppermute | solution.py:43
  318.5 1.5 collective-permute-done.29.other1
  320.7 3.6 %unpack.1 = (f32[48,768]{1,0:T(8,128)}, f32[48,768]{1,0:T(8,128)}, f32[48,768]{1,0:T(8,128)}, f32[48,768]{1,0:T(8,128)}, f32[48,3072]{1,0:T(8,128)}, /*index=5*/...) custom-call(s32[2]{0:T(128)} %pad_add_fusion.ids, ...), custom_call_target="tpu_custom_call" | custom-call | flops 3449999872 | bytes 10800000 | tf_op jit(solution)/shard_map/unpack/pallas_call | solution.py:1217
  (104 shorter events, 15.3 us)
Async XLA Ops:
  1.3 8.3 %copy-start.4 = (bf16[1024,768]{1,0:T(8,128)(2,1)S(1)}, bf16[1024,768]{1,0:T(8,128)(2,1)}, u32[]{:S(2)}) copy-start(bf16[1024,768]{1,0:T(8,128)(2,1)} %tok.3) | copy-start | bytes 4718596
  4.5 20.2 %copy-start.7 = (bf16[1,304,768]{2,1,0:T(8,128)(2,1)S(1)}, bf16[1,304,768]{2,1,0:T(8,128)(2,1)}, u32[]{:S(2)}) copy-start(bf16[1,304,768]{2,1,0:T(8,128)(2,1)} %pack.1) | copy-start | bytes 1400836
  4.5 27.9 %copy-start.12 = (s32[256]{0:T(256)S(1)}, s32[256]{0:T(256)}, u32[]{:S(2)}) copy-start(s32[256]{0:T(256)} %param.21) | copy-start | bytes 3076
  5.4 9.2 %collective-permute-start = (bf16[1,80,768]{2,1,0:T(8,128)(2,1)S(1)}, bf16[1,80,768]{2,1,0:T(8,128)(2,1)S(1)}, u32[]{:S(2)}, u32[]{:S(2)}) collective-permute-start(bf16[1,80,768]{2,1,0:T(8,128)(2,1)S(1)} %slice.173), channel_id=1, source_target_pairs={{0,8},{1,9},{2,10},{3,11},{4,12},{5,13},{6,14},{7,15},{8,0},{9,1},... | collective-permute-start | bytes 368648 | tf_op jit(solution)/shard_map/ppermute | solution.py:43
  10.5 13.0 %collective-permute-start.2 = (bf16[256,768]{1,0:T(8,128)(2,1)S(1)}, bf16[256,768]{1,0:T(8,128)(2,1)}, u32[]{:S(2)}, u32[]{:S(2)}) collective-permute-start(bf16[256,768]{1,0:T(8,128)(2,1)S(1)} %get-tuple-element.213), channel_id=1, source_target_pairs={{0,1},{1,2},{2,3},{3,4},{4,5},{5,6},{6,7},{7,8},{8,9},{9,10},{10,1... | collective-permute-start | bytes 1179656 | tf_op jit(solution)/shard_map/ppermute | solution.py:1278
  14.7 8.8 %collective-permute-start.1 = (bf16[2,80,768]{2,1,0:T(8,128)(2,1)S(1)}, bf16[2,80,768]{2,1,0:T(8,128)(2,1)S(1)}, u32[]{:S(2)}, u32[]{:S(2)}) collective-permute-start(bf16[2,80,768]{2,1,0:T(8,128)(2,1)S(1)} %pad_maximum_fusion.4), channel_id=1, source_target_pairs={{0,4},{1,5},{2,6},{3,7},{4,0},{5,1},{6,2},{7,3},{8,12},{9,13},{10,... | collective-permute-start | bytes 737288 | tf_op jit(solution)/shard_map/ppermute | solution.py:43
  23.6 19.8 %collective-permute-start.3 = (bf16[4,80,768]{2,1,0:T(8,128)(2,1)S(1)}, bf16[4,80,768]{2,1,0:T(8,128)(2,1)S(1)}, u32[]{:S(2)}, u32[]{:S(2)}) collective-permute-start(bf16[4,80,768]{2,1,0:T(8,128)(2,1)S(1)} %pad_maximum_fusion.3), channel_id=1, source_target_pairs={{0,2},{1,3},{2,0},{3,1},{4,6},{5,7},{6,4},{7,5},{8,10},{9,11},{10,... | collective-permute-start | bytes 1474568 | tf_op jit(solution)/shard_map/ppermute | solution.py:43
  24.7 18.0 %collective-permute-start.5 = (bf16[256,768]{1,0:T(8,128)(2,1)}, bf16[256,768]{1,0:T(8,128)(2,1)S(1)}, u32[]{:S(2)}, u32[]{:S(2)}) collective-permute-start(bf16[256,768]{1,0:T(8,128)(2,1)} %get-tuple-element.110), channel_id=1, source_target_pairs={{0,1},{1,2},{2,3},{3,4},{4,5},{5,6},{6,7},{7,8},{8,9},{9,10},{10,1... | collective-permute-start | bytes 1179656 | tf_op jit(solution)/shard_map/ppermute | solution.py:1283
  30.7 11.9 %collective-permute-start.4 = (bf16[1,224,768]{2,1,0:T(8,128)(2,1)S(1)}, bf16[1,224,768]{2,1,0:T(8,128)(2,1)S(1)}, u32[]{:S(2)}, u32[]{:S(2)}) collective-permute-start(bf16[1,224,768]{2,1,0:T(8,128)(2,1)S(1)} %slice.174), channel_id=1, source_target_pairs={{0,8},{1,9},{2,10},{3,11},{4,12},{5,13},{6,14},{7,15},{8,0},{9,1},... | collective-permute-start | bytes 1032200 | tf_op jit(solution)/shard_map/ppermute | solution.py:43
  43.5 27.6 %copy-start.5 = (bf16[8,80,768]{2,1,0:T(8,128)(2,1)}, bf16[8,80,768]{2,1,0:T(8,128)(2,1)S(1)}, u32[]{:S(2)}) copy-start(bf16[8,80,768]{2,1,0:T(8,128)(2,1)S(1)} %pad_maximum_fusion.1.low) | copy-start | bytes 2949124
  43.5 22.7 %collective-permute-start.7 = (bf16[8,80,768]{2,1,0:T(8,128)(2,1)S(1)}, bf16[8,80,768]{2,1,0:T(8,128)(2,1)S(1)}, u32[]{:S(2)}, u32[]{:S(2)}) collective-permute-start(bf16[8,80,768]{2,1,0:T(8,128)(2,1)S(1)} %pad_maximum_fusion.1.low), channel_id=1, source_target_pairs={{0,16},{16,0},{1,17},{17,1},{2,18},{18,2},{3,19},{19,3},{4,20},{20... | collective-permute-start | bytes 2949128 | tf_op jit(solution)/shard_map/ppermute | solution.py:47
  43.6 23.3 %collective-permute-start.6 = (bf16[8,80,768]{2,1,0:T(8,128)(2,1)S(1)}, bf16[8,80,768]{2,1,0:T(8,128)(2,1)S(1)}, u32[]{:S(2)}, u32[]{:S(2)}) collective-permute-start(bf16[8,80,768]{2,1,0:T(8,128)(2,1)S(1)} %pad_maximum_fusion.1.low), channel_id=1, source_target_pairs={{0,1},{1,0},{2,3},{3,2},{4,5},{5,4},{6,7},{7,6},{8,9},{9,8},{10,11... | collective-permute-start | bytes 2949128 | tf_op jit(solution)/shard_map/ppermute | solution.py:43
  45.6 20.5 %collective-permute-start.8 = (bf16[2,224,768]{2,1,0:T(8,128)(2,1)S(1)}, bf16[2,224,768]{2,1,0:T(8,128)(2,1)S(1)}, u32[]{:S(2)}, u32[]{:S(2)}) collective-permute-start(bf16[2,224,768]{2,1,0:T(8,128)(2,1)S(1)} %pad_maximum_fusion.2), channel_id=1, source_target_pairs={{0,4},{1,5},{2,6},{3,7},{4,0},{5,1},{6,2},{7,3},{8,12},{9,13},{10,... | collective-permute-start | bytes 2064392 | tf_op jit(solution)/shard_map/ppermute | solution.py:43
  46.4 19.7 %collective-permute-start.9 = (bf16[256,768]{1,0:T(8,128)(2,1)}, bf16[256,768]{1,0:T(8,128)(2,1)S(1)}, u32[]{:S(2)}, u32[]{:S(2)}) collective-permute-start(bf16[256,768]{1,0:T(8,128)(2,1)} %get-tuple-element.113), channel_id=1, source_target_pairs={{1,0},{2,1},{3,2},{4,3},{5,4},{6,5},{7,6},{8,7},{9,8},{10,9},{11,1... | collective-permute-start | bytes 1179656 | tf_op jit(solution)/shard_map/ppermute | solution.py:1292
  66.9 2.7 copy-start.14
  66.9 8.3 %copy-start.15 = (bf16[8,80,768]{2,1,0:T(8,128)(2,1)}, bf16[8,80,768]{2,1,0:T(8,128)(2,1)S(1)}, u32[]{:S(2)}) copy-start(bf16[8,80,768]{2,1,0:T(8,128)(2,1)S(1)} %collective-permute-done.6.high) | copy-start | bytes 2949124
  66.9 9.9 %collective-permute-start.10 = (bf16[8,80,768]{2,1,0:T(8,128)(2,1)S(1)}, bf16[8,80,768]{2,1,0:T(8,128)(2,1)S(1)}, u32[]{:S(2)}, u32[]{:S(2)}) collective-permute-start(bf16[8,80,768]{2,1,0:T(8,128)(2,1)S(1)} %collective-permute-done.6.high), channel_id=1, source_target_pairs={{0,16},{16,0},{1,17},{17,1},{2,18},{18,2},{3,19},{19,3},{4,20},{20... | collective-permute-start | bytes 2949128 | tf_op jit(solution)/shard_map/ppermute | solution.py:47
  69.6 18.6 %collective-permute-start.11 = (bf16[256,768]{1,0:T(8,128)(2,1)S(1)}, bf16[256,768]{1,0:T(8,128)(2,1)}, u32[]{:S(2)}, u32[]{:S(2)}) collective-permute-start(bf16[256,768]{1,0:T(8,128)(2,1)S(1)} %get-tuple-element.122), channel_id=1, source_target_pairs={{1,0},{2,1},{3,2},{4,3},{5,4},{6,5},{7,6},{8,7},{9,8},{10,9},{11,1... | collective-permute-start | bytes 1179656 | tf_op jit(solution)/shard_map/ppermute | solution.py:1298
  71.0 24.3 %collective-permute-start.12 = (bf16[4,224,768]{2,1,0:T(8,128)(2,1)S(1)}, bf16[4,224,768]{2,1,0:T(8,128)(2,1)S(1)}, u32[]{:S(2)}, u32[]{:S(2)}) collective-permute-start(bf16[4,224,768]{2,1,0:T(8,128)(2,1)S(1)} %pad_maximum_fusion), channel_id=1, source_target_pairs={{0,2},{1,3},{2,0},{3,1},{4,6},{5,7},{6,4},{7,5},{8,10},{9,11},{10,... | collective-permute-start | bytes 4128776 | tf_op jit(solution)/shard_map/ppermute | solution.py:43
  75.3 1.5 copy-start.9
  76.8 1.0 copy-start.16
  88.2 7.2 %copy-start.10 = (bf16[8,224,768]{2,1,0:T(8,128)(2,1)S(1)}, bf16[8,224,768]{2,1,0:T(8,128)(2,1)}, u32[]{:S(2)}) copy-start(bf16[8,224,768]{2,1,0:T(8,128)(2,1)} %copy-done.9) | copy-start | bytes 8257540
  95.5 32.0 %copy-start.11 = (bf16[8,224,768]{2,1,0:T(8,128)(2,1)}, bf16[8,224,768]{2,1,0:T(8,128)(2,1)S(1)}, u32[]{:S(2)}) copy-start(bf16[8,224,768]{2,1,0:T(8,128)(2,1)S(1)} %constant_dynamic-update-slice_fusion.low) | copy-start | bytes 8257540
  95.5 39.5 %collective-permute-start.14 = (bf16[8,224,768]{2,1,0:T(8,128)(2,1)S(1)}, bf16[8,224,768]{2,1,0:T(8,128)(2,1)S(1)}, u32[]{:S(2)}, u32[]{:S(2)}) collective-permute-start(bf16[8,224,768]{2,1,0:T(8,128)(2,1)S(1)} %constant_dynamic-update-slice_fusion.low), channel_id=1, source_target_pairs={{0,16},{16,0},{1,17},{17,1},{2,18},{18,2},{3,19},{19,3},{4,20},{20... | collective-permute-start | bytes 8257544 | tf_op jit(solution)/shard_map/ppermute | solution.py:47
  101.7 33.3 %collective-permute-start.13 = (bf16[8,224,768]{2,1,0:T(8,128)(2,1)S(1)}, bf16[8,224,768]{2,1,0:T(8,128)(2,1)}, u32[]{:S(2)}, u32[]{:S(2)}) collective-permute-start(bf16[8,224,768]{2,1,0:T(8,128)(2,1)S(1)} %constant_dynamic-update-slice_fusion.low), channel_id=1, source_target_pairs={{0,1},{1,0},{2,3},{3,2},{4,5},{5,4},{6,7},{7,6},{8,9},{9,8},{10,11... | collective-permute-start | bytes 8257544 | tf_op jit(solution)/shard_map/ppermute | solution.py:43
  135.0 5.4 %collective-permute-start.15 = (bf16[8,224,768]{2,1,0:T(8,128)(2,1)}, bf16[8,224,768]{2,1,0:T(8,128)(2,1)}, u32[]{:S(2)}, u32[]{:S(2)}) collective-permute-start(bf16[8,224,768]{2,1,0:T(8,128)(2,1)} %collective-permute-done.13.high), channel_id=1, source_target_pairs={{0,16},{16,0},{1,17},{17,1},{2,18},{18,2},{3,19},{19,3},{4,20},{20... | collective-permute-start | bytes 8257544 | tf_op jit(solution)/shard_map/ppermute | solution.py:47
  135.0 5.4 %copy-start.13 = (bf16[8,224,768]{2,1,0:T(8,128)(2,1)}, bf16[8,224,768]{2,1,0:T(8,128)(2,1)S(1)}, u32[]{:S(2)}) copy-start(bf16[8,224,768]{2,1,0:T(8,128)(2,1)S(1)} %collective-permute-done.14.olow) | copy-start | bytes 8257540
  176.7 9.3 %collective-permute-start.16 = (bf16[16,224,768]{2,1,0:T(8,128)(2,1)}, bf16[16,224,768]{2,1,0:T(8,128)(2,1)S(1)}, u32[]{:S(2)}, u32[]{:S(2)}) collective-permute-start(bf16[16,224,768]{2,1,0:T(8,128)(2,1)} %get-tuple-element.146), channel_id=1, source_target_pairs={{0,16},{16,0},{1,17},{17,1},{2,18},{18,2},{3,19},{19,3},{4,20},{20... | collective-permute-start | bytes 16515080 | tf_op jit(solution)/shard_map/ppermute | solution.py:47
  178.9 39.4 %collective-permute-start.19 = (bf16[256,896]{1,0:T(8,128)(2,1)}, bf16[256,896]{1,0:T(8,128)(2,1)}, u32[]{:S(2)}, u32[]{:S(2)}) collective-permute-start(bf16[256,896]{1,0:T(8,128)(2,1)} %get-tuple-element.216), channel_id=1, source_target_pairs={{1,0},{2,1},{3,2},{4,3},{5,4},{6,5},{7,6},{8,7},{9,8},{10,9},{11,1... | collective-permute-start | bytes 1376264 | tf_op jit(solution)/shard_map/ppermute | solution.py:1354
  180.2 38.2 %collective-permute-start.18 = (bf16[256,896]{1,0:T(8,128)(2,1)S(1)}, bf16[256,896]{1,0:T(8,128)(2,1)}, u32[]{:S(2)}, u32[]{:S(2)}) collective-permute-start(bf16[256,896]{1,0:T(8,128)(2,1)S(1)} %get-tuple-element.217), channel_id=1, source_target_pairs={{0,1},{1,2},{2,3},{3,4},{4,5},{5,6},{6,7},{7,8},{8,9},{9,10},{10,1... | collective-permute-start | bytes 1376264 | tf_op jit(solution)/shard_map/ppermute | solution.py:1353
  186.0 4.5 %copy-start = (bf16[16,224,768]{2,1,0:T(8,128)(2,1)}, bf16[16,224,768]{2,1,0:T(8,128)(2,1)S(1)}, u32[]{:S(2)}) copy-start(bf16[16,224,768]{2,1,0:T(8,128)(2,1)S(1)} %collective-permute-done.16) | copy-start | bytes 16515076
  190.6 44.4 %collective-permute-start.17 = (bf16[8,224,768]{2,1,0:T(8,128)(2,1)S(1)}, bf16[8,224,768]{2,1,0:T(8,128)(2,1)S(1)}, u32[]{:S(2)}, u32[]{:S(2)}) collective-permute-start(bf16[8,224,768]{2,1,0:T(8,128)(2,1)S(1)} %add_convert_fusion), channel_id=1, source_target_pairs={{0,1},{1,0},{2,3},{3,2},{4,5},{5,4},{6,7},{7,6},{8,9},{9,8},{10,11... | collective-permute-start | bytes 8257544 | tf_op jit(solution)/shard_map/ppermute | solution.py:43
  239.8 19.4 %collective-permute-start.20 = (bf16[4,224,768]{2,1,0:T(8,128)(2,1)}, bf16[4,224,768]{2,1,0:T(8,128)(2,1)}, u32[]{:S(2)}, u32[]{:S(2)}) collective-permute-start(bf16[4,224,768]{2,1,0:T(8,128)(2,1)} %get-tuple-element.205), channel_id=1, source_target_pairs={{0,2},{1,3},{2,0},{3,1},{4,6},{5,7},{6,4},{7,5},{8,10},{9,11},{10,... | collective-permute-start | bytes 4128776 | tf_op jit(solution)/shard_map/ppermute | solution.py:43
  259.2 4.2 %collective-permute-start.21 = (bf16[16,80,768]{2,1,0:T(8,128)(2,1)}, bf16[16,80,768]{2,1,0:T(8,128)(2,1)S(1)}, u32[]{:S(2)}, u32[]{:S(2)}) collective-permute-start(bf16[16,80,768]{2,1,0:T(8,128)(2,1)} %get-tuple-element.168), channel_id=1, source_target_pairs={{0,16},{16,0},{1,17},{17,1},{2,18},{18,2},{3,19},{19,3},{4,20},{20... | collective-permute-start | bytes 5898248 | tf_op jit(solution)/shard_map/ppermute | solution.py:47
  259.3 5.5 %copy-start.1 = (bf16[16,80,768]{2,1,0:T(8,128)(2,1)S(1)}, bf16[16,80,768]{2,1,0:T(8,128)(2,1)}, u32[]{:S(2)}) copy-start(bf16[16,80,768]{2,1,0:T(8,128)(2,1)} %get-tuple-element.171) | copy-start | bytes 5898244
  263.4 1.3 copy-start.2
  266.0 22.6 %collective-permute-start.23 = (bf16[8,80,768]{2,1,0:T(8,128)(2,1)}, bf16[8,80,768]{2,1,0:T(8,128)(2,1)}, u32[]{:S(2)}, u32[]{:S(2)}) collective-permute-start(bf16[8,80,768]{2,1,0:T(8,128)(2,1)} %add_convert_fusion.2), channel_id=1, source_target_pairs={{0,1},{1,0},{2,3},{3,2},{4,5},{5,4},{6,7},{7,6},{8,9},{9,8},{10,11... | collective-permute-start | bytes 2949128 | tf_op jit(solution)/shard_map/ppermute | solution.py:43
  269.8 18.7 %collective-permute-start.22 = (bf16[2,224,768]{2,1,0:T(8,128)(2,1)}, bf16[2,224,768]{2,1,0:T(8,128)(2,1)S(1)}, u32[]{:S(2)}, u32[]{:S(2)}) collective-permute-start(bf16[2,224,768]{2,1,0:T(8,128)(2,1)} %get-tuple-element.170), channel_id=1, source_target_pairs={{0,4},{1,5},{2,6},{3,7},{4,0},{5,1},{6,2},{7,3},{8,12},{9,13},{10,... | collective-permute-start | bytes 2064392 | tf_op jit(solution)/shard_map/ppermute | solution.py:43
  272.6 15.9 %copy-start.3 = (bf16[16,80,768]{2,1,0:T(8,128)(2,1)S(1)}, bf16[16,80,768]{2,1,0:T(8,128)(2,1)}, u32[]{:S(2)}) copy-start(bf16[16,80,768]{2,1,0:T(8,128)(2,1)} %copy-done.2) | copy-start | bytes 5898244
  290.0 11.9 %collective-permute-start.25 = (bf16[4,80,768]{2,1,0:T(8,128)(2,1)S(1)}, bf16[4,80,768]{2,1,0:T(8,128)(2,1)S(1)}, u32[]{:S(2)}, u32[]{:S(2)}) collective-permute-start(bf16[4,80,768]{2,1,0:T(8,128)(2,1)S(1)} %get-tuple-element.206), channel_id=1, source_target_pairs={{0,2},{1,3},{2,0},{3,1},{4,6},{5,7},{6,4},{7,5},{8,10},{9,11},{10,... | collective-permute-start | bytes 1474568 | tf_op jit(solution)/shard_map/ppermute | solution.py:43
  290.7 11.3 %collective-permute-start.24 = (bf16[1,224,768]{2,1,0:T(8,128)(2,1)S(1)}, bf16[1,224,768]{2,1,0:T(8,128)(2,1)S(1)}, u32[]{:S(2)}, u32[]{:S(2)}) collective-permute-start(bf16[1,224,768]{2,1,0:T(8,128)(2,1)S(1)} %fusion.5), channel_id=1, source_target_pairs={{0,8},{1,9},{2,10},{3,11},{4,12},{5,13},{6,14},{7,15},{8,0},{9,1},... | collective-permute-start | bytes 1032200 | tf_op jit(solution)/shard_map/ppermute | solution.py:43
  302.1 17.9 %copy-start.6 = (f32[224,768]{1,0:T(8,128)}, f32[224,768]{1,0:T(8,128)S(1)}, u32[]{:S(2)}) copy-start(f32[224,768]{1,0:T(8,128)S(1)} %fusion.4.mine2) | copy-start | bytes 2064388
  302.1 9.1 %collective-permute-start.27 = (f32[224,768]{1,0:T(8,128)S(1)}, f32[224,768]{1,0:T(8,128)S(1)}, u32[]{:S(2)}, u32[]{:S(2)}) collective-permute-start(f32[224,768]{1,0:T(8,128)S(1)} %fusion.4.mine2), channel_id=1, source_target_pairs={{0,16},{16,0},{1,17},{17,1},{2,18},{18,2},{3,19},{19,3},{4,20},{20... | collective-permute-start | bytes 2064392 | tf_op jit(solution)/shard_map/ppermute | solution.py:47
  302.3 8.9 %collective-permute-start.26 = (bf16[2,80,768]{2,1,0:T(8,128)(2,1)S(1)}, bf16[2,80,768]{2,1,0:T(8,128)(2,1)S(1)}, u32[]{:S(2)}, u32[]{:S(2)}) collective-permute-start(bf16[2,80,768]{2,1,0:T(8,128)(2,1)S(1)} %get-tuple-element.214), channel_id=1, source_target_pairs={{0,4},{1,5},{2,6},{3,7},{4,0},{5,1},{6,2},{7,3},{8,12},{9,13},{10,... | collective-permute-start | bytes 737288 | tf_op jit(solution)/shard_map/ppermute | solution.py:43
  311.2 8.8 %copy-start.17 = (f32[224,768]{1,0:T(8,128)}, f32[224,768]{1,0:T(8,128)S(1)}, u32[]{:S(2)}) copy-start(f32[224,768]{1,0:T(8,128)S(1)} %collective-permute-done.27.other2) | copy-start | bytes 2064388
  311.2 7.2 %collective-permute-start.28 = (bf16[1,80,768]{2,1,0:T(8,128)(2,1)S(1)}, bf16[1,80,768]{2,1,0:T(8,128)(2,1)S(1)}, u32[]{:S(2)}, u32[]{:S(2)}) collective-permute-start(bf16[1,80,768]{2,1,0:T(8,128)(2,1)S(1)} %fusion.7), channel_id=1, source_target_pairs={{0,8},{1,9},{2,10},{3,11},{4,12},{5,13},{6,14},{7,15},{8,0},{9,1},... | collective-permute-start | bytes 368648 | tf_op jit(solution)/shard_map/ppermute | solution.py:43
  318.4 1.6 copy-start.8
  318.4 1.6 collective-permute-start.29
  (3 other events, 2.2 us)
where the time goes:
time: 326 us; the launch traced here: 325 us
  Pallas kernels  137 us (42%)
  waiting for transfers between devices  100 us (31%)
  starting transfers between devices  57.4 us (18%)
  other arithmetic  17.7 us (5%)
  local copies, waits for them, and re-layouts  12.2 us (4%)
    ppermute x16, waiting for transfers between devices, exchange(): return lax.ppermute(x, ('dp', 'seq'), pairs)  73.3 us
    pallas_call x1, Pallas kernels, middle(): pl.pallas_call(middle_kernel, name='middle', cost_estimate=takes(36), gri...  36.3 us
    ppermute x16, starting transfers between devices, exchange(): return lax.ppermute(x, ('dp', 'seq'), pairs)  29.3 us
    pallas_call x1, Pallas kernels, attend_own(): pl.pallas_call(own_kernel, name='attend_own', cost_estimate=takes(30), gr...  25.7 us
    pallas_call x1, Pallas kernels, attend_forward(): pl.pallas_call(forward_kernel, name='attend_forward', cost_estimate=takes...  23.6 us
    ppermute x1, waiting for transfers between devices, local(): lax.ppermute(after(tokens[:halo // 2], x1), order, down_pairs)  17.7 us
    pallas_call x1, Pallas kernels, qkv(): pl.pallas_call(qkv_kernel, name='qkv', cost_estimate=takes(9), grid_spec=...  10.4 us
    pallas_call x1, Pallas kernels, attend_halo(): pl.pallas_call(halo_kernel, name='attend_halo', cost_estimate=takes(12),...  9.84 us
  transfers between devices with their start and end apart: 30, of which 13 were waited for; matrix products, arithmetic and copies ran while one was open for 4% of the time, Pallas kernels for 29%

commit v1 on v0

--- a/solution.py
+++ b/solution.py
@@ -594,21 +594,50 @@
 
 
 def halo_kernel(
-    spans, slopes, q, k, v, low_pay, high_pay, bounds, dk0, dv0, dk_out, dv_out, q2, da2, qt, dat, st, dk, dv
+    spans,
+    slopes,
+    q,
+    ka,
+    kb,
+    va,
+    vb,
+    low_pay,
+    high_pay,
+    low_stats,
+    high_stats,
+    bounds,
+    dk0,
+    dv0,
+    dk_out,
+    dv_out,
+    q2,
+    da2,
+    qt,
+    dat,
+    st,
+    k,
+    v,
+    dk,
+    dv,
 ):
-    width = q.shape[2]
-    pairs = width // 128
+    half = pl.program_id(0)
+    pairs = q.shape[2] // 128
     total_blocks = bounds.shape[1] // QB
-    quarter = k.shape[0] // KC // 4
+    edge = ka.shape[0]
+    first = edge // KC
     count = low_pay.shape[0] // QB
     dk[...] = dk0[...]
     dv[...] = dv0[...]
+    for into, parts in ((k, (ka, kb)), (v, (va, vb))):
+        into[0:edge] = parts[0][...]
+        into[edge:] = parts[1][...]
     qt[...] = jnp.zeros(qt.shape, BF)
     dat[...] = jnp.zeros(dat.shape, BF)
     ones = value_lines()
-    for side, pay in enumerate((low_pay, high_pay)):
-        x = pay[:, width : width + 128].astype(FL)
-        st[side] = (x + pltpu.roll(x, 96, 1) + pltpu.roll(x, 64, 1)).T
+    for side, pay in enumerate((low_stats, high_stats)):
+        x = pay[...].astype(FL)
+        x = (x + pltpu.roll(x, 96, 1) + pltpu.roll(x, 64, 1)).T
+        st[side] = jnp.where(half == 0, x[0:16], x[16:32])
 
     def query_block(i, _):
         side = i // count
@@ -628,28 +657,24 @@
             for j in range(pairs):
                 cols = slice(128 * j, 128 * j + 128)
                 h = 2 * j
-                at = 16 * (h // (width // 128)) + h % (width // 128)
-                lse = jnp.concatenate([st[side, at : at + 1, rows], st[side, at + 1 : at + 2, rows]], 1)
-                delta = jnp.concatenate([st[side, at + 8 : at + 9, rows], st[side, at + 9 : at + 10, rows]], 1)
+                lse = jnp.concatenate([st[side, h : h + 1, rows], st[side, h + 1 : h + 2, rows]], 1)
+                delta = jnp.concatenate([st[side, h + 8 : h + 9, rows], st[side, h + 9 : h + 10, rows]], 1)
                 d = jnp.where(side == 0, low_pay[rows, cols], high_pay[rows, cols])
-                fill_queries(
-                    j, q[side, rows, cols], d, lse, delta, slope_line(slopes, h), setup, q2, da2, qt, dat
-                )
+                slope = slope_line(slopes, 2 * pairs * half + h)
+                fill_queries(j, q[side, rows, cols], d, lse, delta, slope, setup, q2, da2, qt, dat)
 
             def step(c, _):
-                keys = pl.ds(pl.multiple_of(c * KC, KC), KC)
-                mine = pl.ds(pl.multiple_of((c - quarter) * KC, KC), KC)
+                mine = pl.ds(pl.multiple_of((c - first) * KC, KC), KC)
                 lines = chunk_lines(base, (c - block).astype(FL), sign, limit)
-                for g in range(0, pairs, 3):
-                    js = range(g, g + 3)
-                    col = {j: slice(128 * j, 128 * j + 128) for j in js}
-                    p = [jnp.exp(dot(jnp.concatenate([k[keys, col[j]], lines], 1), qt[j])) for j in js]
-                    dp = [dot(jnp.concatenate([v[keys, col[j]], ones], 1), dat[j]) for j in js]
-                    new_v = [dot(x.astype(BF), da2[j]) for x, j in zip(p, js)]
-                    new_k = [dot((x * y).astype(BF), q2[j]) for x, y, j in zip(p, dp, js)]
-                    for j, x, y in zip(js, new_v, new_k):
-                        dv[mine, col[j]] = dv[mine, col[j]] + x
-                        dk[mine, col[j]] = dk[mine, col[j]] + y
+                js = range(pairs)
+                col = [slice(128 * j, 128 * j + 128) for j in js]
+                p = [jnp.exp(dot(jnp.concatenate([k[mine, col[j]], lines], 1), qt[j])) for j in js]
+                dp = [dot(jnp.concatenate([v[mine, col[j]], ones], 1), dat[j]) for j in js]
+                new_v = [dot(p[j].astype(BF), da2[j]) for j in js]
+                new_k = [dot((p[j] * dp[j]).astype(BF), q2[j]) for j in js]
+                for j in js:
+                    dv[mine, col[j]] = dv[mine, col[j]] + new_v[j]
+                    dk[mine, col[j]] = dk[mine, col[j]] + new_k[j]
                 return 0
 
             lax.fori_loop(c0, c1, step, 0)
@@ -663,32 +688,42 @@
 
 def attend_halo(spans, slopes, q, k, v, low_pay, high_pay, bounds, dk0, dv0):
     width = q.shape[2]
-    pairs = width // 128
+    wide = width // 2
+    pairs = wide // 128
     keys = dk0.shape[0]
-    full = lambda x: pl.BlockSpec(x.shape, lambda i, *_: (0,) * len(x.shape))
+    rows = low_pay.shape[0]
     shape = jax.ShapeDtypeStruct((keys, width), BF)
+    col = lambda i, *_: (0, i)
+    parts = [pl.BlockSpec((keys // 2, wide), lambda i, *_: (1, i)), pl.BlockSpec((keys // 2, wide), lambda i, *_: (2, i))]
+    tail = pl.BlockSpec((rows, 128), lambda i, *_: (0, width // 128))
+    whole = pl.BlockSpec((keys, wide), col)
+    pay = pl.BlockSpec((rows, wide), col)
     return pl.pallas_call(
         halo_kernel,
         name="attend_halo",
         cost_estimate=takes(12),
         grid_spec=pltpu.PrefetchScalarGridSpec(
             num_scalar_prefetch=2,
-            grid=(1,),
-            in_specs=[full(x) for x in (q, k, v, low_pay, high_pay, bounds, dk0, dv0)],
-            out_specs=[full(shape), full(shape)],
+            grid=(2,),
+            in_specs=[pl.BlockSpec((2, q.shape[1], wide), lambda i, *_: (0, 0, i))]
+            + parts * 2
+            + [pay, pay, tail, tail, pl.BlockSpec(bounds.shape, lambda i, *_: (0, 0)), whole, whole],
+            out_specs=[whole, whole],
             scratch_shapes=[
                 pltpu.VMEM((pairs, 2 * QB, 128), BF),
                 pltpu.VMEM((pairs, 2 * QB, 128), BF),
                 pltpu.VMEM((pairs, 256, 2 * QB), BF),
                 pltpu.VMEM((pairs, 256, 2 * QB), BF),
-                pltpu.VMEM((2, 128, low_pay.shape[0]), FL),
-                pltpu.VMEM((keys, width), FL),
-                pltpu.VMEM((keys, width), FL),
+                pltpu.VMEM((2, 16, rows), FL),
+                pltpu.VMEM((keys, wide), BF),
+                pltpu.VMEM((keys, wide), BF),
+                pltpu.VMEM((keys, wide), FL),
+                pltpu.VMEM((keys, wide), FL),
             ],
         ),
         out_shape=[shape, shape],
         compiler_params=params(),
-    )(spans, slopes, q, k, v, low_pay, high_pay, bounds, dk0, dv0)
+    )(spans, slopes, q, k, k, v, v, low_pay, high_pay, low_pay, high_pay, bounds, dk0, dv0)
 
 
 def normalize(z):
@@ -720,6 +755,8 @@
     ohigh,
     out,
     pay,
+    pay_low,
+    pay_high,
     stats,
     mixed,
     gvec,
@@ -784,17 +821,20 @@
     c0 = 0.7978845608028654
 
     def up(c, _):
+        before = jnp.maximum(c - 1, 0)
+        z[...] = z[...] + dot(active[before], w2[pl.ds(pl.multiple_of(before * width, 128), width), :])
         inner = dot(hid_low[...], w1[c]) + upb[pl.ds(0, 1), pl.ds(pl.multiple_of(c * width, 128), width)]
         sq = inner * inner
-        t = jnp.tanh(c0 * (inner + 0.044715 * (inner * sq)))
-        cdf = 0.5 * (1.0 + t)
+        t = jnp.tanh(inner * (c0 + (0.044715 * c0) * sq))
+        cdf = 0.5 + 0.5 * t
         active[c] = (inner * cdf).astype(BF)
-        slope[c] = cdf + inner * (0.5 * (1.0 - t * t)) * (c0 + (3 * 0.044715 * c0) * sq)
-        part = dot(active[c], w2[pl.ds(pl.multiple_of(c * width, 128), width), :])
-        z[...] = jnp.where(c == 0, part, z[...] + part)
+        slope[c] = cdf + (inner * (1.0 - t * t)) * (0.5 * c0 + (1.5 * 0.044715 * c0) * sq)
         return 0
 
+    active[0] = jnp.zeros((n, width), BF)
+    z[...] = jnp.zeros(z.shape, FL)
     lax.fori_loop(0, parts, up, 0)
+    z[...] = z[...] + dot(active[parts - 1], w2[pl.ds((parts - 1) * width, width), :])
     gvec[...] = jnp.zeros(gvec.shape, FL)
 
     def second_norm(r, i):
@@ -902,7 +942,10 @@
         pieces.append(piece)
         st = st - piece
     pieces.append(jnp.zeros_like(st))
-    pay[:, width:] = jnp.concatenate(pieces, 1).astype(BF)
+    pay_low[:, width:] = jnp.concatenate(pieces, 1)[: n // 2].astype(BF)
+    pay_high[:, width:] = jnp.concatenate(pieces, 1)[n // 2 :].astype(BF)
+    pay_low[:, 0:width] = pay[0 : n // 2, :]
+    pay_high[:, 0:width] = pay[n // 2 :, :]
     wait_all(keep, sems.at[3])
     wait_all(send, sems.at[3])
 
@@ -915,7 +958,9 @@
     full = lambda x: pl.BlockSpec(x.shape, whole)
     shapes = [
         jax.ShapeDtypeStruct((n, width), BF),
-        jax.ShapeDtypeStruct((n, width + 128), BF),
+        jax.ShapeDtypeStruct((n, width), BF),
+        jax.ShapeDtypeStruct((n // 2, width + 128), BF),
+        jax.ShapeDtypeStruct((n // 2, width + 128), BF),
         jax.ShapeDtypeStruct((32, n), FL),
         jax.ShapeDtypeStruct((n, width), FL),
         jax.ShapeDtypeStruct((8, width), FL),
@@ -955,7 +1000,11 @@
     )(ids, pool, att, exact, lse, cot, vec, upb, *sets)
 
 
-def weights_kernel(ids, pool, tok, dq, dk, dv, gvec, gup, sl, keep, send, dwq, dwk, dwv, bias, tt, sems):
+def weights_kernel(
+    ids, pool, tok, dq, dk, dv, gvec, gup, sl, keep_low, keep_up, send_low, send_up, dwq, dwk, dwv, bias, tt, sems
+):
+    keep = (keep_low, keep_up)
+    send = (send_low, send_up)
     width = tok.shape[1]
     ff = gup.shape[1]
     rb = width // NB
@@ -979,11 +1028,11 @@
     def store_sets(a_ref, b_ref):
         for p in range(NB):
             s = ids[0] ^ rel_a(p)
-            go(dwq.at[rows(s * rb, 48)], a_ref.at[p, pl.ds(0, 48)])
-            go(dwk.at[rows(s * rb, 32)], a_ref.at[p, pl.ds(48, 32)])
+            go(dwq.at[rows(s * rb, 48)], a_ref[p // 8].at[p % 8, pl.ds(0, 48)])
+            go(dwk.at[rows(s * rb, 32)], a_ref[p // 8].at[p % 8, pl.ds(48, 32)])
             s = ids[0] ^ rel_b(p)
-            go(dwk.at[rows(s * rb + 32, 16)], b_ref.at[p, pl.ds(0, 16)])
-            go(dwv.at[rows(s * rb, 48)], b_ref.at[p, pl.ds(16, 48)])
+            go(dwk.at[rows(s * rb + 32, 16)], b_ref[p // 8].at[p % 8, pl.ds(0, 16)])
+            go(dwv.at[rows(s * rb, 48)], b_ref[p // 8].at[p % 8, pl.ds(16, 48)])
 
     @pl.when(ids[1] == 0)
     def _():
@@ -1023,7 +1072,7 @@
 
     def store_bias(b_ref):
         for p in range(NB):
-            go(bias.at[pl.ds(16 * p, 16)], b_ref.at[p, pl.ds(64, 16)])
+            go(bias.at[pl.ds(16 * p, 16)], b_ref[p // 8].at[p % 8, pl.ds(64, 16)])
 
     @pl.when(ids[1] == 0)
     def _():
@@ -1033,14 +1082,14 @@
     def _():
         store_bias(keep)
 
-    wait_all(keep, sems.at[0])
-    wait_all(send, sems.at[0])
+    for x in keep + send:
+        wait_all(x, sems.at[0])
 
 
 def weight_grads(ids, pool, tok, dq, dk, dv, gvec, gup, sl, set_rows):
     width = tok.shape[1]
     full = lambda x: pl.BlockSpec(x.shape, lambda i, *_: (0, 0))
-    big = jax.ShapeDtypeStruct((NB, set_rows, width), BF)
+    big = jax.ShapeDtypeStruct((NB // 2, set_rows, width), BF)
     square = pltpu.VMEM((width, width), BF)
     return pl.pallas_call(
         weights_kernel,
@@ -1050,7 +1099,7 @@
             num_scalar_prefetch=1,
             grid=(1,),
             in_specs=[full(x) for x in (pool, tok, dq, dk, dv, gvec, gup, sl)],
-            out_specs=[ANY, ANY],
+            out_specs=[ANY] * 4,
             scratch_shapes=[
                 square,
                 square,
@@ -1060,7 +1109,7 @@
                 pltpu.SemaphoreType.DMA((1,)),
             ],
         ),
-        out_shape=[big, big],
+        out_shape=[big] * 4,
         compiler_params=params(),
     )(ids, pool, tok, dq, dk, dv, gvec, gup, sl)
 
@@ -1180,9 +1229,11 @@
     )(ids, *args)
 
 
-def unpack_kernel(ids, mine1, other1, mine2, other2, wq, wk, wv, wo, w1, w2, *vectors):
+def unpack_kernel(ids, low1, got1, olow1, ogot1, mine2, other2, wq, wk, wv, wo, w1, w2, *vectors):
     width = wq.shape[1]
     rb = wq.shape[0]
+    mine1 = low1[...] + got1[...].astype(FL)
+    other1 = olow1[...] + ogot1[...].astype(FL)
 
     def store(a1, b1, a2, b2):
         wq[...] = a1[0:48]
@@ -1347,49 +1398,50 @@
     if direct:
         high2, lse = lax.optimization_barrier((exchange(low2, 1, 2), lse))
         sets2 = (low2, high2, swap_core(low2), swap_core(high2))
-    out, pay, stats, mixed, gvec, gup, keep2, send2 = middle(
+    out, pay, pay_low, pay_high, stats, mixed, gvec, gup, keep2, send2 = middle(
         ids, pool, att, exact, lse, cotangent, vec, upb, sets2, 224
     )
-    low_pay = lax.ppermute(pay[own // 2 :], order, up_pairs)
-    high_pay = lax.ppermute(pay[: own // 2], order, down_pairs)
+    low_pay = lax.ppermute(pay_high, order, up_pairs)
+    high_pay = lax.ppermute(pay_low, order, down_pairs)
     if direct:
         got = swap_core(send2)
         up = add(keep2[8:], got[8:]).astype(BF)
         bounds = after(bounds, up)
     dq, dk, dv, sl = attend_own(spans, slopes, q, k, v, kt, pay, stats, bounds)
     if direct:
-        got1, dq, low_pay, high_pay = lax.optimization_barrier((exchange(up, 1, 2), dq, low_pay, high_pay))
+        dq, low_pay, high_pay = lax.optimization_barrier((dq, low_pay, high_pay))
+    dk, dv = attend_halo(spans, slopes, qh, k, v, low_pay, high_pay, bounds, dk, dv)
+    if direct:
+        got1, dk = lax.optimization_barrier((exchange(up, 1, 2), dk))
         up = add(keep2[4:8], got[4:8], got1[4:]).astype(BF)
-        bounds = after(bounds, up)
-    dk, dv = attend_halo(spans, slopes, qh, k, v, low_pay, high_pay, bounds, dk, dv)
-    keep1, send1 = weight_grads(ids, pool, tokens, dq, dk, dv, gvec, gup, sl, 80)
+        sl = after(sl, up)
+    keep1, keep1_up, send1, send1_up = weight_grads(ids, pool, tokens, dq, dk, dv, gvec, gup, sl, 80)
     if direct:
-        got2, keep1, send1 = lax.optimization_barrier((exchange(up, 2, 1), keep1, send1))
+        gots = swap_core(send1)
+        part, got2 = lax.optimization_barrier((add(keep1_up, swap_core(send1_up)).astype(BF), exchange(up, 2, 1)))
         low = add(keep2[:4], got[:4], got1[:4])
         up = (low[2:] + got2[2:].astype(FL)).astype(BF)
         low = low[:2] + got2[:2].astype(FL)
-        got, up = lax.optimization_barrier((swap_core(send1), up))
-        part = add(keep1[8:], got[8:]).astype(BF)
-        mixed = after(mixed, part)
+        mixed = after(mixed, part, up)
     grad_tokens = token_grads(mixed, dq, dk, dv, wq, wk, wv)
 
     if direct:
-        got3, got1, grad_tokens = lax.optimization_barrier((exchange(up, 4, 8), exchange(part, 1, 2), grad_tokens))
-        part = add(keep1[4:8], got[4:8], got1[4:]).astype(BF)
+        got3, one, grad_tokens = lax.optimization_barrier((exchange(up, 4, 8), exchange(part, 1, 2), grad_tokens))
+        part = add(keep1[4:8], gots[4:8], one[4:]).astype(BF)
         up = (low[1:] + got3[1:].astype(FL)).astype(BF)
         low = low[:1] + got3[:1].astype(FL)
-        got4, got2 = lax.optimization_barrier((exchange(up, 8, 4), exchange(part, 2, 1)))
+        got4, two = lax.optimization_barrier((exchange(up, 8, 4), exchange(part, 2, 1)))
         mine = (low + got4.astype(FL))[0]
-        low = add(keep1[:4], got[:4], got1[:4])
-        part = (low[2:] + got2[2:].astype(FL)).astype(BF)
-        low = low[:2] + got2[:2].astype(FL)
-        got3, other = lax.optimization_barrier((exchange(part, 4, 8), swap_core(mine)))
+        rest = add(keep1[:4], gots[:4], one[:4])
+        part = (rest[2:] + two[2:].astype(FL)).astype(BF)
+        rest = rest[:2] + two[:2].astype(FL)
+        three, other = lax.optimization_barrier((exchange(part, 4, 8), swap_core(mine)))
         second = (mine, other)
-        part = (low[1:] + got3[1:].astype(FL)).astype(BF)
-        low = low[:1] + got3[:1].astype(FL)
-        mine = (low + exchange(part, 8, 4).astype(FL))[0]
-        other = swap_core(mine)
-        gq, gk, gv, go, g1, g2, *small = unpack_own(ids, (mine, other) + second, ff)
+        part = (rest[1:] + three[1:].astype(FL)).astype(BF)
+        rest = rest[:1] + three[:1].astype(FL)
+        over = [(s, seq + (s ^ 8)) for s in range(seq)] + [(seq + s, s ^ 4) for s in range(seq)]
+        first = (rest[0], exchange(part, 8, 4)[0], swap_core(rest)[0], lax.ppermute(part, order, over)[0])
+        gq, gk, gv, go, g1, g2, *small = unpack_own(ids, first + second, ff)
         g_up, g_slope = small[8][0], small[9][0, : distance_slope.shape[0]]
         small = [x[0] for x in small[:8]]
     else:
@@ -1400,7 +1452,8 @@
             inv_b[rel_b(p)] = p
         inv_a = jnp.array(inv_a)
         inv_b = jnp.array(inv_b)
-        gq, gk, gv, go, g1, g2, gb = unpack(keep1[inv_a], send1[inv_b], keep2[inv_a], send2[inv_b], width)
+        joined = [jnp.concatenate(x, 0) for x in ((keep1, keep1_up), (send1, send1_up))]
+        gq, gk, gv, go, g1, g2, gb = unpack(joined[0][inv_a], joined[1][inv_b], keep2[inv_a], send2[inv_b], width)
         rb = width // NB
 
         def share(x):

time: 326 us -> 316 us (0.969)
  local copies, waits for them, and re-layouts: 12.2 us -> 8.86 us
    ppermute x16, waiting for transfers between devices: 73.3 us -> 66.4 us  [exchange(): return lax.ppermute(x, ('dp', 'seq'), pairs)]
    convert_element_type x4 -> x5, other arithmetic: 2.85 us -> 8.96 us  [the longest x1 4.62 us: local(): up = add(keep2[4:8], got[4:8], got1[4:]).astype(BF)]
    add x1 -> x0, other arithmetic: 4.75 us -> none  [add(): total = total + x.astype(FL)]
    ppermute x16, starting transfers between devices: 29.3 us -> 25.7 us  [exchange(): return lax.ppermute(x, ('dp', 'seq'), pairs)]
    ppermute x8 -> x9, waiting for transfers between devices: 8.98 us -> 11.7 us  [swap_core(): return lax.ppermute(x, 'dp', [(0, 1), (1, 0)])]
    ppermute x8 -> x9, starting transfers between devices: 8.65 us -> 10.5 us  [swap_core(): return lax.ppermute(x, 'dp', [(0, 1), (1, 0)])]
    ppermute x2 -> x3, starting transfers between devices: 6.65 us -> 5.61 us  [the longest x1 3.94 us: local(): low_pay = lax.ppermute(pay_high, order, up_pairs)]
  transfers between devices with their start and end apart: 30 -> 32, of which waited for: 13 -> 14; matrix products, arithmetic and copies ran while one was open for 4% -> 3% of each run, Pallas kernels for 29% -> 29%
where the time goes in v1:
time: 316 us
  Pallas kernels  135 us (43%)
  waiting for transfers between devices  97.9 us (31%)
  starting transfers between devices  56.1 us (18%)
  other arithmetic  16.6 us (5%)
  local copies, waits for them, and re-layouts  8.86 us (3%)
    ppermute x16, waiting for transfers between devices, exchange(): return lax.ppermute(x, ('dp', 'seq'), pairs)  66.4 us
    pallas_call x1, Pallas kernels, middle(): pl.pallas_call(middle_kernel, name='middle', cost_estimate=takes(36), gri...  36.7 us
    pallas_call x1, Pallas kernels, attend_own(): pl.pallas_call(own_kernel, name='attend_own', cost_estimate=takes(30), gr...  25.7 us
    ppermute x16, starting transfers between devices, exchange(): return lax.ppermute(x, ('dp', 'seq'), pairs)  25.7 us
    pallas_call x1, Pallas kernels, attend_forward(): pl.pallas_call(forward_kernel, name='attend_forward', cost_estimate=takes...  23.6 us
    ppermute x1, waiting for transfers between devices, local(): lax.ppermute(after(tokens[:halo // 2], x1), order, down_pairs)  18.4 us
    ppermute x9, waiting for transfers between devices, swap_core(): return lax.ppermute(x, 'dp', [(0, 1), (1, 0)])  11.7 us
    ppermute x9, starting transfers between devices, swap_core(): return lax.ppermute(x, 'dp', [(0, 1), (1, 0)])  10.5 us
  transfers between devices with their start and end apart: 32, of which 14 were waited for; matrix products, arithmetic and copies ran while one was open for 3% of the time, Pallas kernels for 29%

profile of v1, /device:TPU:0, one launch (start us, length us, event | category | flops | bytes accessed | tf_op | source)
XLA Modules:
  0.0 316.0 jit_solution(9476588346104527237)
XLA Ops:
  1.2 3.2 %pack.1 = bf16[1,304,768]{2,1,0:T(8,128)(2,1)} custom-call(s32[2]{0:T(128)} %pad_add_fusion.ids, f32[48,768]{1,0:T(8,128)} %wq.1, f32[48,768]{1,0:T(8,128)} %wk.1, f32[48,768]{1,0:T(8,128)} %wv.1, f32[48,768]{1,0:T(8,128)} %wo.1, f32[48,3072]{1,0:T(8,128)} %w1.1, f32[192,768]{1,0:T(8,128)} %w2.1, f32[1,192]{1,0:T(1,128)} %bitcast.48, f32[1,48]{1,0:T(1,128)} %bitcast.49, ...), custom_call_target="tpu_custom_call" | custom-call | flops 3449999872 | bytes 10800000 | tf_op jit(solution)/shard_map/pack/pallas_call | solution.py:1216
  5.4 4.1 %collective-permute-start = (bf16[1,80,768]{2,1,0:T(8,128)(2,1)S(1)}, bf16[1,80,768]{2,1,0:T(8,128)(2,1)S(1)}, u32[]{:S(2)}, u32[]{:S(2)}) collective-permute-start(bf16[1,80,768]{2,1,0:T(8,128)(2,1)S(1)} %slice.157), channel_id=1, source_target_pairs={{0,8},{1,9},{2,10},{3,11},{4,12},{5,13},{6,14},{7,15},{8,0},{9,1},... | collective-permute-start | bytes 368648 | tf_op jit(solution)/shard_map/ppermute | solution.py:43
  9.6 4.2 %collective-permute-start.2 = (bf16[256,768]{1,0:T(8,128)(2,1)S(1)}, bf16[256,768]{1,0:T(8,128)(2,1)}, u32[]{:S(2)}, u32[]{:S(2)}) collective-permute-start(bf16[256,768]{1,0:T(8,128)(2,1)S(1)} %get-tuple-element.217), channel_id=1, source_target_pairs={{0,1},{1,2},{2,3},{3,4},{4,5},{5,6},{6,7},{7,8},{8,9},{9,10},{10,1... | collective-permute-start | bytes 1179656 | tf_op jit(solution)/shard_map/ppermute | solution.py:1329
  14.7 7.6 %collective-permute-done.1 = bf16[2,80,768]{2,1,0:T(8,128)(2,1)S(1)} collective-permute-done((bf16[2,80,768]{2,1,0:T(8,128)(2,1)S(1)}, bf16[2,80,768]{2,1,0:T(8,128)(2,1)S(1)}, u32[]{:S(2)}, u32[]{:S(2)}) %collective-permute-start.1) | collective-permute-done | bytes 245792 | tf_op jit(solution)/shard_map/ppermute | solution.py:43
  22.4 1.3 collective-permute-start.3
  23.7 7.5 %collective-permute-start.5 = (bf16[256,768]{1,0:T(8,128)(2,1)S(1)}, bf16[256,768]{1,0:T(8,128)(2,1)}, u32[]{:S(2)}, u32[]{:S(2)}) collective-permute-start(bf16[256,768]{1,0:T(8,128)(2,1)S(1)} %get-tuple-element.112), channel_id=1, source_target_pairs={{0,1},{1,2},{2,3},{3,4},{4,5},{5,6},{6,7},{7,8},{8,9},{9,10},{10,1... | collective-permute-start | bytes 1179656 | tf_op jit(solution)/shard_map/ppermute | solution.py:1334
  31.3 1.3 collective-permute-start.4
  33.2 9.9 %collective-permute-done.4 = bf16[1,224,768]{2,1,0:T(8,128)(2,1)S(1)} collective-permute-done((bf16[1,224,768]{2,1,0:T(8,128)(2,1)S(1)}, bf16[1,224,768]{2,1,0:T(8,128)(2,1)S(1)}, u32[]{:S(2)}, u32[]{:S(2)}) %collective-permute-start.4) | collective-permute-done | bytes 344096 | tf_op jit(solution)/shard_map/ppermute | solution.py:43
  43.3 1.3 collective-permute-start.6
  45.5 1.3 collective-permute-start.9
  47.5 18.4 %collective-permute-done.9.high_a = bf16[256,768]{1,0:T(8,128)(2,1)S(1)} collective-permute-done((bf16[256,768]{1,0:T(8,128)(2,1)S(1)}, bf16[256,768]{1,0:T(8,128)(2,1)S(1)}, u32[]{:S(2)}, u32[]{:S(2)}) %collective-permute-start.9) | collective-permute-done | bytes 393248 | tf_op jit(solution)/shard_map/ppermute | solution.py:1343
  66.0 1.6 collective-permute-start.10
  68.3 1.3 collective-permute-start.11
  69.7 2.7 collective-permute-start.12
  72.5 1.5 copy-done.7
  74.0 10.4 %qkv.1 = (bf16[512,768]{1,0:T(8,128)(2,1)}, bf16[2048,768]{1,0:T(8,128)(2,1)}, bf16[2048,768]{1,0:T(8,128)(2,1)}, bf16[8,768,256]{2,1,0:T(8,128)(2,1)}, bf16[8,7...) custom-call(s32[2]{0:T(128)} %pad_add_fusion.ids, ...), custom_call_target="tpu_custom_call" | custom-call | flops 10350000128 | bytes 32400000 | tf_op jit(solution)/shard_map/qkv/pallas_call | solution.py:168
  84.4 7.0 %halo_qkv.1 = (bf16[2,256,768]{2,1,0:T(8,128)(2,1)}, bf16[2048,768]{1,0:T(8,128)(2,1)}, bf16[2048,768]{1,0:T(8,128)(2,1)}, bf16[8,768,256]{2,1,0:T(8,128)(2,1)}, bf16[8,768,256]{2,1,0:T(8,128)(2,1)}) custom-call(bf16[256,768]{1,0:T(8,128)(2,1)} %collective-permute-done.2.low_a, ...), custom_call_target="tpu_custom_call", output_to_operand_aliasing={{1}: (8, {}), {2}: (9, {}), {3}: (10, {}), {4}: (11, {})} | custom-call | flops 8049999872 | bytes 25200000 | tf_op jit(solution)/shard_map/halo_qkv/pallas_call | solution.py:217
  92.7 7.9 %collective-permute-start.14 = (bf16[8,224,768]{2,1,0:T(8,128)(2,1)}, bf16[8,224,768]{2,1,0:T(8,128)(2,1)S(1)}, u32[]{:S(2)}, u32[]{:S(2)}) collective-permute-start(bf16[8,224,768]{2,1,0:T(8,128)(2,1)} %constant_dynamic-update-slice_fusion.low), channel_id=1, source_target_pairs={{0,16},{16,0},{1,17},{17,1},{2,18},{18,2},{3,19},{19,3},{4,20},{20... | collective-permute-start | bytes 8257544 | tf_op jit(solution)/shard_map/ppermute | solution.py:47
  100.6 2.4 collective-permute-start.13
  103.0 23.6 %attend_forward.1 = (bf16[512,768]{1,0:T(8,128)(2,1)}, f32[512,768]{1,0:T(8,128)}, f32[16,512]{1,0:T(8,128)}) custom-call(s32[16]{0:T(128)} %pad_add_fusion.1.spans, f32[12]{0:T(128)} %slopes.5, bf16[512,768]{1,0:T(8,128)(2,1)} %get-tuple-element.119.q, bf16[2048,768]{1,0:T(8,128)(2,1)} %get-tuple-element.134.k.ka.kb, ...), custom_call_target="tpu_custom_call" | custom-call | flops 34500001792 | bytes 108000000 | tf_op jit(solution)/shard_map/attend_forward/pallas_call | solution.py:343
  126.7 7.6 %collective-permute-done.13.high = bf16[8,224,768]{2,1,0:T(8,128)(2,1)S(1)} collective-permute-done((bf16[8,224,768]{2,1,0:T(8,128)(2,1)}, bf16[8,224,768]{2,1,0:T(8,128)(2,1)S(1)}, u32[]{:S(2)}, u32[]{:S(2)}) %collective-permute-start.13) | collective-permute-done | bytes 2752544 | tf_op jit(solution)/shard_map/ppermute | solution.py:43
  134.3 5.1 %collective-permute-done.15.ohigh = bf16[8,224,768]{2,1,0:T(8,128)(2,1)S(1)} collective-permute-done((bf16[8,224,768]{2,1,0:T(8,128)(2,1)S(1)}, bf16[8,224,768]{2,1,0:T(8,128)(2,1)S(1)}, u32[]{:S(2)}, u32[]{:S(2)}) %collective-permute-start.15) | collective-permute-done | bytes 2752544 | tf_op jit(solution)/shard_map/ppermute | solution.py:47
  139.4 1.5 copy-done.11
  140.9 36.7 %middle.1 = (bf16[512,768]{1,0:T(8,128)(2,1)}, bf16[512,768]{1,0:T(8,128)(2,1)}, bf16[256,896]{1,0:T(8,128)(2,1)}, bf16[256,896]{1,0:T(8,128)(2,1)}, f32[32,512]...) custom-call(s32[2]{0:T(128)} %pad_add_fusion.ids, ...), custom_call_target="tpu_custom_call" | custom-call | flops 41400000512 | bytes 129600000 | tf_op jit(solution)/shard_map/middle/pallas_call | solution.py:970
  177.7 3.9 %collective-permute-start.18 = (bf16[256,896]{1,0:T(8,128)(2,1)}, bf16[256,896]{1,0:T(8,128)(2,1)S(1)}, u32[]{:S(2)}, u32[]{:S(2)}) collective-permute-start(bf16[256,896]{1,0:T(8,128)(2,1)} %get-tuple-element.156), channel_id=1, source_target_pairs={{0,1},{1,2},{2,3},{3,4},{4,5},{5,6},{6,7},{7,8},{8,9},{9,10},{10,1... | collective-permute-start | bytes 1376264 | tf_op jit(solution)/shard_map/ppermute | solution.py:1404
  181.6 1.5 collective-permute-start.19
  183.2 3.7 %collective-permute-done.16 = bf16[16,224,768]{2,1,0:T(8,128)(2,1)S(1)} collective-permute-done((bf16[16,224,768]{2,1,0:T(8,128)(2,1)}, bf16[16,224,768]{2,1,0:T(8,128)(2,1)S(1)}, u32[]{:S(2)}, u32[]{:S(2)}) %collective-permute-start.16) | collective-permute-done | bytes 5505056 | tf_op jit(solution)/shard_map/ppermute | solution.py:47
  186.9 4.5 %add_convert_fusion = bf16[8,224,768]{2,1,0:T(8,128)(2,1)S(1)} fusion(bf16[16,224,768]{2,1,0:T(8,128)(2,1)S(1)} %collective-permute-done.16, bf16[16,224,768]{2,1,0:T(8,128)(2,1)} %get-tuple-element.147), kind=kLoop, calls=%fused_computation | loop fusion | flops 5505024 | bytes 8257536 | tf_op jit(solution)/shard_map/convert_element_type | solution.py:1408
  191.4 2.1 collective-permute-start.17
  193.5 25.7 %attend_own.1 = (bf16[512,768]{1,0:T(8,128)(2,1)}, f32[1024,768]{1,0:T(8,128)}, f32[1024,768]{1,0:T(8,128)}, f32[48,256]{1,0:T(8,128)}) custom-call(s32[16]{0:T(128)} %pad_add_fusion.1.spans, f32[12]{0:T(128)} %slopes.5, bf16[512,768]{1,0:T(8,128)(2,1)} %get-tuple-element.119.q, bf16[2048,768]{1,0:T(8,128)(2,1)} %get-tuple-element.134.k.ka.kb, ...), custom_call_target="tpu_custom_call" | custom-call | flops 34500001792 | bytes 108000000 | tf_op jit(solution)/shard_map/attend_own/pallas_call | solution.py:554
  220.0 7.9 %attend_halo.1 = (bf16[1024,768]{1,0:T(8,128)(2,1)}, bf16[1024,768]{1,0:T(8,128)(2,1)}) custom-call(s32[16]{0:T(128)} %pad_add_fusion.1.spans, f32[12]{0:T(128)} %slopes.5, bf16[2,256,768]{2,1,0:T(8,128)(2,1)} %get-tuple-element.149.q, bf16[2048,768]{1,0:T(8,128)(2,1)} %get-tuple-element.134.k.ka.kb, bf16[2048,768]{1,0:T(8,128)(2,1)} %get-tuple-element.134.k.ka.kb, ...), custom_call_target="tpu_custom_call" | custom-call | flops 13799999488 | bytes 43200000 | tf_op jit(solution)/shard_map/attend_halo/pallas_call | solution.py:701
  227.8 6.1 %collective-permute-done.17 = bf16[8,224,768]{2,1,0:T(8,128)(2,1)S(1)} collective-permute-done((bf16[8,224,768]{2,1,0:T(8,128)(2,1)S(1)}, bf16[8,224,768]{2,1,0:T(8,128)(2,1)S(1)}, u32[]{:S(2)}, u32[]{:S(2)}) %collective-permute-start.17) | collective-permute-done | bytes 2752544 | tf_op jit(solution)/shard_map/ppermute | solution.py:43
  233.9 4.6 %add_convert_fusion.1 = (bf16[4,224,768]{2,1,0:T(8,128)(2,1)}, f32[4,224,768]{2,1,0:T(8,128)S(1)}) fusion(bf16[16,224,768]{2,1,0:T(8,128)(2,1)} %copy-done, bf16[8,224,768]{2,1,0:T(8,128)(2,1)S(1)} %collective-permute-done.17, bf16[16,224,768]{2,1,0:T(8,128)(2,1)} %get-tuple-element.147), kind=kLoop, calls=%fused_computation.1 | loop fusion | flops 7569408 | bytes 12386304 | tf_op jit(solution)/shard_map/convert_element_type | solution.py:1416
  238.5 2.4 collective-permute-start.21
  240.9 9.6 %weight_grads.1 = (bf16[8,80,768]{2,1,0:T(8,128)(2,1)}, bf16[8,80,768]{2,1,0:T(8,128)(2,1)}, bf16[8,80,768]{2,1,0:T(8,128)(2,1)}, bf16[8,80,768]{2,1,0:T(8,128)(2,1)}) custom-call(s32[2]{0:T(128)} %pad_add_fusion.ids, f32[512,768]{1,0:T(8,128)} %get-tuple-element.118.pool, bf16[1024,768]{1,0:T(8,128)(2,1)} %tok.3, bf16[512,768]{1,0:T(8,128)(2,1)} %get-tuple-element.164.dq, ...), custom_call_target="tpu_custom_call" | custom-call | flops 10350000128 | bytes 32400000 | tf_op jit(solution)/shard_map/weight_grads/pallas_call | solution.py:1094
  251.1 2.9 collective-permute-done.20
  254.0 2.4 add_convert_fusion.2
  257.9 1.7 collective-permute-start.22
  259.6 7.7 %token_grads.1 = f32[1024,768]{1,0:T(8,128)} custom-call(f32[512,768]{1,0:T(8,128)} %get-tuple-element.176.mixed, bf16[512,768]{1,0:T(8,128)(2,1)} %get-tuple-element.164.dq, bf16[1024,768]{1,0:T(8,128)(2,1)} %get-tuple-element.165.dk, bf16[1024,768]{1,0:T(8,128)(2,1)} %get-tuple-element.166.dv, bf16[768,768]{1,0:T(8,128)(2,1)} %get-tuple-element.126.wq, ...), custom_call_target="tpu_custom_call" | custom-call | flops 9200000000 | bytes 28800000 | tf_op jit(solution)/shard_map/token_grads/pallas_call | solution.py:1134
  267.3 8.9 %collective-permute-done.22 = bf16[2,224,768]{2,1,0:T(8,128)(2,1)S(1)} collective-permute-done((bf16[2,224,768]{2,1,0:T(8,128)(2,1)S(1)}, bf16[2,224,768]{2,1,0:T(8,128)(2,1)S(1)}, u32[]{:S(2)}, u32[]{:S(2)}) %collective-permute-start.22) | collective-permute-done | bytes 688160 | tf_op jit(solution)/shard_map/ppermute | solution.py:43
  276.2 1.8 add_convert_fusion.3
  278.0 2.1 collective-permute-start.26
  280.2 11.3 %collective-permute-done.25 = bf16[1,224,768]{2,1,0:T(8,128)(2,1)S(1)} collective-permute-done((bf16[1,224,768]{2,1,0:T(8,128)(2,1)S(1)}, bf16[1,224,768]{2,1,0:T(8,128)(2,1)S(1)}, u32[]{:S(2)}, u32[]{:S(2)}) %collective-permute-start.25) | collective-permute-done | bytes 344096 | tf_op jit(solution)/shard_map/ppermute | solution.py:43
  292.0 8.8 %collective-permute-done.27 = bf16[2,80,768]{2,1,0:T(8,128)(2,1)S(1)} collective-permute-done((bf16[2,80,768]{2,1,0:T(8,128)(2,1)S(1)}, bf16[2,80,768]{2,1,0:T(8,128)(2,1)S(1)}, u32[]{:S(2)}, u32[]{:S(2)}) %collective-permute-start.27) | collective-permute-done | bytes 245792 | tf_op jit(solution)/shard_map/ppermute | solution.py:43
  301.1 2.9 collective-permute-start.29
  303.9 1.3 collective-permute-done.31
  305.3 5.1 %collective-permute-done.29 = bf16[1,80,768]{2,1,0:T(8,128)(2,1)S(1)} collective-permute-done((bf16[1,80,768]{2,1,0:T(8,128)(2,1)S(1)}, bf16[1,80,768]{2,1,0:T(8,128)(2,1)S(1)}, u32[]{:S(2)}, u32[]{:S(2)}) %collective-permute-start.29) | collective-permute-done | bytes 122912 | tf_op jit(solution)/shard_map/ppermute | solution.py:43
  311.1 3.7 %unpack.1 = (f32[48,768]{1,0:T(8,128)}, f32[48,768]{1,0:T(8,128)}, f32[48,768]{1,0:T(8,128)}, f32[48,768]{1,0:T(8,128)}, f32[48,3072]{1,0:T(8,128)}, /*index=5*/...) custom-call(s32[2]{0:T(128)} %pad_add_fusion.ids, ...), custom_call_target="tpu_custom_call" | custom-call | flops 3449999872 | bytes 10800000 | tf_op jit(solution)/shard_map/unpack/pallas_call | solution.py:1268
  (104 shorter events, 12.7 us)
Async XLA Ops:
  1.2 8.3 %copy-start.1 = (bf16[1024,768]{1,0:T(8,128)(2,1)S(1)}, bf16[1024,768]{1,0:T(8,128)(2,1)}, u32[]{:S(2)}) copy-start(bf16[1024,768]{1,0:T(8,128)(2,1)} %tok.3) | copy-start | bytes 4718596
  4.4 19.3 %copy-start.5 = (bf16[1,304,768]{2,1,0:T(8,128)(2,1)S(1)}, bf16[1,304,768]{2,1,0:T(8,128)(2,1)}, u32[]{:S(2)}) copy-start(bf16[1,304,768]{2,1,0:T(8,128)(2,1)} %pack.1) | copy-start | bytes 1400836
  4.4 28.2 %copy-start.8 = (s32[256]{0:T(256)S(1)}, s32[256]{0:T(256)}, u32[]{:S(2)}) copy-start(s32[256]{0:T(256)} %param.21) | copy-start | bytes 3076
  5.4 8.4 %collective-permute-start = (bf16[1,80,768]{2,1,0:T(8,128)(2,1)S(1)}, bf16[1,80,768]{2,1,0:T(8,128)(2,1)S(1)}, u32[]{:S(2)}, u32[]{:S(2)}) collective-permute-start(bf16[1,80,768]{2,1,0:T(8,128)(2,1)S(1)} %slice.157), channel_id=1, source_target_pairs={{0,8},{1,9},{2,10},{3,11},{4,12},{5,13},{6,14},{7,15},{8,0},{9,1},... | collective-permute-start | bytes 368648 | tf_op jit(solution)/shard_map/ppermute | solution.py:43
  9.6 12.8 %collective-permute-start.2 = (bf16[256,768]{1,0:T(8,128)(2,1)S(1)}, bf16[256,768]{1,0:T(8,128)(2,1)}, u32[]{:S(2)}, u32[]{:S(2)}) collective-permute-start(bf16[256,768]{1,0:T(8,128)(2,1)S(1)} %get-tuple-element.217), channel_id=1, source_target_pairs={{0,1},{1,2},{2,3},{3,4},{4,5},{5,6},{6,7},{7,8},{8,9},{9,10},{10,1... | collective-permute-start | bytes 1179656 | tf_op jit(solution)/shard_map/ppermute | solution.py:1329
  13.8 8.6 %collective-permute-start.1 = (bf16[2,80,768]{2,1,0:T(8,128)(2,1)S(1)}, bf16[2,80,768]{2,1,0:T(8,128)(2,1)S(1)}, u32[]{:S(2)}, u32[]{:S(2)}) collective-permute-start(bf16[2,80,768]{2,1,0:T(8,128)(2,1)S(1)} %pad_maximum_fusion.4), channel_id=1, source_target_pairs={{0,4},{1,5},{2,6},{3,7},{4,0},{5,1},{6,2},{7,3},{8,12},{9,13},{10,... | collective-permute-start | bytes 737288 | tf_op jit(solution)/shard_map/ppermute | solution.py:43
  22.4 20.7 %collective-permute-start.3 = (bf16[4,80,768]{2,1,0:T(8,128)(2,1)S(1)}, bf16[4,80,768]{2,1,0:T(8,128)(2,1)S(1)}, u32[]{:S(2)}, u32[]{:S(2)}) collective-permute-start(bf16[4,80,768]{2,1,0:T(8,128)(2,1)S(1)} %pad_maximum_fusion.3), channel_id=1, source_target_pairs={{0,2},{1,3},{2,0},{3,1},{4,6},{5,7},{6,4},{7,5},{8,10},{9,11},{10,... | collective-permute-start | bytes 1474568 | tf_op jit(solution)/shard_map/ppermute | solution.py:43
  23.7 19.4 %collective-permute-start.5 = (bf16[256,768]{1,0:T(8,128)(2,1)S(1)}, bf16[256,768]{1,0:T(8,128)(2,1)}, u32[]{:S(2)}, u32[]{:S(2)}) collective-permute-start(bf16[256,768]{1,0:T(8,128)(2,1)S(1)} %get-tuple-element.112), channel_id=1, source_target_pairs={{0,1},{1,2},{2,3},{3,4},{4,5},{5,6},{6,7},{7,8},{8,9},{9,10},{10,1... | collective-permute-start | bytes 1179656 | tf_op jit(solution)/shard_map/ppermute | solution.py:1334
  31.3 11.8 %collective-permute-start.4 = (bf16[1,224,768]{2,1,0:T(8,128)(2,1)S(1)}, bf16[1,224,768]{2,1,0:T(8,128)(2,1)S(1)}, u32[]{:S(2)}, u32[]{:S(2)}) collective-permute-start(bf16[1,224,768]{2,1,0:T(8,128)(2,1)S(1)} %slice.158), channel_id=1, source_target_pairs={{0,8},{1,9},{2,10},{3,11},{4,12},{5,13},{6,14},{7,15},{8,0},{9,1},... | collective-permute-start | bytes 1032200 | tf_op jit(solution)/shard_map/ppermute | solution.py:43
  43.2 26.5 %copy-start.2 = (bf16[8,80,768]{2,1,0:T(8,128)(2,1)}, bf16[8,80,768]{2,1,0:T(8,128)(2,1)S(1)}, u32[]{:S(2)}) copy-start(bf16[8,80,768]{2,1,0:T(8,128)(2,1)S(1)} %pad_maximum_fusion.1.low) | copy-start | bytes 2949124
  43.3 22.7 %collective-permute-start.7 = (bf16[8,80,768]{2,1,0:T(8,128)(2,1)S(1)}, bf16[8,80,768]{2,1,0:T(8,128)(2,1)S(1)}, u32[]{:S(2)}, u32[]{:S(2)}) collective-permute-start(bf16[8,80,768]{2,1,0:T(8,128)(2,1)S(1)} %pad_maximum_fusion.1.low), channel_id=1, source_target_pairs={{0,16},{16,0},{1,17},{17,1},{2,18},{18,2},{3,19},{19,3},{4,20},{20... | collective-permute-start | bytes 2949128 | tf_op jit(solution)/shard_map/ppermute | solution.py:47
  43.3 22.6 %collective-permute-start.6 = (bf16[8,80,768]{2,1,0:T(8,128)(2,1)S(1)}, bf16[8,80,768]{2,1,0:T(8,128)(2,1)S(1)}, u32[]{:S(2)}, u32[]{:S(2)}) collective-permute-start(bf16[8,80,768]{2,1,0:T(8,128)(2,1)S(1)} %pad_maximum_fusion.1.low), channel_id=1, source_target_pairs={{0,1},{1,0},{2,3},{3,2},{4,5},{5,4},{6,7},{7,6},{8,9},{9,8},{10,11... | collective-permute-start | bytes 2949128 | tf_op jit(solution)/shard_map/ppermute | solution.py:43
  44.7 21.2 %collective-permute-start.8 = (bf16[2,224,768]{2,1,0:T(8,128)(2,1)S(1)}, bf16[2,224,768]{2,1,0:T(8,128)(2,1)S(1)}, u32[]{:S(2)}, u32[]{:S(2)}) collective-permute-start(bf16[2,224,768]{2,1,0:T(8,128)(2,1)S(1)} %pad_maximum_fusion.2), channel_id=1, source_target_pairs={{0,4},{1,5},{2,6},{3,7},{4,0},{5,1},{6,2},{7,3},{8,12},{9,13},{10,... | collective-permute-start | bytes 2064392 | tf_op jit(solution)/shard_map/ppermute | solution.py:43
  45.5 20.4 %collective-permute-start.9 = (bf16[256,768]{1,0:T(8,128)(2,1)S(1)}, bf16[256,768]{1,0:T(8,128)(2,1)S(1)}, u32[]{:S(2)}, u32[]{:S(2)}) collective-permute-start(bf16[256,768]{1,0:T(8,128)(2,1)S(1)} %get-tuple-element.115), channel_id=1, source_target_pairs={{1,0},{2,1},{3,2},{4,3},{5,4},{6,5},{7,6},{8,7},{9,8},{10,9},{11,1... | collective-permute-start | bytes 1179656 | tf_op jit(solution)/shard_map/ppermute | solution.py:1343
  65.9 2.4 copy-start.16
  65.9 6.6 %copy-start.12 = (bf16[8,80,768]{2,1,0:T(8,128)(2,1)}, bf16[8,80,768]{2,1,0:T(8,128)(2,1)S(1)}, u32[]{:S(2)}) copy-start(bf16[8,80,768]{2,1,0:T(8,128)(2,1)S(1)} %collective-permute-done.7.olow) | copy-start | bytes 2949124
  66.0 6.6 %copy-start.13 = (bf16[8,80,768]{2,1,0:T(8,128)(2,1)}, bf16[8,80,768]{2,1,0:T(8,128)(2,1)S(1)}, u32[]{:S(2)}) copy-start(bf16[8,80,768]{2,1,0:T(8,128)(2,1)S(1)} %collective-permute-done.6.high) | copy-start | bytes 2949124
  66.0 8.1 %collective-permute-start.10 = (bf16[8,80,768]{2,1,0:T(8,128)(2,1)S(1)}, bf16[8,80,768]{2,1,0:T(8,128)(2,1)}, u32[]{:S(2)}, u32[]{:S(2)}) collective-permute-start(bf16[8,80,768]{2,1,0:T(8,128)(2,1)S(1)} %collective-permute-done.6.high), channel_id=1, source_target_pairs={{0,16},{16,0},{1,17},{17,1},{2,18},{18,2},{3,19},{19,3},{4,20},{20... | collective-permute-start | bytes 2949128 | tf_op jit(solution)/shard_map/ppermute | solution.py:47
  68.3 16.1 %collective-permute-start.11 = (bf16[256,768]{1,0:T(8,128)(2,1)S(1)}, bf16[256,768]{1,0:T(8,128)(2,1)}, u32[]{:S(2)}, u32[]{:S(2)}) collective-permute-start(bf16[256,768]{1,0:T(8,128)(2,1)S(1)} %get-tuple-element.124), channel_id=1, source_target_pairs={{1,0},{2,1},{3,2},{4,3},{5,4},{6,5},{7,6},{8,7},{9,8},{10,9},{11,1... | collective-permute-start | bytes 1179656 | tf_op jit(solution)/shard_map/ppermute | solution.py:1349
  69.7 21.7 %collective-permute-start.12 = (bf16[4,224,768]{2,1,0:T(8,128)(2,1)S(1)}, bf16[4,224,768]{2,1,0:T(8,128)(2,1)S(1)}, u32[]{:S(2)}, u32[]{:S(2)}) collective-permute-start(bf16[4,224,768]{2,1,0:T(8,128)(2,1)S(1)} %pad_maximum_fusion), channel_id=1, source_target_pairs={{0,2},{1,3},{2,0},{3,1},{4,6},{5,7},{6,4},{7,5},{8,10},{9,11},{10,... | collective-permute-start | bytes 4128776 | tf_op jit(solution)/shard_map/ppermute | solution.py:43
  72.5 1.5 copy-start.7
  92.7 41.6 %collective-permute-start.14 = (bf16[8,224,768]{2,1,0:T(8,128)(2,1)}, bf16[8,224,768]{2,1,0:T(8,128)(2,1)S(1)}, u32[]{:S(2)}, u32[]{:S(2)}) collective-permute-start(bf16[8,224,768]{2,1,0:T(8,128)(2,1)} %constant_dynamic-update-slice_fusion.low), channel_id=1, source_target_pairs={{0,16},{16,0},{1,17},{17,1},{2,18},{18,2},{3,19},{19,3},{4,20},{20... | collective-permute-start | bytes 8257544 | tf_op jit(solution)/shard_map/ppermute | solution.py:47
  100.6 33.7 %collective-permute-start.13 = (bf16[8,224,768]{2,1,0:T(8,128)(2,1)}, bf16[8,224,768]{2,1,0:T(8,128)(2,1)S(1)}, u32[]{:S(2)}, u32[]{:S(2)}) collective-permute-start(bf16[8,224,768]{2,1,0:T(8,128)(2,1)} %constant_dynamic-update-slice_fusion.low), channel_id=1, source_target_pairs={{0,1},{1,0},{2,3},{3,2},{4,5},{5,4},{6,7},{7,6},{8,9},{9,8},{10,11... | collective-permute-start | bytes 8257544 | tf_op jit(solution)/shard_map/ppermute | solution.py:43
  134.3 6.6 %copy-start.10 = (bf16[8,224,768]{2,1,0:T(8,128)(2,1)}, bf16[8,224,768]{2,1,0:T(8,128)(2,1)S(1)}, u32[]{:S(2)}) copy-start(bf16[8,224,768]{2,1,0:T(8,128)(2,1)S(1)} %collective-permute-done.13.high) | copy-start | bytes 8257540
  134.3 5.1 %collective-permute-start.15 = (bf16[8,224,768]{2,1,0:T(8,128)(2,1)S(1)}, bf16[8,224,768]{2,1,0:T(8,128)(2,1)S(1)}, u32[]{:S(2)}, u32[]{:S(2)}) collective-permute-start(bf16[8,224,768]{2,1,0:T(8,128)(2,1)S(1)} %collective-permute-done.13.high), channel_id=1, source_target_pairs={{0,16},{16,0},{1,17},{17,1},{2,18},{18,2},{3,19},{19,3},{4,20},{20... | collective-permute-start | bytes 8257544 | tf_op jit(solution)/shard_map/ppermute | solution.py:47
  134.3 6.6 %copy-start.9 = (bf16[8,224,768]{2,1,0:T(8,128)(2,1)}, bf16[8,224,768]{2,1,0:T(8,128)(2,1)S(1)}, u32[]{:S(2)}) copy-start(bf16[8,224,768]{2,1,0:T(8,128)(2,1)S(1)} %collective-permute-done.14.olow) | copy-start | bytes 8257540
  177.5 9.3 %collective-permute-start.16 = (bf16[16,224,768]{2,1,0:T(8,128)(2,1)}, bf16[16,224,768]{2,1,0:T(8,128)(2,1)S(1)}, u32[]{:S(2)}, u32[]{:S(2)}) collective-permute-start(bf16[16,224,768]{2,1,0:T(8,128)(2,1)} %get-tuple-element.148), channel_id=1, source_target_pairs={{0,16},{16,0},{1,17},{17,1},{2,18},{18,2},{3,19},{19,3},{4,20},{20... | collective-permute-start | bytes 16515080 | tf_op jit(solution)/shard_map/ppermute | solution.py:47
  177.7 41.5 %collective-permute-start.18 = (bf16[256,896]{1,0:T(8,128)(2,1)}, bf16[256,896]{1,0:T(8,128)(2,1)S(1)}, u32[]{:S(2)}, u32[]{:S(2)}) collective-permute-start(bf16[256,896]{1,0:T(8,128)(2,1)} %get-tuple-element.156), channel_id=1, source_target_pairs={{0,1},{1,2},{2,3},{3,4},{4,5},{5,6},{6,7},{7,8},{8,9},{9,10},{10,1... | collective-permute-start | bytes 1376264 | tf_op jit(solution)/shard_map/ppermute | solution.py:1404
  181.6 37.6 %collective-permute-start.19 = (bf16[256,896]{1,0:T(8,128)(2,1)}, bf16[256,896]{1,0:T(8,128)(2,1)}, u32[]{:S(2)}, u32[]{:S(2)}) collective-permute-start(bf16[256,896]{1,0:T(8,128)(2,1)} %get-tuple-element.157), channel_id=1, source_target_pairs={{1,0},{2,1},{3,2},{4,3},{5,4},{6,5},{7,6},{8,7},{9,8},{10,9},{11,1... | collective-permute-start | bytes 1376264 | tf_op jit(solution)/shard_map/ppermute | solution.py:1405
  186.9 4.5 %copy-start = (bf16[16,224,768]{2,1,0:T(8,128)(2,1)}, bf16[16,224,768]{2,1,0:T(8,128)(2,1)S(1)}, u32[]{:S(2)}) copy-start(bf16[16,224,768]{2,1,0:T(8,128)(2,1)S(1)} %collective-permute-done.16) | copy-start | bytes 16515076
  191.4 42.5 %collective-permute-start.17 = (bf16[8,224,768]{2,1,0:T(8,128)(2,1)S(1)}, bf16[8,224,768]{2,1,0:T(8,128)(2,1)S(1)}, u32[]{:S(2)}, u32[]{:S(2)}) collective-permute-start(bf16[8,224,768]{2,1,0:T(8,128)(2,1)S(1)} %add_convert_fusion), channel_id=1, source_target_pairs={{0,1},{1,0},{2,3},{3,2},{4,5},{5,4},{6,7},{7,6},{8,9},{9,8},{10,11... | collective-permute-start | bytes 8257544 | tf_op jit(solution)/shard_map/ppermute | solution.py:43
  238.5 18.9 %collective-permute-start.21 = (bf16[4,224,768]{2,1,0:T(8,128)(2,1)}, bf16[4,224,768]{2,1,0:T(8,128)(2,1)S(1)}, u32[]{:S(2)}, u32[]{:S(2)}) collective-permute-start(bf16[4,224,768]{2,1,0:T(8,128)(2,1)} %get-tuple-element.208), channel_id=1, source_target_pairs={{0,2},{1,3},{2,0},{3,1},{4,6},{5,7},{6,4},{7,5},{8,10},{9,11},{10,... | collective-permute-start | bytes 4128776 | tf_op jit(solution)/shard_map/ppermute | solution.py:43
  250.5 3.5 %collective-permute-start.20 = (bf16[8,80,768]{2,1,0:T(8,128)(2,1)}, bf16[8,80,768]{2,1,0:T(8,128)(2,1)S(1)}, u32[]{:S(2)}, u32[]{:S(2)}) collective-permute-start(bf16[8,80,768]{2,1,0:T(8,128)(2,1)} %get-tuple-element.172), channel_id=1, source_target_pairs={{0,16},{16,0},{1,17},{17,1},{2,18},{18,2},{3,19},{19,3},{4,20},{20... | collective-permute-start | bytes 2949128 | tf_op jit(solution)/shard_map/ppermute | solution.py:47
  250.6 25.6 %collective-permute-start.24 = (bf16[8,80,768]{2,1,0:T(8,128)(2,1)}, bf16[8,80,768]{2,1,0:T(8,128)(2,1)}, u32[]{:S(2)}, u32[]{:S(2)}) collective-permute-start(bf16[8,80,768]{2,1,0:T(8,128)(2,1)} %get-tuple-element.179), channel_id=1, source_target_pairs={{0,16},{16,0},{1,17},{17,1},{2,18},{18,2},{3,19},{19,3},{4,20},{20... | collective-permute-start | bytes 2949128 | tf_op jit(solution)/shard_map/ppermute | solution.py:47
  257.4 18.8 %collective-permute-start.23 = (bf16[8,80,768]{2,1,0:T(8,128)(2,1)}, bf16[8,80,768]{2,1,0:T(8,128)(2,1)}, u32[]{:S(2)}, u32[]{:S(2)}) collective-permute-start(bf16[8,80,768]{2,1,0:T(8,128)(2,1)} %add_convert_fusion.2), channel_id=1, source_target_pairs={{0,1},{1,0},{2,3},{3,2},{4,5},{5,4},{6,7},{7,6},{8,9},{9,8},{10,11... | collective-permute-start | bytes 2949128 | tf_op jit(solution)/shard_map/ppermute | solution.py:43
  257.9 18.3 %collective-permute-start.22 = (bf16[2,224,768]{2,1,0:T(8,128)(2,1)S(1)}, bf16[2,224,768]{2,1,0:T(8,128)(2,1)S(1)}, u32[]{:S(2)}, u32[]{:S(2)}) collective-permute-start(bf16[2,224,768]{2,1,0:T(8,128)(2,1)S(1)} %get-tuple-element.211), channel_id=1, source_target_pairs={{0,4},{1,5},{2,6},{3,7},{4,0},{5,1},{6,2},{7,3},{8,12},{9,13},{10,... | collective-permute-start | bytes 2064392 | tf_op jit(solution)/shard_map/ppermute | solution.py:43
  259.6 16.6 %copy-start.3 = (bf16[8,80,768]{2,1,0:T(8,128)(2,1)S(1)}, bf16[8,80,768]{2,1,0:T(8,128)(2,1)}, u32[]{:S(2)}) copy-start(bf16[8,80,768]{2,1,0:T(8,128)(2,1)} %get-tuple-element.178) | copy-start | bytes 2949124
  278.0 13.6 %collective-permute-start.26 = (bf16[4,80,768]{2,1,0:T(8,128)(2,1)S(1)}, bf16[4,80,768]{2,1,0:T(8,128)(2,1)S(1)}, u32[]{:S(2)}, u32[]{:S(2)}) collective-permute-start(bf16[4,80,768]{2,1,0:T(8,128)(2,1)S(1)} %get-tuple-element.212), channel_id=1, source_target_pairs={{0,2},{1,3},{2,0},{3,1},{4,6},{5,7},{6,4},{7,5},{8,10},{9,11},{10,... | collective-permute-start | bytes 1474568 | tf_op jit(solution)/shard_map/ppermute | solution.py:43
  280.2 11.4 %collective-permute-start.25 = (bf16[1,224,768]{2,1,0:T(8,128)(2,1)S(1)}, bf16[1,224,768]{2,1,0:T(8,128)(2,1)S(1)}, u32[]{:S(2)}, u32[]{:S(2)}) collective-permute-start(bf16[1,224,768]{2,1,0:T(8,128)(2,1)S(1)} %fusion.5), channel_id=1, source_target_pairs={{0,8},{1,9},{2,10},{3,11},{4,12},{5,13},{6,14},{7,15},{8,0},{9,1},... | collective-permute-start | bytes 1032200 | tf_op jit(solution)/shard_map/ppermute | solution.py:43
  291.7 18.7 %copy-start.4 = (f32[224,768]{1,0:T(8,128)}, f32[224,768]{1,0:T(8,128)S(1)}, u32[]{:S(2)}) copy-start(f32[224,768]{1,0:T(8,128)S(1)} %fusion.4.mine2) | copy-start | bytes 2064388
  291.7 9.1 %collective-permute-start.28 = (f32[224,768]{1,0:T(8,128)S(1)}, f32[224,768]{1,0:T(8,128)S(1)}, u32[]{:S(2)}, u32[]{:S(2)}) collective-permute-start(f32[224,768]{1,0:T(8,128)S(1)} %fusion.4.mine2), channel_id=1, source_target_pairs={{0,16},{16,0},{1,17},{17,1},{2,18},{18,2},{3,19},{19,3},{4,20},{20... | collective-permute-start | bytes 2064392 | tf_op jit(solution)/shard_map/ppermute | solution.py:47
  291.9 8.9 %collective-permute-start.27 = (bf16[2,80,768]{2,1,0:T(8,128)(2,1)S(1)}, bf16[2,80,768]{2,1,0:T(8,128)(2,1)S(1)}, u32[]{:S(2)}, u32[]{:S(2)}) collective-permute-start(bf16[2,80,768]{2,1,0:T(8,128)(2,1)S(1)} %get-tuple-element.218), channel_id=1, source_target_pairs={{0,4},{1,5},{2,6},{3,7},{4,0},{5,1},{6,2},{7,3},{8,12},{9,13},{10,... | collective-permute-start | bytes 737288 | tf_op jit(solution)/shard_map/ppermute | solution.py:43
  300.8 9.6 %copy-start.14 = (f32[224,768]{1,0:T(8,128)}, f32[224,768]{1,0:T(8,128)S(1)}, u32[]{:S(2)}) copy-start(f32[224,768]{1,0:T(8,128)S(1)} %collective-permute-done.28.other2) | copy-start | bytes 2064388
  300.8 9.6 %copy-start.6 = (f32[1,80,768]{2,1,0:T(8,128)}, f32[1,80,768]{2,1,0:T(8,128)S(1)}, u32[]{:S(2)}) copy-start(f32[1,80,768]{2,1,0:T(8,128)S(1)} %get-tuple-element.221) | copy-start | bytes 737284
  300.8 9.5 %collective-permute-start.30 = (f32[1,80,768]{2,1,0:T(8,128)S(1)}, f32[1,80,768]{2,1,0:T(8,128)S(1)}, u32[]{:S(2)}, u32[]{:S(2)}) collective-permute-start(f32[1,80,768]{2,1,0:T(8,128)S(1)} %get-tuple-element.221), channel_id=1, source_target_pairs={{0,16},{16,0},{1,17},{17,1},{2,18},{18,2},{3,19},{19,3},{4,20},{20... | collective-permute-start | bytes 737288 | tf_op jit(solution)/shard_map/ppermute | solution.py:47
  300.9 4.4 %collective-permute-start.31 = (bf16[1,80,768]{2,1,0:T(8,128)(2,1)S(1)}, bf16[1,80,768]{2,1,0:T(8,128)(2,1)S(1)}, u32[]{:S(2)}, u32[]{:S(2)}) collective-permute-start(bf16[1,80,768]{2,1,0:T(8,128)(2,1)S(1)} %get-tuple-element.220), channel_id=1, source_target_pairs={{0,24},{1,25},{2,26},{3,27},{4,28},{5,29},{6,30},{7,31},{8,16},{9,... | collective-permute-start | bytes 368648 | tf_op jit(solution)/shard_map/ppermute | solution.py:1443
  301.1 9.3 %collective-permute-start.29 = (bf16[1,80,768]{2,1,0:T(8,128)(2,1)S(1)}, bf16[1,80,768]{2,1,0:T(8,128)(2,1)S(1)}, u32[]{:S(2)}, u32[]{:S(2)}) collective-permute-start(bf16[1,80,768]{2,1,0:T(8,128)(2,1)S(1)} %get-tuple-element.220), channel_id=1, source_target_pairs={{0,8},{1,9},{2,10},{3,11},{4,12},{5,13},{6,14},{7,15},{8,0},{9,1},... | collective-permute-start | bytes 368648 | tf_op jit(solution)/shard_map/ppermute | solution.py:43
  305.3 5.1 %copy-start.18 = (bf16[1,80,768]{2,1,0:T(8,128)(2,1)}, bf16[1,80,768]{2,1,0:T(8,128)(2,1)S(1)}, u32[]{:S(2)}) copy-start(bf16[1,80,768]{2,1,0:T(8,128)(2,1)S(1)} %collective-permute-done.31) | copy-start | bytes 368644
  (4 other events, 3.6 us)

commit v2 on v1

--- a/solution.py
+++ b/solution.py
@@ -742,11 +742,11 @@
 
 def middle_kernel(
     ids,
-    pool,
+    pool_in,
     att,
-    exact,
+    exact_in,
     lse,
-    cot,
+    cot_in,
     vec,
     upb,
     low,
@@ -776,9 +776,15 @@
     dw1,
     dw2,
     dwo,
+    pool,
+    exact,
+    cot,
     sems,
+    load_sems,
 ):
     n, width = att.shape
+    loads = [(pool_in, pool), (cot_in, cot), (exact_in, exact)]
+    loads = [pltpu.make_async_copy(a, b, load_sems.at[i]) for i, (a, b) in enumerate(loads)]
     rb = width // NB
     fb = w2.shape[0] // NB
     parts = w1.shape[0]
@@ -796,8 +802,11 @@
             pltpu.make_async_copy(block.at[pl.ds(48 * c, 48)], w1.at[c, rows(s * rb, 48)], sems.at[1]).start()
 
     load_sets(ids, low, high, olow, ohigh, copies_a, copies_b)
+    for x in loads:
+        x.start()
     wait_all(wo, sems.at[0])
     z[...] = dot(att[...], wo[...])
+    loads[0].wait()
     rc = 128
 
     def row_loop(f):
@@ -836,6 +845,7 @@
     lax.fori_loop(0, parts, up, 0)
     z[...] = z[...] + dot(active[parts - 1], w2[pl.ds((parts - 1) * width, width), :])
     gvec[...] = jnp.zeros(gvec.shape, FL)
+    loads[1].wait()
 
     def second_norm(r, i):
         unit, scale = normalize(hid[r, :] + (z[r, :] + vec[5:6]))
@@ -921,6 +931,8 @@
     pick = (head_of == lax.broadcasted_iota(jnp.int32, (16, width), 0)).astype(FL).astype(BF)
     stats[0:8, :] = lse[0:8, :]
     stats[16:24, :] = lse[8:16, :]
+
+    loads[2].wait()
 
     def last(r, i):
         d_low = z[r, :].astype(BF)
@@ -974,8 +986,7 @@
         grid_spec=pltpu.PrefetchScalarGridSpec(
             num_scalar_prefetch=1,
             grid=(1,),
-            in_specs=[full(pool)]
-            + [full(x) for x in (att, exact, lse, cot, vec, upb)]
+            in_specs=[ANY, full(att), ANY, full(lse), ANY, full(vec), full(upb)]
             + [ANY] * 4,
             out_specs=[full(x) for x in shapes] + [ANY, ANY],
             scratch_shapes=[
@@ -992,7 +1003,11 @@
                 pltpu.VMEM((parts, width, width), BF),
                 pltpu.VMEM((ff, width), BF),
                 pltpu.VMEM((width, width), BF),
+                pltpu.VMEM(pool.shape, FL),
+                pltpu.VMEM(exact.shape, FL),
+                pltpu.VMEM(cot.shape, BF),
                 pltpu.SemaphoreType.DMA((4,)),
+                pltpu.SemaphoreType.DMA((3,)),
             ],
         ),
         out_shape=shapes + [big, big],
@@ -1001,15 +1016,48 @@
 
 
 def weights_kernel(
-    ids, pool, tok, dq, dk, dv, gvec, gup, sl, keep_low, keep_up, send_low, send_up, dwq, dwk, dwv, bias, tt, sems
+    ids,
+    pool_in,
+    tok_in,
+    dq_in,
+    dk_in,
+    dv_in,
+    gvec,
+    gup,
+    sl,
+    keep_low,
+    keep_up,
+    send_low,
+    send_up,
+    dwq,
+    dwk,
+    dwv,
+    bias,
+    tt,
+    pool,
+    tok,
+    dq,
+    dk,
+    dv,
+    sems,
+    load_sems,
 ):
+    loads = [(tok_in, tok), (pool_in, pool), (dq_in, dq), (dk_in, dk), (dv_in, dv)]
+    loads = [pltpu.make_async_copy(a, b, load_sems.at[i]) for i, (a, b) in enumerate(loads)]
+    for x in loads:
+        x.start()
     keep = (keep_low, keep_up)
     send = (send_low, send_up)
     width = tok.shape[1]
     ff = gup.shape[1]
     rb = width // NB
+    for x in loads[:3]:
+        x.wait()
     tt[...] = tok[...].T
     dwq[...] = t_dot(pool[...].astype(BF), dq[...]).astype(BF)
+
+    for x in loads[3:]:
+        x.wait()
 
     def columns(c, _):
         cols = pl.ds(pl.multiple_of(c * 256, 256), 256)
@@ -1098,7 +1146,7 @@
         grid_spec=pltpu.PrefetchScalarGridSpec(
             num_scalar_prefetch=1,
             grid=(1,),
-            in_specs=[full(x) for x in (pool, tok, dq, dk, dv, gvec, gup, sl)],
+            in_specs=[ANY] * 5 + [full(x) for x in (gvec, gup, sl)],
             out_specs=[ANY] * 4,
             scratch_shapes=[
                 square,
@@ -1106,7 +1154,11 @@
                 square,
                 pltpu.VMEM((16 * NB, width), BF),
                 pltpu.VMEM((width, tok.shape[0]), BF),
+            ]
+            + [pltpu.VMEM(x.shape, x.dtype) for x in (pool, tok, dq, dk, dv)]
+            + [
                 pltpu.SemaphoreType.DMA((1,)),
+                pltpu.SemaphoreType.DMA((5,)),
             ],
         ),
         out_shape=[big] * 4,
@@ -1229,46 +1281,57 @@
     )(ids, *args)
 
 
-def unpack_kernel(ids, low1, got1, olow1, ogot1, mine2, other2, wq, wk, wv, wo, w1, w2, *vectors):
-    width = wq.shape[1]
+def unpack_kernel(ids, low1, got1, olow1, ogot1, wq, wk, wv, *vectors):
     rb = wq.shape[0]
-    mine1 = low1[...] + got1[...].astype(FL)
-    other1 = olow1[...] + ogot1[...].astype(FL)
-
-    def store(a1, b1, a2, b2):
-        wq[...] = a1[0:48]
-        wk[0:32] = a1[48:80]
-        wk[32:48] = b1[0:16]
-        wv[...] = b1[16:64]
+    mine = low1[...] + got1[...].astype(FL)
+    other = olow1[...] + ogot1[...].astype(FL)
+
+    def store(a, b):
+        wq[...] = a[0:48]
+        wk[0:32] = a[48:80]
+        wk[32:48] = b[0:16]
+        wv[...] = b[16:64]
         for i in range(8):
-            vectors[i][...] = b1[64 + i : 65 + i, 0:rb]
+            vectors[i][...] = b[64 + i : 65 + i, 0:rb]
         for c in range(4):
-            vectors[8][:, rb * c : rb * c + rb] = b1[72 + c : 73 + c, 0:rb]
-            w1[:, width * c : width * c + width] = b2[48 * c : 48 * c + 48]
-        vectors[9][...] = b1[76:77, 0:128]
-        w2[...] = a2[0:192]
-        wo[0:32] = a2[192:224]
-        wo[32:48] = b2[192:208]
+            vectors[8][:, rb * c : rb * c + rb] = b[72 + c : 73 + c, 0:rb]
+        vectors[9][...] = b[76:77, 0 : vectors[9].shape[1]]
 
     @pl.when(ids[1] == 0)
     def _():
-        store(mine1, other1, mine2, other2)
+        store(mine, other)
 
     @pl.when(ids[1] != 0)
     def _():
-        store(other1, mine1, other2, mine2)
-
-
-def unpack_own(ids, args, ff):
-    width = args[0].shape[1]
-    rb = width // NB
-    dims = [(rb, width)] * 4 + [(rb, ff), (ff // NB, width)] + [(1, rb)] * 8 + [(1, ff // NB), (1, 128)]
+        store(other, mine)
+
+
+def unpack_wide_kernel(ids, mine, other, wo, w1, w2):
+    width = wo.shape[1]
+
+    def store(a, b):
+        for c in range(4):
+            w1[:, width * c : width * c + width] = b[48 * c : 48 * c + 48]
+        w2[...] = a[0:192]
+        wo[0:32] = a[192:224]
+        wo[32:48] = b[192:208]
+
+    @pl.when(ids[1] == 0)
+    def _():
+        store(mine, other)
+
+    @pl.when(ids[1] != 0)
+    def _():
+        store(other, mine)
+
+
+def unpack_call(kernel, name, ids, args, dims):
     shapes = [jax.ShapeDtypeStruct(d, FL) for d in dims]
     full = lambda x: pl.BlockSpec(x.shape, lambda i, *_: (0, 0))
     return pl.pallas_call(
-        unpack_kernel,
-        name="unpack",
-        cost_estimate=takes(3),
+        kernel,
+        name=name,
+        cost_estimate=takes(2),
         grid_spec=pltpu.PrefetchScalarGridSpec(
             num_scalar_prefetch=1,
             grid=(1,),
@@ -1441,8 +1504,11 @@
         rest = rest[:1] + three[:1].astype(FL)
         over = [(s, seq + (s ^ 8)) for s in range(seq)] + [(seq + s, s ^ 4) for s in range(seq)]
         first = (rest[0], exchange(part, 8, 4)[0], swap_core(rest)[0], lax.ppermute(part, order, over)[0])
-        gq, gk, gv, go, g1, g2, *small = unpack_own(ids, first + second, ff)
-        g_up, g_slope = small[8][0], small[9][0, : distance_slope.shape[0]]
+        rb = width // NB
+        go, g1, g2 = unpack_call(unpack_wide_kernel, "unpack_wide", ids, second, [(rb, width), (rb, ff), (ff // NB, width)])
+        dims = [(rb, width)] * 3 + [(1, rb)] * 8 + [(1, ff // NB), (1, distance_slope.shape[0])]
+        gq, gk, gv, *small = unpack_call(unpack_kernel, "unpack", ids, first, dims)
+        g_up, g_slope = small[8][0], small[9][0]
         small = [x[0] for x in small[:8]]
     else:
         inv_a = [0] * NB

time: 316 us -> 313 us (level)
  Pallas kernels: 135 us -> 131 us
  transfers between devices with their start and end apart: 32 -> 32, of which waited for: 14 -> 13; matrix products, arithmetic and copies ran while one was open for 3% -> 3% of each run, Pallas kernels for 29% -> 29%
where the time goes in v2:
time: 313 us; the launch traced here: 312 us
  Pallas kernels  131 us (42%)
  waiting for transfers between devices  99.2 us (32%)
  starting transfers between devices  56.6 us (18%)
  other arithmetic  16.7 us (5%)
  local copies, waits for them, and re-layouts  7.73 us (2%)
    ppermute x16, waiting for transfers between devices, exchange(): return lax.ppermute(x, ('dp', 'seq'), pairs)  69.1 us
    pallas_call x1, Pallas kernels, middle(): pl.pallas_call(middle_kernel, name='middle', cost_estimate=takes(36), gri...  35.5 us
    ppermute x16, starting transfers between devices, exchange(): return lax.ppermute(x, ('dp', 'seq'), pairs)  23.7 us
    pallas_call x1, Pallas kernels, attend_own(): pl.pallas_call(own_kernel, name='attend_own', cost_estimate=takes(30), gr...  22.7 us
    pallas_call x1, Pallas kernels, attend_forward(): pl.pallas_call(forward_kernel, name='attend_forward', cost_estimate=takes...  20.9 us
    ppermute x1, waiting for transfers between devices, local(): lax.ppermute(after(tokens[:halo // 2], x1), order, down_pairs)  18.4 us
    ppermute x9, starting transfers between devices, swap_core(): return lax.ppermute(x, 'dp', [(0, 1), (1, 0)])  11.9 us
    ppermute x9, waiting for transfers between devices, swap_core(): return lax.ppermute(x, 'dp', [(0, 1), (1, 0)])  11.7 us
  transfers between devices with their start and end apart: 32, of which 13 were waited for; matrix products, arithmetic and copies ran while one was open for 3% of the time, Pallas kernels for 29%

profile of v2, /device:TPU:0, one launch (start us, length us, event | category | flops | bytes accessed | tf_op | source)
XLA Modules:
  0.0 312.3 jit_solution(2274333201995173191)
XLA Ops:
  1.3 3.2 %pack.1 = bf16[1,304,768]{2,1,0:T(8,128)(2,1)} custom-call(s32[2]{0:T(128)} %pad_add_fusion.ids, f32[48,768]{1,0:T(8,128)} %wq.1, f32[48,768]{1,0:T(8,128)} %wk.1, f32[48,768]{1,0:T(8,128)} %wv.1, f32[48,768]{1,0:T(8,128)} %wo.1, f32[48,3072]{1,0:T(8,128)} %w1.1, f32[192,768]{1,0:T(8,128)} %w2.1, f32[1,192]{1,0:T(1,128)} %bitcast.47, f32[1,48]{1,0:T(1,128)} %bitcast.48, ...), custom_call_target="tpu_custom_call" | custom-call | flops 3449999872 | bytes 10800000 | tf_op jit(solution)/shard_map/pack/pallas_call | solution.py:1268
  5.5 4.1 %collective-permute-start = (bf16[1,80,768]{2,1,0:T(8,128)(2,1)S(1)}, bf16[1,80,768]{2,1,0:T(8,128)(2,1)S(1)}, u32[]{:S(2)}, u32[]{:S(2)}) collective-permute-start(bf16[1,80,768]{2,1,0:T(8,128)(2,1)S(1)} %slice.153), channel_id=1, source_target_pairs={{0,8},{1,9},{2,10},{3,11},{4,12},{5,13},{6,14},{7,15},{8,0},{9,1},... | collective-permute-start | bytes 368648 | tf_op jit(solution)/shard_map/ppermute | solution.py:43
  9.7 4.2 %collective-permute-start.2 = (bf16[256,768]{1,0:T(8,128)(2,1)S(1)}, bf16[256,768]{1,0:T(8,128)(2,1)}, u32[]{:S(2)}, u32[]{:S(2)}) collective-permute-start(bf16[256,768]{1,0:T(8,128)(2,1)S(1)} %get-tuple-element.217), channel_id=1, source_target_pairs={{0,1},{1,2},{2,3},{3,4},{4,5},{5,6},{6,7},{7,8},{8,9},{9,10},{10,1... | collective-permute-start | bytes 1179656 | tf_op jit(solution)/shard_map/ppermute | solution.py:1392
  14.8 7.6 %collective-permute-done.1 = bf16[2,80,768]{2,1,0:T(8,128)(2,1)S(1)} collective-permute-done((bf16[2,80,768]{2,1,0:T(8,128)(2,1)S(1)}, bf16[2,80,768]{2,1,0:T(8,128)(2,1)S(1)}, u32[]{:S(2)}, u32[]{:S(2)}) %collective-permute-start.1) | collective-permute-done | bytes 245792 | tf_op jit(solution)/shard_map/ppermute | solution.py:43
  23.8 7.6 %collective-permute-start.5 = (bf16[256,768]{1,0:T(8,128)(2,1)S(1)}, bf16[256,768]{1,0:T(8,128)(2,1)}, u32[]{:S(2)}, u32[]{:S(2)}) collective-permute-start(bf16[256,768]{1,0:T(8,128)(2,1)S(1)} %get-tuple-element.112), channel_id=1, source_target_pairs={{0,1},{1,2},{2,3},{3,4},{4,5},{5,6},{6,7},{7,8},{8,9},{9,10},{10,1... | collective-permute-start | bytes 1179656 | tf_op jit(solution)/shard_map/ppermute | solution.py:1397
  31.4 1.3 collective-permute-start.4
  33.3 9.9 %collective-permute-done.4 = bf16[1,224,768]{2,1,0:T(8,128)(2,1)S(1)} collective-permute-done((bf16[1,224,768]{2,1,0:T(8,128)(2,1)S(1)}, bf16[1,224,768]{2,1,0:T(8,128)(2,1)S(1)}, u32[]{:S(2)}, u32[]{:S(2)}) %collective-permute-start.4) | collective-permute-done | bytes 344096 | tf_op jit(solution)/shard_map/ppermute | solution.py:43
  43.4 1.3 collective-permute-start.6
  45.6 1.3 collective-permute-start.9
  47.6 18.4 %collective-permute-done.9.high_a = bf16[256,768]{1,0:T(8,128)(2,1)S(1)} collective-permute-done((bf16[256,768]{1,0:T(8,128)(2,1)S(1)}, bf16[256,768]{1,0:T(8,128)(2,1)S(1)}, u32[]{:S(2)}, u32[]{:S(2)}) %collective-permute-start.9) | collective-permute-done | bytes 393248 | tf_op jit(solution)/shard_map/ppermute | solution.py:1406
  66.1 1.6 collective-permute-start.10
  69.8 2.7 collective-permute-start.12
  72.6 1.5 copy-done.7
  74.1 10.4 %qkv.1 = (bf16[512,768]{1,0:T(8,128)(2,1)}, bf16[2048,768]{1,0:T(8,128)(2,1)}, bf16[2048,768]{1,0:T(8,128)(2,1)}, bf16[8,768,256]{2,1,0:T(8,128)(2,1)}, bf16[8,7...) custom-call(s32[2]{0:T(128)} %pad_add_fusion.ids, ...), custom_call_target="tpu_custom_call" | custom-call | flops 10350000128 | bytes 32400000 | tf_op jit(solution)/shard_map/qkv/pallas_call | solution.py:168
  84.5 7.0 %halo_qkv.1 = (bf16[2,256,768]{2,1,0:T(8,128)(2,1)}, bf16[2048,768]{1,0:T(8,128)(2,1)}, bf16[2048,768]{1,0:T(8,128)(2,1)}, bf16[8,768,256]{2,1,0:T(8,128)(2,1)}, bf16[8,768,256]{2,1,0:T(8,128)(2,1)}) custom-call(bf16[256,768]{1,0:T(8,128)(2,1)} %collective-permute-done.2.low_a, ...), custom_call_target="tpu_custom_call", output_to_operand_aliasing={{1}: (8, {}), {2}: (9, {}), {3}: (10, {}), {4}: (11, {})} | custom-call | flops 8049999872 | bytes 25200000 | tf_op jit(solution)/shard_map/halo_qkv/pallas_call | solution.py:217
  92.8 7.9 %collective-permute-start.14 = (bf16[8,224,768]{2,1,0:T(8,128)(2,1)}, bf16[8,224,768]{2,1,0:T(8,128)(2,1)S(1)}, u32[]{:S(2)}, u32[]{:S(2)}) collective-permute-start(bf16[8,224,768]{2,1,0:T(8,128)(2,1)} %constant_dynamic-update-slice_fusion.low), channel_id=1, source_target_pairs={{0,16},{16,0},{1,17},{17,1},{2,18},{18,2},{3,19},{19,3},{4,20},{20... | collective-permute-start | bytes 8257544 | tf_op jit(solution)/shard_map/ppermute | solution.py:47
  100.7 2.4 collective-permute-start.13
  103.1 20.9 %attend_forward.1 = (bf16[512,768]{1,0:T(8,128)(2,1)}, f32[512,768]{1,0:T(8,128)}, f32[16,512]{1,0:T(8,128)}) custom-call(s32[16]{0:T(128)} %pad_add_fusion.1.spans, f32[12]{0:T(128)} %slopes.5, bf16[512,768]{1,0:T(8,128)(2,1)} %get-tuple-element.119.q, bf16[2048,768]{1,0:T(8,128)(2,1)} %get-tuple-element.134.k.ka.kb, ...), custom_call_target="tpu_custom_call" | custom-call | flops 34500001792 | bytes 108000000 | tf_op jit(solution)/shard_map/attend_forward/pallas_call | solution.py:343
  124.0 10.3 %collective-permute-done.13.high = bf16[8,224,768]{2,1,0:T(8,128)(2,1)S(1)} collective-permute-done((bf16[8,224,768]{2,1,0:T(8,128)(2,1)}, bf16[8,224,768]{2,1,0:T(8,128)(2,1)S(1)}, u32[]{:S(2)}, u32[]{:S(2)}) %collective-permute-start.13) | collective-permute-done | bytes 2752544 | tf_op jit(solution)/shard_map/ppermute | solution.py:43
  134.4 5.1 %collective-permute-done.15.ohigh = bf16[8,224,768]{2,1,0:T(8,128)(2,1)S(1)} collective-permute-done((bf16[8,224,768]{2,1,0:T(8,128)(2,1)S(1)}, bf16[8,224,768]{2,1,0:T(8,128)(2,1)S(1)}, u32[]{:S(2)}, u32[]{:S(2)}) %collective-permute-start.15) | collective-permute-done | bytes 2752544 | tf_op jit(solution)/shard_map/ppermute | solution.py:47
  139.5 1.5 copy-done.11
  141.0 35.5 %middle.1 = (bf16[512,768]{1,0:T(8,128)(2,1)}, bf16[512,768]{1,0:T(8,128)(2,1)}, bf16[256,896]{1,0:T(8,128)(2,1)}, bf16[256,896]{1,0:T(8,128)(2,1)}, f32[32,512]...) custom-call(s32[2]{0:T(128)} %pad_add_fusion.ids, ...), custom_call_target="tpu_custom_call" | custom-call | flops 41400000512 | bytes 129600000 | tf_op jit(solution)/shard_map/middle/pallas_call | solution.py:982
  176.7 4.0 %collective-permute-start.18 = (bf16[256,896]{1,0:T(8,128)(2,1)}, bf16[256,896]{1,0:T(8,128)(2,1)S(1)}, u32[]{:S(2)}, u32[]{:S(2)}) collective-permute-start(bf16[256,896]{1,0:T(8,128)(2,1)} %get-tuple-element.156), channel_id=1, source_target_pairs={{0,1},{1,2},{2,3},{3,4},{4,5},{5,6},{6,7},{7,8},{8,9},{9,10},{10,1... | collective-permute-start | bytes 1376264 | tf_op jit(solution)/shard_map/ppermute | solution.py:1467
  180.7 1.5 collective-permute-start.19
  182.2 3.6 %collective-permute-done.16 = bf16[16,224,768]{2,1,0:T(8,128)(2,1)S(1)} collective-permute-done((bf16[16,224,768]{2,1,0:T(8,128)(2,1)}, bf16[16,224,768]{2,1,0:T(8,128)(2,1)S(1)}, u32[]{:S(2)}, u32[]{:S(2)}) %collective-permute-start.16) | collective-permute-done | bytes 5505056 | tf_op jit(solution)/shard_map/ppermute | solution.py:47
  185.8 4.5 %add_convert_fusion = bf16[8,224,768]{2,1,0:T(8,128)(2,1)S(1)} fusion(bf16[16,224,768]{2,1,0:T(8,128)(2,1)S(1)} %collective-permute-done.16, bf16[16,224,768]{2,1,0:T(8,128)(2,1)} %get-tuple-element.147), kind=kLoop, calls=%fused_computation | loop fusion | flops 5505024 | bytes 8257536 | tf_op jit(solution)/shard_map/convert_element_type | solution.py:1471
  190.3 2.1 collective-permute-start.17
  192.4 22.7 %attend_own.1 = (bf16[512,768]{1,0:T(8,128)(2,1)}, f32[1024,768]{1,0:T(8,128)}, f32[1024,768]{1,0:T(8,128)}, f32[48,256]{1,0:T(8,128)}) custom-call(s32[16]{0:T(128)} %pad_add_fusion.1.spans, f32[12]{0:T(128)} %slopes.5, bf16[512,768]{1,0:T(8,128)(2,1)} %get-tuple-element.119.q, bf16[2048,768]{1,0:T(8,128)(2,1)} %get-tuple-element.134.k.ka.kb, ...), custom_call_target="tpu_custom_call" | custom-call | flops 34500001792 | bytes 108000000 | tf_op jit(solution)/shard_map/attend_own/pallas_call | solution.py:554
  216.0 7.8 %attend_halo.1 = (bf16[1024,768]{1,0:T(8,128)(2,1)}, bf16[1024,768]{1,0:T(8,128)(2,1)}) custom-call(s32[16]{0:T(128)} %pad_add_fusion.1.spans, f32[12]{0:T(128)} %slopes.5, bf16[2,256,768]{2,1,0:T(8,128)(2,1)} %get-tuple-element.149.q, bf16[2048,768]{1,0:T(8,128)(2,1)} %get-tuple-element.134.k.ka.kb, bf16[2048,768]{1,0:T(8,128)(2,1)} %get-tuple-element.134.k.ka.kb, ...), custom_call_target="tpu_custom_call" | custom-call | flops 13799999488 | bytes 43200000 | tf_op jit(solution)/shard_map/attend_halo/pallas_call | solution.py:701
  223.8 9.1 %collective-permute-done.17 = bf16[8,224,768]{2,1,0:T(8,128)(2,1)S(1)} collective-permute-done((bf16[8,224,768]{2,1,0:T(8,128)(2,1)S(1)}, bf16[8,224,768]{2,1,0:T(8,128)(2,1)S(1)}, u32[]{:S(2)}, u32[]{:S(2)}) %collective-permute-start.17) | collective-permute-done | bytes 2752544 | tf_op jit(solution)/shard_map/ppermute | solution.py:43
  232.8 4.6 %add_convert_fusion.1 = (bf16[4,224,768]{2,1,0:T(8,128)(2,1)}, f32[4,224,768]{2,1,0:T(8,128)S(1)}) fusion(bf16[16,224,768]{2,1,0:T(8,128)(2,1)} %copy-done, bf16[8,224,768]{2,1,0:T(8,128)(2,1)S(1)} %collective-permute-done.17, bf16[16,224,768]{2,1,0:T(8,128)(2,1)} %get-tuple-element.147), kind=kLoop, calls=%fused_computation.1 | loop fusion | flops 7569408 | bytes 12386304 | tf_op jit(solution)/shard_map/convert_element_type | solution.py:1479
  237.6 9.7 %weight_grads.1 = (bf16[8,80,768]{2,1,0:T(8,128)(2,1)}, bf16[8,80,768]{2,1,0:T(8,128)(2,1)}, bf16[8,80,768]{2,1,0:T(8,128)(2,1)}, bf16[8,80,768]{2,1,0:T(8,128)(2,1)}) custom-call(s32[2]{0:T(128)} %pad_add_fusion.ids, f32[512,768]{1,0:T(8,128)} %get-tuple-element.118.pool_in, bf16[1024,768]{1,0:T(8,128)(2,1)} %tok_in.1, ...), custom_call_target="tpu_custom_call" | custom-call | flops 10350000128 | bytes 32400000 | tf_op jit(solution)/shard_map/weight_grads/pallas_call | solution.py:1142
  247.3 1.4 collective-permute-start.20
  248.7 2.9 collective-permute-done.20
  251.7 2.4 add_convert_fusion.2
  254.1 1.9 collective-permute-done.21
  256.8 1.7 collective-permute-start.22
  258.5 7.7 %token_grads.1 = f32[1024,768]{1,0:T(8,128)} custom-call(f32[512,768]{1,0:T(8,128)} %get-tuple-element.176.mixed, bf16[512,768]{1,0:T(8,128)(2,1)} %get-tuple-element.164.dq_in.dq, bf16[1024,768]{1,0:T(8,128)(2,1)} %get-tuple-element.165.dk_in.dk, bf16[1024,768]{1,0:T(8,128)(2,1)} %get-tuple-element.166.dv_in.dv, bf16[768,768]{1,0:T(8,128)(2,1)} %get-tuple-element.126.wq, ...), custom_call_target="tpu_custom_call" | custom-call | flops 9200000000 | bytes 28800000 | tf_op jit(solution)/shard_map/token_grads/pallas_call | solution.py:1186
  266.2 8.5 %collective-permute-done.22 = bf16[2,224,768]{2,1,0:T(8,128)(2,1)S(1)} collective-permute-done((bf16[2,224,768]{2,1,0:T(8,128)(2,1)S(1)}, bf16[2,224,768]{2,1,0:T(8,128)(2,1)S(1)}, u32[]{:S(2)}, u32[]{:S(2)}) %collective-permute-start.22) | collective-permute-done | bytes 688160 | tf_op jit(solution)/shard_map/ppermute | solution.py:43
  274.8 1.8 add_convert_fusion.3
  276.6 1.9 collective-permute-start.26
  278.6 1.6 collective-permute-start.25
  280.1 10.3 %collective-permute-done.25 = bf16[1,224,768]{2,1,0:T(8,128)(2,1)S(1)} collective-permute-done((bf16[1,224,768]{2,1,0:T(8,128)(2,1)S(1)}, bf16[1,224,768]{2,1,0:T(8,128)(2,1)S(1)}, u32[]{:S(2)}, u32[]{:S(2)}) %collective-permute-start.25) | collective-permute-done | bytes 344096 | tf_op jit(solution)/shard_map/ppermute | solution.py:43
  290.9 8.4 %collective-permute-done.27 = bf16[2,80,768]{2,1,0:T(8,128)(2,1)S(1)} collective-permute-done((bf16[2,80,768]{2,1,0:T(8,128)(2,1)S(1)}, bf16[2,80,768]{2,1,0:T(8,128)(2,1)S(1)}, u32[]{:S(2)}, u32[]{:S(2)}) %collective-permute-start.27) | collective-permute-done | bytes 245792 | tf_op jit(solution)/shard_map/ppermute | solution.py:43
  301.2 1.3 collective-permute-start.29
  302.5 3.1 unpack_wide.1
  305.6 3.0 collective-permute-done.29
  309.4 2.8 unpack.1
  (104 shorter events, 14.9 us)
Async XLA Ops:
  1.3 8.3 %copy-start.1 = (bf16[1024,768]{1,0:T(8,128)(2,1)S(1)}, bf16[1024,768]{1,0:T(8,128)(2,1)}, u32[]{:S(2)}) copy-start(bf16[1024,768]{1,0:T(8,128)(2,1)} %tok_in.1) | copy-start | bytes 4718596
  4.5 19.3 %copy-start.5 = (bf16[1,304,768]{2,1,0:T(8,128)(2,1)S(1)}, bf16[1,304,768]{2,1,0:T(8,128)(2,1)}, u32[]{:S(2)}) copy-start(bf16[1,304,768]{2,1,0:T(8,128)(2,1)} %pack.1) | copy-start | bytes 1400836
  4.5 28.2 %copy-start.8 = (s32[256]{0:T(256)S(1)}, s32[256]{0:T(256)}, u32[]{:S(2)}) copy-start(s32[256]{0:T(256)} %param.21) | copy-start | bytes 3076
  5.5 8.4 %collective-permute-start = (bf16[1,80,768]{2,1,0:T(8,128)(2,1)S(1)}, bf16[1,80,768]{2,1,0:T(8,128)(2,1)S(1)}, u32[]{:S(2)}, u32[]{:S(2)}) collective-permute-start(bf16[1,80,768]{2,1,0:T(8,128)(2,1)S(1)} %slice.153), channel_id=1, source_target_pairs={{0,8},{1,9},{2,10},{3,11},{4,12},{5,13},{6,14},{7,15},{8,0},{9,1},... | collective-permute-start | bytes 368648 | tf_op jit(solution)/shard_map/ppermute | solution.py:43
  9.7 12.8 %collective-permute-start.2 = (bf16[256,768]{1,0:T(8,128)(2,1)S(1)}, bf16[256,768]{1,0:T(8,128)(2,1)}, u32[]{:S(2)}, u32[]{:S(2)}) collective-permute-start(bf16[256,768]{1,0:T(8,128)(2,1)S(1)} %get-tuple-element.217), channel_id=1, source_target_pairs={{0,1},{1,2},{2,3},{3,4},{4,5},{5,6},{6,7},{7,8},{8,9},{9,10},{10,1... | collective-permute-start | bytes 1179656 | tf_op jit(solution)/shard_map/ppermute | solution.py:1392
  13.9 8.6 %collective-permute-start.1 = (bf16[2,80,768]{2,1,0:T(8,128)(2,1)S(1)}, bf16[2,80,768]{2,1,0:T(8,128)(2,1)S(1)}, u32[]{:S(2)}, u32[]{:S(2)}) collective-permute-start(bf16[2,80,768]{2,1,0:T(8,128)(2,1)S(1)} %pad_maximum_fusion.4), channel_id=1, source_target_pairs={{0,4},{1,5},{2,6},{3,7},{4,0},{5,1},{6,2},{7,3},{8,12},{9,13},{10,... | collective-permute-start | bytes 737288 | tf_op jit(solution)/shard_map/ppermute | solution.py:43
  22.5 20.7 %collective-permute-start.3 = (bf16[4,80,768]{2,1,0:T(8,128)(2,1)S(1)}, bf16[4,80,768]{2,1,0:T(8,128)(2,1)S(1)}, u32[]{:S(2)}, u32[]{:S(2)}) collective-permute-start(bf16[4,80,768]{2,1,0:T(8,128)(2,1)S(1)} %pad_maximum_fusion.3), channel_id=1, source_target_pairs={{0,2},{1,3},{2,0},{3,1},{4,6},{5,7},{6,4},{7,5},{8,10},{9,11},{10,... | collective-permute-start | bytes 1474568 | tf_op jit(solution)/shard_map/ppermute | solution.py:43
  23.8 19.4 %collective-permute-start.5 = (bf16[256,768]{1,0:T(8,128)(2,1)S(1)}, bf16[256,768]{1,0:T(8,128)(2,1)}, u32[]{:S(2)}, u32[]{:S(2)}) collective-permute-start(bf16[256,768]{1,0:T(8,128)(2,1)S(1)} %get-tuple-element.112), channel_id=1, source_target_pairs={{0,1},{1,2},{2,3},{3,4},{4,5},{5,6},{6,7},{7,8},{8,9},{9,10},{10,1... | collective-permute-start | bytes 1179656 | tf_op jit(solution)/shard_map/ppermute | solution.py:1397
  31.4 11.8 %collective-permute-start.4 = (bf16[1,224,768]{2,1,0:T(8,128)(2,1)S(1)}, bf16[1,224,768]{2,1,0:T(8,128)(2,1)S(1)}, u32[]{:S(2)}, u32[]{:S(2)}) collective-permute-start(bf16[1,224,768]{2,1,0:T(8,128)(2,1)S(1)} %slice.154), channel_id=1, source_target_pairs={{0,8},{1,9},{2,10},{3,11},{4,12},{5,13},{6,14},{7,15},{8,0},{9,1},... | collective-permute-start | bytes 1032200 | tf_op jit(solution)/shard_map/ppermute | solution.py:43
  43.3 26.5 %copy-start.2 = (bf16[8,80,768]{2,1,0:T(8,128)(2,1)}, bf16[8,80,768]{2,1,0:T(8,128)(2,1)S(1)}, u32[]{:S(2)}) copy-start(bf16[8,80,768]{2,1,0:T(8,128)(2,1)S(1)} %pad_maximum_fusion.1.low) | copy-start | bytes 2949124
  43.4 22.7 %collective-permute-start.7 = (bf16[8,80,768]{2,1,0:T(8,128)(2,1)S(1)}, bf16[8,80,768]{2,1,0:T(8,128)(2,1)S(1)}, u32[]{:S(2)}, u32[]{:S(2)}) collective-permute-start(bf16[8,80,768]{2,1,0:T(8,128)(2,1)S(1)} %pad_maximum_fusion.1.low), channel_id=1, source_target_pairs={{0,16},{16,0},{1,17},{17,1},{2,18},{18,2},{3,19},{19,3},{4,20},{20... | collective-permute-start | bytes 2949128 | tf_op jit(solution)/shard_map/ppermute | solution.py:47
  43.4 22.6 %collective-permute-start.6 = (bf16[8,80,768]{2,1,0:T(8,128)(2,1)S(1)}, bf16[8,80,768]{2,1,0:T(8,128)(2,1)S(1)}, u32[]{:S(2)}, u32[]{:S(2)}) collective-permute-start(bf16[8,80,768]{2,1,0:T(8,128)(2,1)S(1)} %pad_maximum_fusion.1.low), channel_id=1, source_target_pairs={{0,1},{1,0},{2,3},{3,2},{4,5},{5,4},{6,7},{7,6},{8,9},{9,8},{10,11... | collective-permute-start | bytes 2949128 | tf_op jit(solution)/shard_map/ppermute | solution.py:43
  44.8 21.2 %collective-permute-start.8 = (bf16[2,224,768]{2,1,0:T(8,128)(2,1)S(1)}, bf16[2,224,768]{2,1,0:T(8,128)(2,1)S(1)}, u32[]{:S(2)}, u32[]{:S(2)}) collective-permute-start(bf16[2,224,768]{2,1,0:T(8,128)(2,1)S(1)} %pad_maximum_fusion.2), channel_id=1, source_target_pairs={{0,4},{1,5},{2,6},{3,7},{4,0},{5,1},{6,2},{7,3},{8,12},{9,13},{10,... | collective-permute-start | bytes 2064392 | tf_op jit(solution)/shard_map/ppermute | solution.py:43
  45.6 20.4 %collective-permute-start.9 = (bf16[256,768]{1,0:T(8,128)(2,1)S(1)}, bf16[256,768]{1,0:T(8,128)(2,1)S(1)}, u32[]{:S(2)}, u32[]{:S(2)}) collective-permute-start(bf16[256,768]{1,0:T(8,128)(2,1)S(1)} %get-tuple-element.115), channel_id=1, source_target_pairs={{1,0},{2,1},{3,2},{4,3},{5,4},{6,5},{7,6},{8,7},{9,8},{10,9},{11,1... | collective-permute-start | bytes 1179656 | tf_op jit(solution)/shard_map/ppermute | solution.py:1406
  66.0 2.3 copy-start.16
  66.0 6.6 %copy-start.12 = (bf16[8,80,768]{2,1,0:T(8,128)(2,1)}, bf16[8,80,768]{2,1,0:T(8,128)(2,1)S(1)}, u32[]{:S(2)}) copy-start(bf16[8,80,768]{2,1,0:T(8,128)(2,1)S(1)} %collective-permute-done.7.olow) | copy-start | bytes 2949124
  66.1 6.6 %copy-start.13 = (bf16[8,80,768]{2,1,0:T(8,128)(2,1)}, bf16[8,80,768]{2,1,0:T(8,128)(2,1)S(1)}, u32[]{:S(2)}) copy-start(bf16[8,80,768]{2,1,0:T(8,128)(2,1)S(1)} %collective-permute-done.6.high) | copy-start | bytes 2949124
  66.1 8.1 %collective-permute-start.10 = (bf16[8,80,768]{2,1,0:T(8,128)(2,1)S(1)}, bf16[8,80,768]{2,1,0:T(8,128)(2,1)}, u32[]{:S(2)}, u32[]{:S(2)}) collective-permute-start(bf16[8,80,768]{2,1,0:T(8,128)(2,1)S(1)} %collective-permute-done.6.high), channel_id=1, source_target_pairs={{0,16},{16,0},{1,17},{17,1},{2,18},{18,2},{3,19},{19,3},{4,20},{20... | collective-permute-start | bytes 2949128 | tf_op jit(solution)/shard_map/ppermute | solution.py:47
  68.4 16.2 %collective-permute-start.11 = (bf16[256,768]{1,0:T(8,128)(2,1)S(1)}, bf16[256,768]{1,0:T(8,128)(2,1)}, u32[]{:S(2)}, u32[]{:S(2)}) collective-permute-start(bf16[256,768]{1,0:T(8,128)(2,1)S(1)} %get-tuple-element.124), channel_id=1, source_target_pairs={{1,0},{2,1},{3,2},{4,3},{5,4},{6,5},{7,6},{8,7},{9,8},{10,9},{11,1... | collective-permute-start | bytes 1179656 | tf_op jit(solution)/shard_map/ppermute | solution.py:1412
  69.8 21.8 %collective-permute-start.12 = (bf16[4,224,768]{2,1,0:T(8,128)(2,1)S(1)}, bf16[4,224,768]{2,1,0:T(8,128)(2,1)S(1)}, u32[]{:S(2)}, u32[]{:S(2)}) collective-permute-start(bf16[4,224,768]{2,1,0:T(8,128)(2,1)S(1)} %pad_maximum_fusion), channel_id=1, source_target_pairs={{0,2},{1,3},{2,0},{3,1},{4,6},{5,7},{6,4},{7,5},{8,10},{9,11},{10,... | collective-permute-start | bytes 4128776 | tf_op jit(solution)/shard_map/ppermute | solution.py:43
  72.6 1.5 copy-start.7
  92.8 41.6 %collective-permute-start.14 = (bf16[8,224,768]{2,1,0:T(8,128)(2,1)}, bf16[8,224,768]{2,1,0:T(8,128)(2,1)S(1)}, u32[]{:S(2)}, u32[]{:S(2)}) collective-permute-start(bf16[8,224,768]{2,1,0:T(8,128)(2,1)} %constant_dynamic-update-slice_fusion.low), channel_id=1, source_target_pairs={{0,16},{16,0},{1,17},{17,1},{2,18},{18,2},{3,19},{19,3},{4,20},{20... | collective-permute-start | bytes 8257544 | tf_op jit(solution)/shard_map/ppermute | solution.py:47
  100.7 33.7 %collective-permute-start.13 = (bf16[8,224,768]{2,1,0:T(8,128)(2,1)}, bf16[8,224,768]{2,1,0:T(8,128)(2,1)S(1)}, u32[]{:S(2)}, u32[]{:S(2)}) collective-permute-start(bf16[8,224,768]{2,1,0:T(8,128)(2,1)} %constant_dynamic-update-slice_fusion.low), channel_id=1, source_target_pairs={{0,1},{1,0},{2,3},{3,2},{4,5},{5,4},{6,7},{7,6},{8,9},{9,8},{10,11... | collective-permute-start | bytes 8257544 | tf_op jit(solution)/shard_map/ppermute | solution.py:43
  134.4 6.6 %copy-start.10 = (bf16[8,224,768]{2,1,0:T(8,128)(2,1)}, bf16[8,224,768]{2,1,0:T(8,128)(2,1)S(1)}, u32[]{:S(2)}) copy-start(bf16[8,224,768]{2,1,0:T(8,128)(2,1)S(1)} %collective-permute-done.13.high) | copy-start | bytes 8257540
  134.4 5.1 %collective-permute-start.15 = (bf16[8,224,768]{2,1,0:T(8,128)(2,1)S(1)}, bf16[8,224,768]{2,1,0:T(8,128)(2,1)S(1)}, u32[]{:S(2)}, u32[]{:S(2)}) collective-permute-start(bf16[8,224,768]{2,1,0:T(8,128)(2,1)S(1)} %collective-permute-done.13.high), channel_id=1, source_target_pairs={{0,16},{16,0},{1,17},{17,1},{2,18},{18,2},{3,19},{19,3},{4,20},{20... | collective-permute-start | bytes 8257544 | tf_op jit(solution)/shard_map/ppermute | solution.py:47
  134.4 6.6 %copy-start.9 = (bf16[8,224,768]{2,1,0:T(8,128)(2,1)}, bf16[8,224,768]{2,1,0:T(8,128)(2,1)S(1)}, u32[]{:S(2)}) copy-start(bf16[8,224,768]{2,1,0:T(8,128)(2,1)S(1)} %collective-permute-done.14.olow) | copy-start | bytes 8257540
  176.5 9.3 %collective-permute-start.16 = (bf16[16,224,768]{2,1,0:T(8,128)(2,1)}, bf16[16,224,768]{2,1,0:T(8,128)(2,1)S(1)}, u32[]{:S(2)}, u32[]{:S(2)}) collective-permute-start(bf16[16,224,768]{2,1,0:T(8,128)(2,1)} %get-tuple-element.148), channel_id=1, source_target_pairs={{0,16},{16,0},{1,17},{17,1},{2,18},{18,2},{3,19},{19,3},{4,20},{20... | collective-permute-start | bytes 16515080 | tf_op jit(solution)/shard_map/ppermute | solution.py:47
  176.7 38.5 %collective-permute-start.18 = (bf16[256,896]{1,0:T(8,128)(2,1)}, bf16[256,896]{1,0:T(8,128)(2,1)S(1)}, u32[]{:S(2)}, u32[]{:S(2)}) collective-permute-start(bf16[256,896]{1,0:T(8,128)(2,1)} %get-tuple-element.156), channel_id=1, source_target_pairs={{0,1},{1,2},{2,3},{3,4},{4,5},{5,6},{6,7},{7,8},{8,9},{9,10},{10,1... | collective-permute-start | bytes 1376264 | tf_op jit(solution)/shard_map/ppermute | solution.py:1467
  180.7 34.5 %collective-permute-start.19 = (bf16[256,896]{1,0:T(8,128)(2,1)}, bf16[256,896]{1,0:T(8,128)(2,1)}, u32[]{:S(2)}, u32[]{:S(2)}) collective-permute-start(bf16[256,896]{1,0:T(8,128)(2,1)} %get-tuple-element.157), channel_id=1, source_target_pairs={{1,0},{2,1},{3,2},{4,3},{5,4},{6,5},{7,6},{8,7},{9,8},{10,9},{11,1... | collective-permute-start | bytes 1376264 | tf_op jit(solution)/shard_map/ppermute | solution.py:1468
  185.8 4.5 %copy-start = (bf16[16,224,768]{2,1,0:T(8,128)(2,1)}, bf16[16,224,768]{2,1,0:T(8,128)(2,1)S(1)}, u32[]{:S(2)}) copy-start(bf16[16,224,768]{2,1,0:T(8,128)(2,1)S(1)} %collective-permute-done.16) | copy-start | bytes 16515076
  190.3 42.5 %collective-permute-start.17 = (bf16[8,224,768]{2,1,0:T(8,128)(2,1)S(1)}, bf16[8,224,768]{2,1,0:T(8,128)(2,1)S(1)}, u32[]{:S(2)}, u32[]{:S(2)}) collective-permute-start(bf16[8,224,768]{2,1,0:T(8,128)(2,1)S(1)} %add_convert_fusion), channel_id=1, source_target_pairs={{0,1},{1,0},{2,3},{3,2},{4,5},{5,4},{6,7},{7,6},{8,9},{9,8},{10,11... | collective-permute-start | bytes 8257544 | tf_op jit(solution)/shard_map/ppermute | solution.py:43
  237.4 18.5 %collective-permute-start.21 = (bf16[4,224,768]{2,1,0:T(8,128)(2,1)}, bf16[4,224,768]{2,1,0:T(8,128)(2,1)S(1)}, u32[]{:S(2)}, u32[]{:S(2)}) collective-permute-start(bf16[4,224,768]{2,1,0:T(8,128)(2,1)} %get-tuple-element.208), channel_id=1, source_target_pairs={{0,2},{1,3},{2,0},{3,1},{4,6},{5,7},{6,4},{7,5},{8,10},{9,11},{10,... | collective-permute-start | bytes 4128776 | tf_op jit(solution)/shard_map/ppermute | solution.py:43
  247.3 4.4 %collective-permute-start.20 = (bf16[8,80,768]{2,1,0:T(8,128)(2,1)}, bf16[8,80,768]{2,1,0:T(8,128)(2,1)S(1)}, u32[]{:S(2)}, u32[]{:S(2)}) collective-permute-start(bf16[8,80,768]{2,1,0:T(8,128)(2,1)} %get-tuple-element.172), channel_id=1, source_target_pairs={{0,16},{16,0},{1,17},{17,1},{2,18},{18,2},{3,19},{19,3},{4,20},{20... | collective-permute-start | bytes 2949128 | tf_op jit(solution)/shard_map/ppermute | solution.py:47
  248.7 26.1 %collective-permute-start.24 = (bf16[8,80,768]{2,1,0:T(8,128)(2,1)}, bf16[8,80,768]{2,1,0:T(8,128)(2,1)}, u32[]{:S(2)}, u32[]{:S(2)}) collective-permute-start(bf16[8,80,768]{2,1,0:T(8,128)(2,1)} %get-tuple-element.179), channel_id=1, source_target_pairs={{0,16},{16,0},{1,17},{17,1},{2,18},{18,2},{3,19},{19,3},{4,20},{20... | collective-permute-start | bytes 2949128 | tf_op jit(solution)/shard_map/ppermute | solution.py:47
  256.0 18.8 %collective-permute-start.23 = (bf16[8,80,768]{2,1,0:T(8,128)(2,1)}, bf16[8,80,768]{2,1,0:T(8,128)(2,1)}, u32[]{:S(2)}, u32[]{:S(2)}) collective-permute-start(bf16[8,80,768]{2,1,0:T(8,128)(2,1)} %add_convert_fusion.2), channel_id=1, source_target_pairs={{0,1},{1,0},{2,3},{3,2},{4,5},{5,4},{6,7},{7,6},{8,9},{9,8},{10,11... | collective-permute-start | bytes 2949128 | tf_op jit(solution)/shard_map/ppermute | solution.py:43
  256.8 17.9 %collective-permute-start.22 = (bf16[2,224,768]{2,1,0:T(8,128)(2,1)S(1)}, bf16[2,224,768]{2,1,0:T(8,128)(2,1)S(1)}, u32[]{:S(2)}, u32[]{:S(2)}) collective-permute-start(bf16[2,224,768]{2,1,0:T(8,128)(2,1)S(1)} %get-tuple-element.211), channel_id=1, source_target_pairs={{0,4},{1,5},{2,6},{3,7},{4,0},{5,1},{6,2},{7,3},{8,12},{9,13},{10,... | collective-permute-start | bytes 2064392 | tf_op jit(solution)/shard_map/ppermute | solution.py:43
  258.5 16.2 %copy-start.3 = (bf16[8,80,768]{2,1,0:T(8,128)(2,1)S(1)}, bf16[8,80,768]{2,1,0:T(8,128)(2,1)}, u32[]{:S(2)}) copy-start(bf16[8,80,768]{2,1,0:T(8,128)(2,1)} %get-tuple-element.178) | copy-start | bytes 2949124
  276.6 13.9 %collective-permute-start.26 = (bf16[4,80,768]{2,1,0:T(8,128)(2,1)S(1)}, bf16[4,80,768]{2,1,0:T(8,128)(2,1)S(1)}, u32[]{:S(2)}, u32[]{:S(2)}) collective-permute-start(bf16[4,80,768]{2,1,0:T(8,128)(2,1)S(1)} %get-tuple-element.212), channel_id=1, source_target_pairs={{0,2},{1,3},{2,0},{3,1},{4,6},{5,7},{6,4},{7,5},{8,10},{9,11},{10,... | collective-permute-start | bytes 1474568 | tf_op jit(solution)/shard_map/ppermute | solution.py:43
  278.6 11.9 %collective-permute-start.25 = (bf16[1,224,768]{2,1,0:T(8,128)(2,1)S(1)}, bf16[1,224,768]{2,1,0:T(8,128)(2,1)S(1)}, u32[]{:S(2)}, u32[]{:S(2)}) collective-permute-start(bf16[1,224,768]{2,1,0:T(8,128)(2,1)S(1)} %fusion.5), channel_id=1, source_target_pairs={{0,8},{1,9},{2,10},{3,11},{4,12},{5,13},{6,14},{7,15},{8,0},{9,1},... | collective-permute-start | bytes 1032200 | tf_op jit(solution)/shard_map/ppermute | solution.py:43
  290.6 12.0 %copy-start.4 = (f32[224,768]{1,0:T(8,128)}, f32[224,768]{1,0:T(8,128)S(1)}, u32[]{:S(2)}) copy-start(f32[224,768]{1,0:T(8,128)S(1)} %fusion.4.mine) | copy-start | bytes 2064388
  290.6 8.7 %collective-permute-start.28 = (f32[224,768]{1,0:T(8,128)S(1)}, f32[224,768]{1,0:T(8,128)S(1)}, u32[]{:S(2)}, u32[]{:S(2)}) collective-permute-start(f32[224,768]{1,0:T(8,128)S(1)} %fusion.4.mine), channel_id=1, source_target_pairs={{0,16},{16,0},{1,17},{17,1},{2,18},{18,2},{3,19},{19,3},{4,20},{20... | collective-permute-start | bytes 2064392 | tf_op jit(solution)/shard_map/ppermute | solution.py:47
  290.7 8.6 %collective-permute-start.27 = (bf16[2,80,768]{2,1,0:T(8,128)(2,1)S(1)}, bf16[2,80,768]{2,1,0:T(8,128)(2,1)S(1)}, u32[]{:S(2)}, u32[]{:S(2)}) collective-permute-start(bf16[2,80,768]{2,1,0:T(8,128)(2,1)S(1)} %get-tuple-element.218), channel_id=1, source_target_pairs={{0,4},{1,5},{2,6},{3,7},{4,0},{5,1},{6,2},{7,3},{8,12},{9,13},{10,... | collective-permute-start | bytes 737288 | tf_op jit(solution)/shard_map/ppermute | solution.py:43
  299.3 3.2 %copy-start.14 = (f32[224,768]{1,0:T(8,128)}, f32[224,768]{1,0:T(8,128)S(1)}, u32[]{:S(2)}) copy-start(f32[224,768]{1,0:T(8,128)S(1)} %collective-permute-done.28.other) | copy-start | bytes 2064388
  299.4 6.3 %copy-start.6 = (f32[1,80,768]{2,1,0:T(8,128)}, f32[1,80,768]{2,1,0:T(8,128)S(1)}, u32[]{:S(2)}) copy-start(f32[1,80,768]{2,1,0:T(8,128)S(1)} %get-tuple-element.221) | copy-start | bytes 737284
  299.4 9.3 %collective-permute-start.30 = (f32[1,80,768]{2,1,0:T(8,128)S(1)}, f32[1,80,768]{2,1,0:T(8,128)S(1)}, u32[]{:S(2)}, u32[]{:S(2)}) collective-permute-start(f32[1,80,768]{2,1,0:T(8,128)S(1)} %get-tuple-element.221), channel_id=1, source_target_pairs={{0,16},{16,0},{1,17},{17,1},{2,18},{18,2},{3,19},{19,3},{4,20},{20... | collective-permute-start | bytes 737288 | tf_op jit(solution)/shard_map/ppermute | solution.py:47
  299.9 5.7 %collective-permute-start.31 = (bf16[1,80,768]{2,1,0:T(8,128)(2,1)S(1)}, bf16[1,80,768]{2,1,0:T(8,128)(2,1)S(1)}, u32[]{:S(2)}, u32[]{:S(2)}) collective-permute-start(bf16[1,80,768]{2,1,0:T(8,128)(2,1)S(1)} %get-tuple-element.220), channel_id=1, source_target_pairs={{0,24},{1,25},{2,26},{3,27},{4,28},{5,29},{6,30},{7,31},{8,16},{9,... | collective-permute-start | bytes 368648 | tf_op jit(solution)/shard_map/ppermute | solution.py:1506
  301.2 7.5 %collective-permute-start.29 = (bf16[1,80,768]{2,1,0:T(8,128)(2,1)S(1)}, bf16[1,80,768]{2,1,0:T(8,128)(2,1)S(1)}, u32[]{:S(2)}, u32[]{:S(2)}) collective-permute-start(bf16[1,80,768]{2,1,0:T(8,128)(2,1)S(1)} %get-tuple-element.220), channel_id=1, source_target_pairs={{0,8},{1,9},{2,10},{3,11},{4,12},{5,13},{6,14},{7,15},{8,0},{9,1},... | collective-permute-start | bytes 368648 | tf_op jit(solution)/shard_map/ppermute | solution.py:43
  305.6 3.0 copy-start.18
  (4 other events, 3.7 us)

commit v3 on v2

--- a/solution.py
+++ b/solution.py
@@ -457,13 +457,16 @@
     dk[...] = jnp.zeros(dk.shape, FL)
     dv[...] = jnp.zeros(dv.shape, FL)
     sl[...] = jnp.zeros(sl.shape, FL)
-    qt[...] = jnp.zeros(qt.shape, BF)
-    dat[...] = jnp.zeros(dat.shape, BF)
+    @pl.when(pl.program_id(0) == 0)
+    def _():
+        qt[...] = jnp.zeros(qt.shape, BF)
+        dat[...] = jnp.zeros(dat.shape, BF)
+        base[0] = key_lines(1.0, 13)
+        base[1] = key_lines(-1.0, 14)
+
     line = lax.broadcasted_iota(jnp.int32, (16, KC), 0)
     spot = lax.broadcasted_iota(jnp.int32, (16, KC), 1).astype(FL)
     extra = jnp.where(line == 0, 1.0, jnp.where(line == 1, spot, 0.0)).astype(BF)
-    base[0] = key_lines(1.0, 13)
-    base[1] = key_lines(-1.0, 14)
     own_lines = key_lines(1.0, 0).astype(BF)
     ones = value_lines()
 
@@ -631,8 +634,12 @@
     for into, parts in ((k, (ka, kb)), (v, (va, vb))):
         into[0:edge] = parts[0][...]
         into[edge:] = parts[1][...]
-    qt[...] = jnp.zeros(qt.shape, BF)
-    dat[...] = jnp.zeros(dat.shape, BF)
+
+    @pl.when(pl.program_id(0) == 0)
+    def _():
+        qt[...] = jnp.zeros(qt.shape, BF)
+        dat[...] = jnp.zeros(dat.shape, BF)
+
     ones = value_lines()
     for side, pay in enumerate((low_stats, high_stats)):
         x = pay[...].astype(FL)

time: 313 us -> 314 us (level)
  waiting for transfers between devices: 99.2 us -> 89.7 us
  Pallas kernels: 131 us -> 140 us
    ppermute x16, waiting for transfers between devices: 69.1 us -> 59.6 us  [exchange(): return lax.ppermute(x, ('dp', 'seq'), pairs)]
    pallas_call x1, Pallas kernels: 22.7 us -> 27 us  [attend_own(): pl.pallas_call(own_kernel, name='attend_own', cost_estimate=takes(30), gr...]
    pallas_call x1, Pallas kernels: 20.9 us -> 25 us  [attend_forward(): pl.pallas_call(forward_kernel, name='attend_forward', cost_estimate=takes...]
  transfers between devices with their start and end apart: 32 -> 32, of which waited for: 13 -> 13; matrix products, arithmetic and copies ran while one was open for 3% -> 3% of each run, Pallas kernels for 29% -> 32%
where the time goes in v3:
time: 314 us; the launch traced here: 313 us
  Pallas kernels  140 us (45%)
  waiting for transfers between devices  89.7 us (29%)
  starting transfers between devices  57.5 us (18%)
  other arithmetic  16.7 us (5%)
  local copies, waits for them, and re-layouts  7.73 us (2%)
    ppermute x16, waiting for transfers between devices, exchange(): return lax.ppermute(x, ('dp', 'seq'), pairs)  59.6 us
    pallas_call x1, Pallas kernels, middle(): pl.pallas_call(middle_kernel, name='middle', cost_estimate=takes(36), gri...  35.5 us
    pallas_call x1, Pallas kernels, attend_own(): pl.pallas_call(own_kernel, name='attend_own', cost_estimate=takes(30), gr...  27 us
    ppermute x16, starting transfers between devices, exchange(): return lax.ppermute(x, ('dp', 'seq'), pairs)  25.4 us
    pallas_call x1, Pallas kernels, attend_forward(): pl.pallas_call(forward_kernel, name='attend_forward', cost_estimate=takes...  25 us
    ppermute x1, waiting for transfers between devices, local(): lax.ppermute(after(tokens[:halo // 2], x1), order, down_pairs)  18.4 us
    ppermute x9, starting transfers between devices, swap_core(): return lax.ppermute(x, 'dp', [(0, 1), (1, 0)])  11.7 us
    ppermute x9, waiting for transfers between devices, swap_core(): return lax.ppermute(x, 'dp', [(0, 1), (1, 0)])  11.7 us
  transfers between devices with their start and end apart: 32, of which 13 were waited for; matrix products, arithmetic and copies ran while one was open for 3% of the time, Pallas kernels for 32%

profile of v3, /device:TPU:0, one launch (start us, length us, event | category | flops | bytes accessed | tf_op | source)
XLA Modules:
  0.0 313.2 jit_solution(2198740132673459437)
XLA Ops:
  1.3 3.2 %pack.1 = bf16[1,304,768]{2,1,0:T(8,128)(2,1)} custom-call(s32[2]{0:T(128)} %pad_add_fusion.ids, f32[48,768]{1,0:T(8,128)} %wq.1, f32[48,768]{1,0:T(8,128)} %wk.1, f32[48,768]{1,0:T(8,128)} %wv.1, f32[48,768]{1,0:T(8,128)} %wo.1, f32[48,3072]{1,0:T(8,128)} %w1.1, f32[192,768]{1,0:T(8,128)} %w2.1, f32[1,192]{1,0:T(1,128)} %bitcast.47, f32[1,48]{1,0:T(1,128)} %bitcast.48, ...), custom_call_target="tpu_custom_call" | custom-call | flops 3449999872 | bytes 10800000 | tf_op jit(solution)/shard_map/pack/pallas_call | solution.py:1275
  5.5 4.1 %collective-permute-start = (bf16[1,80,768]{2,1,0:T(8,128)(2,1)S(1)}, bf16[1,80,768]{2,1,0:T(8,128)(2,1)S(1)}, u32[]{:S(2)}, u32[]{:S(2)}) collective-permute-start(bf16[1,80,768]{2,1,0:T(8,128)(2,1)S(1)} %slice.153), channel_id=1, source_target_pairs={{0,8},{1,9},{2,10},{3,11},{4,12},{5,13},{6,14},{7,15},{8,0},{9,1},... | collective-permute-start | bytes 368648 | tf_op jit(solution)/shard_map/ppermute | solution.py:43
  9.7 4.2 %collective-permute-start.2 = (bf16[256,768]{1,0:T(8,128)(2,1)S(1)}, bf16[256,768]{1,0:T(8,128)(2,1)}, u32[]{:S(2)}, u32[]{:S(2)}) collective-permute-start(bf16[256,768]{1,0:T(8,128)(2,1)S(1)} %get-tuple-element.217), channel_id=1, source_target_pairs={{0,1},{1,2},{2,3},{3,4},{4,5},{5,6},{6,7},{7,8},{8,9},{9,10},{10,1... | collective-permute-start | bytes 1179656 | tf_op jit(solution)/shard_map/ppermute | solution.py:1399
  14.8 7.6 %collective-permute-done.1 = bf16[2,80,768]{2,1,0:T(8,128)(2,1)S(1)} collective-permute-done((bf16[2,80,768]{2,1,0:T(8,128)(2,1)S(1)}, bf16[2,80,768]{2,1,0:T(8,128)(2,1)S(1)}, u32[]{:S(2)}, u32[]{:S(2)}) %collective-permute-start.1) | collective-permute-done | bytes 245792 | tf_op jit(solution)/shard_map/ppermute | solution.py:43
  23.8 7.6 %collective-permute-start.5 = (bf16[256,768]{1,0:T(8,128)(2,1)S(1)}, bf16[256,768]{1,0:T(8,128)(2,1)}, u32[]{:S(2)}, u32[]{:S(2)}) collective-permute-start(bf16[256,768]{1,0:T(8,128)(2,1)S(1)} %get-tuple-element.112), channel_id=1, source_target_pairs={{0,1},{1,2},{2,3},{3,4},{4,5},{5,6},{6,7},{7,8},{8,9},{9,10},{10,1... | collective-permute-start | bytes 1179656 | tf_op jit(solution)/shard_map/ppermute | solution.py:1404
  31.4 1.3 collective-permute-start.4
  33.3 9.9 %collective-permute-done.4 = bf16[1,224,768]{2,1,0:T(8,128)(2,1)S(1)} collective-permute-done((bf16[1,224,768]{2,1,0:T(8,128)(2,1)S(1)}, bf16[1,224,768]{2,1,0:T(8,128)(2,1)S(1)}, u32[]{:S(2)}, u32[]{:S(2)}) %collective-permute-start.4) | collective-permute-done | bytes 344096 | tf_op jit(solution)/shard_map/ppermute | solution.py:43
  43.4 1.3 collective-permute-start.6
  45.6 1.3 collective-permute-start.9
  47.6 18.4 %collective-permute-done.9.high_a = bf16[256,768]{1,0:T(8,128)(2,1)S(1)} collective-permute-done((bf16[256,768]{1,0:T(8,128)(2,1)S(1)}, bf16[256,768]{1,0:T(8,128)(2,1)S(1)}, u32[]{:S(2)}, u32[]{:S(2)}) %collective-permute-start.9) | collective-permute-done | bytes 393248 | tf_op jit(solution)/shard_map/ppermute | solution.py:1413
  66.1 1.6 collective-permute-start.10
  68.4 1.3 collective-permute-start.11
  69.8 2.7 collective-permute-start.12
  72.6 1.5 copy-done.7
  74.1 10.4 %qkv.1 = (bf16[512,768]{1,0:T(8,128)(2,1)}, bf16[2048,768]{1,0:T(8,128)(2,1)}, bf16[2048,768]{1,0:T(8,128)(2,1)}, bf16[8,768,256]{2,1,0:T(8,128)(2,1)}, bf16[8,7...) custom-call(s32[2]{0:T(128)} %pad_add_fusion.ids, ...), custom_call_target="tpu_custom_call" | custom-call | flops 10350000128 | bytes 32400000 | tf_op jit(solution)/shard_map/qkv/pallas_call | solution.py:168
  84.5 7.0 %halo_qkv.1 = (bf16[2,256,768]{2,1,0:T(8,128)(2,1)}, bf16[2048,768]{1,0:T(8,128)(2,1)}, bf16[2048,768]{1,0:T(8,128)(2,1)}, bf16[8,768,256]{2,1,0:T(8,128)(2,1)}, bf16[8,768,256]{2,1,0:T(8,128)(2,1)}) custom-call(bf16[256,768]{1,0:T(8,128)(2,1)} %collective-permute-done.2.low_a, ...), custom_call_target="tpu_custom_call", output_to_operand_aliasing={{1}: (8, {}), {2}: (9, {}), {3}: (10, {}), {4}: (11, {})} | custom-call | flops 8049999872 | bytes 25200000 | tf_op jit(solution)/shard_map/halo_qkv/pallas_call | solution.py:217
  92.8 7.9 %collective-permute-start.14 = (bf16[8,224,768]{2,1,0:T(8,128)(2,1)}, bf16[8,224,768]{2,1,0:T(8,128)(2,1)S(1)}, u32[]{:S(2)}, u32[]{:S(2)}) collective-permute-start(bf16[8,224,768]{2,1,0:T(8,128)(2,1)} %constant_dynamic-update-slice_fusion.low), channel_id=1, source_target_pairs={{0,16},{16,0},{1,17},{17,1},{2,18},{18,2},{3,19},{19,3},{4,20},{20... | collective-permute-start | bytes 8257544 | tf_op jit(solution)/shard_map/ppermute | solution.py:47
  100.7 2.4 collective-permute-start.13
  103.1 25.0 %attend_forward.1 = (bf16[512,768]{1,0:T(8,128)(2,1)}, f32[512,768]{1,0:T(8,128)}, f32[16,512]{1,0:T(8,128)}) custom-call(s32[16]{0:T(128)} %pad_add_fusion.1.spans, f32[12]{0:T(128)} %slopes.5, bf16[512,768]{1,0:T(8,128)(2,1)} %get-tuple-element.119.q, bf16[2048,768]{1,0:T(8,128)(2,1)} %get-tuple-element.134.k.ka.kb, ...), custom_call_target="tpu_custom_call" | custom-call | flops 34500001792 | bytes 108000000 | tf_op jit(solution)/shard_map/attend_forward/pallas_call | solution.py:343
  128.1 6.2 %collective-permute-done.13.high = bf16[8,224,768]{2,1,0:T(8,128)(2,1)S(1)} collective-permute-done((bf16[8,224,768]{2,1,0:T(8,128)(2,1)}, bf16[8,224,768]{2,1,0:T(8,128)(2,1)S(1)}, u32[]{:S(2)}, u32[]{:S(2)}) %collective-permute-start.13) | collective-permute-done | bytes 2752544 | tf_op jit(solution)/shard_map/ppermute | solution.py:43
  134.4 5.1 %collective-permute-done.15.ohigh = bf16[8,224,768]{2,1,0:T(8,128)(2,1)S(1)} collective-permute-done((bf16[8,224,768]{2,1,0:T(8,128)(2,1)S(1)}, bf16[8,224,768]{2,1,0:T(8,128)(2,1)S(1)}, u32[]{:S(2)}, u32[]{:S(2)}) %collective-permute-start.15) | collective-permute-done | bytes 2752544 | tf_op jit(solution)/shard_map/ppermute | solution.py:47
  139.5 1.5 copy-done.11
  141.0 35.5 %middle.1 = (bf16[512,768]{1,0:T(8,128)(2,1)}, bf16[512,768]{1,0:T(8,128)(2,1)}, bf16[256,896]{1,0:T(8,128)(2,1)}, bf16[256,896]{1,0:T(8,128)(2,1)}, f32[32,512]...) custom-call(s32[2]{0:T(128)} %pad_add_fusion.ids, ...), custom_call_target="tpu_custom_call" | custom-call | flops 41400000512 | bytes 129600000 | tf_op jit(solution)/shard_map/middle/pallas_call | solution.py:989
  176.7 4.0 %collective-permute-start.18 = (bf16[256,896]{1,0:T(8,128)(2,1)}, bf16[256,896]{1,0:T(8,128)(2,1)S(1)}, u32[]{:S(2)}, u32[]{:S(2)}) collective-permute-start(bf16[256,896]{1,0:T(8,128)(2,1)} %get-tuple-element.156), channel_id=1, source_target_pairs={{0,1},{1,2},{2,3},{3,4},{4,5},{5,6},{6,7},{7,8},{8,9},{9,10},{10,1... | collective-permute-start | bytes 1376264 | tf_op jit(solution)/shard_map/ppermute | solution.py:1474
  180.7 1.5 collective-permute-start.19
  182.2 3.6 %collective-permute-done.16 = bf16[16,224,768]{2,1,0:T(8,128)(2,1)S(1)} collective-permute-done((bf16[16,224,768]{2,1,0:T(8,128)(2,1)}, bf16[16,224,768]{2,1,0:T(8,128)(2,1)S(1)}, u32[]{:S(2)}, u32[]{:S(2)}) %collective-permute-start.16) | collective-permute-done | bytes 5505056 | tf_op jit(solution)/shard_map/ppermute | solution.py:47
  185.8 4.5 %add_convert_fusion = bf16[8,224,768]{2,1,0:T(8,128)(2,1)S(1)} fusion(bf16[16,224,768]{2,1,0:T(8,128)(2,1)S(1)} %collective-permute-done.16, bf16[16,224,768]{2,1,0:T(8,128)(2,1)} %get-tuple-element.147), kind=kLoop, calls=%fused_computation | loop fusion | flops 5505024 | bytes 8257536 | tf_op jit(solution)/shard_map/convert_element_type | solution.py:1478
  190.3 2.1 collective-permute-start.17
  192.4 27.0 %attend_own.1 = (bf16[512,768]{1,0:T(8,128)(2,1)}, f32[1024,768]{1,0:T(8,128)}, f32[1024,768]{1,0:T(8,128)}, f32[48,256]{1,0:T(8,128)}) custom-call(s32[16]{0:T(128)} %pad_add_fusion.1.spans, f32[12]{0:T(128)} %slopes.5, bf16[512,768]{1,0:T(8,128)(2,1)} %get-tuple-element.119.q, bf16[2048,768]{1,0:T(8,128)(2,1)} %get-tuple-element.134.k.ka.kb, ...), custom_call_target="tpu_custom_call" | custom-call | flops 34500001792 | bytes 108000000 | tf_op jit(solution)/shard_map/attend_own/pallas_call | solution.py:557
  220.2 9.1 %attend_halo.1 = (bf16[1024,768]{1,0:T(8,128)(2,1)}, bf16[1024,768]{1,0:T(8,128)(2,1)}) custom-call(s32[16]{0:T(128)} %pad_add_fusion.1.spans, f32[12]{0:T(128)} %slopes.5, bf16[2,256,768]{2,1,0:T(8,128)(2,1)} %get-tuple-element.149.q, bf16[2048,768]{1,0:T(8,128)(2,1)} %get-tuple-element.134.k.ka.kb, bf16[2048,768]{1,0:T(8,128)(2,1)} %get-tuple-element.134.k.ka.kb, ...), custom_call_target="tpu_custom_call" | custom-call | flops 13799999488 | bytes 43200000 | tf_op jit(solution)/shard_map/attend_halo/pallas_call | solution.py:708
  229.3 3.6 %collective-permute-done.17 = bf16[8,224,768]{2,1,0:T(8,128)(2,1)S(1)} collective-permute-done((bf16[8,224,768]{2,1,0:T(8,128)(2,1)S(1)}, bf16[8,224,768]{2,1,0:T(8,128)(2,1)S(1)}, u32[]{:S(2)}, u32[]{:S(2)}) %collective-permute-start.17) | collective-permute-done | bytes 2752544 | tf_op jit(solution)/shard_map/ppermute | solution.py:43
  232.8 4.6 %add_convert_fusion.1 = (bf16[4,224,768]{2,1,0:T(8,128)(2,1)}, f32[4,224,768]{2,1,0:T(8,128)S(1)}) fusion(bf16[16,224,768]{2,1,0:T(8,128)(2,1)} %copy-done, bf16[8,224,768]{2,1,0:T(8,128)(2,1)S(1)} %collective-permute-done.17, bf16[16,224,768]{2,1,0:T(8,128)(2,1)} %get-tuple-element.147), kind=kLoop, calls=%fused_computation.1 | loop fusion | flops 7569408 | bytes 12386304 | tf_op jit(solution)/shard_map/convert_element_type | solution.py:1486
  237.6 9.7 %weight_grads.1 = (bf16[8,80,768]{2,1,0:T(8,128)(2,1)}, bf16[8,80,768]{2,1,0:T(8,128)(2,1)}, bf16[8,80,768]{2,1,0:T(8,128)(2,1)}, bf16[8,80,768]{2,1,0:T(8,128)(2,1)}) custom-call(s32[2]{0:T(128)} %pad_add_fusion.ids, f32[512,768]{1,0:T(8,128)} %get-tuple-element.118.pool_in, bf16[1024,768]{1,0:T(8,128)(2,1)} %tok_in.1, ...), custom_call_target="tpu_custom_call" | custom-call | flops 10350000128 | bytes 32400000 | tf_op jit(solution)/shard_map/weight_grads/pallas_call | solution.py:1149
  247.3 1.4 collective-permute-start.20
  248.7 2.9 collective-permute-done.20
  251.7 2.4 add_convert_fusion.2
  254.1 1.9 collective-permute-done.21
  256.8 1.7 collective-permute-start.22
  258.5 7.7 %token_grads.1 = f32[1024,768]{1,0:T(8,128)} custom-call(f32[512,768]{1,0:T(8,128)} %get-tuple-element.176.mixed, bf16[512,768]{1,0:T(8,128)(2,1)} %get-tuple-element.164.dq_in.dq, bf16[1024,768]{1,0:T(8,128)(2,1)} %get-tuple-element.165.dk_in.dk, bf16[1024,768]{1,0:T(8,128)(2,1)} %get-tuple-element.166.dv_in.dv, bf16[768,768]{1,0:T(8,128)(2,1)} %get-tuple-element.126.wq, ...), custom_call_target="tpu_custom_call" | custom-call | flops 9200000000 | bytes 28800000 | tf_op jit(solution)/shard_map/token_grads/pallas_call | solution.py:1193
  266.2 7.6 %collective-permute-done.22 = bf16[2,224,768]{2,1,0:T(8,128)(2,1)S(1)} collective-permute-done((bf16[2,224,768]{2,1,0:T(8,128)(2,1)S(1)}, bf16[2,224,768]{2,1,0:T(8,128)(2,1)S(1)}, u32[]{:S(2)}, u32[]{:S(2)}) %collective-permute-start.22) | collective-permute-done | bytes 688160 | tf_op jit(solution)/shard_map/ppermute | solution.py:43
  273.8 1.8 add_convert_fusion.3
  275.7 3.3 %collective-permute-start.26 = (bf16[4,80,768]{2,1,0:T(8,128)(2,1)S(1)}, bf16[4,80,768]{2,1,0:T(8,128)(2,1)S(1)}, u32[]{:S(2)}, u32[]{:S(2)}) collective-permute-start(bf16[4,80,768]{2,1,0:T(8,128)(2,1)S(1)} %get-tuple-element.212), channel_id=1, source_target_pairs={{0,2},{1,3},{2,0},{3,1},{4,6},{5,7},{6,4},{7,5},{8,10},{9,11},{10,... | collective-permute-start | bytes 1474568 | tf_op jit(solution)/shard_map/ppermute | solution.py:43
  280.2 10.8 %collective-permute-done.25 = bf16[1,224,768]{2,1,0:T(8,128)(2,1)S(1)} collective-permute-done((bf16[1,224,768]{2,1,0:T(8,128)(2,1)S(1)}, bf16[1,224,768]{2,1,0:T(8,128)(2,1)S(1)}, u32[]{:S(2)}, u32[]{:S(2)}) %collective-permute-start.25) | collective-permute-done | bytes 344096 | tf_op jit(solution)/shard_map/ppermute | solution.py:43
  291.3 8.4 %collective-permute-done.27 = bf16[2,80,768]{2,1,0:T(8,128)(2,1)S(1)} collective-permute-done((bf16[2,80,768]{2,1,0:T(8,128)(2,1)S(1)}, bf16[2,80,768]{2,1,0:T(8,128)(2,1)S(1)}, u32[]{:S(2)}, u32[]{:S(2)}) %collective-permute-start.27) | collective-permute-done | bytes 245792 | tf_op jit(solution)/shard_map/ppermute | solution.py:43
  300.7 2.2 collective-permute-start.29
  302.9 3.1 unpack_wide.1
  306.0 3.5 %collective-permute-done.29 = bf16[1,80,768]{2,1,0:T(8,128)(2,1)S(1)} collective-permute-done((bf16[1,80,768]{2,1,0:T(8,128)(2,1)S(1)}, bf16[1,80,768]{2,1,0:T(8,128)(2,1)S(1)}, u32[]{:S(2)}, u32[]{:S(2)}) %collective-permute-start.29) | collective-permute-done | bytes 122912 | tf_op jit(solution)/shard_map/ppermute | solution.py:43
  310.3 2.8 unpack.1
  (104 shorter events, 13.8 us)
Async XLA Ops:
  1.3 8.3 %copy-start.1 = (bf16[1024,768]{1,0:T(8,128)(2,1)S(1)}, bf16[1024,768]{1,0:T(8,128)(2,1)}, u32[]{:S(2)}) copy-start(bf16[1024,768]{1,0:T(8,128)(2,1)} %tok_in.1) | copy-start | bytes 4718596
  4.5 19.3 %copy-start.5 = (bf16[1,304,768]{2,1,0:T(8,128)(2,1)S(1)}, bf16[1,304,768]{2,1,0:T(8,128)(2,1)}, u32[]{:S(2)}) copy-start(bf16[1,304,768]{2,1,0:T(8,128)(2,1)} %pack.1) | copy-start | bytes 1400836
  4.5 28.2 %copy-start.8 = (s32[256]{0:T(256)S(1)}, s32[256]{0:T(256)}, u32[]{:S(2)}) copy-start(s32[256]{0:T(256)} %param.21) | copy-start | bytes 3076
  5.5 8.4 %collective-permute-start = (bf16[1,80,768]{2,1,0:T(8,128)(2,1)S(1)}, bf16[1,80,768]{2,1,0:T(8,128)(2,1)S(1)}, u32[]{:S(2)}, u32[]{:S(2)}) collective-permute-start(bf16[1,80,768]{2,1,0:T(8,128)(2,1)S(1)} %slice.153), channel_id=1, source_target_pairs={{0,8},{1,9},{2,10},{3,11},{4,12},{5,13},{6,14},{7,15},{8,0},{9,1},... | collective-permute-start | bytes 368648 | tf_op jit(solution)/shard_map/ppermute | solution.py:43
  9.7 12.8 %collective-permute-start.2 = (bf16[256,768]{1,0:T(8,128)(2,1)S(1)}, bf16[256,768]{1,0:T(8,128)(2,1)}, u32[]{:S(2)}, u32[]{:S(2)}) collective-permute-start(bf16[256,768]{1,0:T(8,128)(2,1)S(1)} %get-tuple-element.217), channel_id=1, source_target_pairs={{0,1},{1,2},{2,3},{3,4},{4,5},{5,6},{6,7},{7,8},{8,9},{9,10},{10,1... | collective-permute-start | bytes 1179656 | tf_op jit(solution)/shard_map/ppermute | solution.py:1399
  13.9 8.6 %collective-permute-start.1 = (bf16[2,80,768]{2,1,0:T(8,128)(2,1)S(1)}, bf16[2,80,768]{2,1,0:T(8,128)(2,1)S(1)}, u32[]{:S(2)}, u32[]{:S(2)}) collective-permute-start(bf16[2,80,768]{2,1,0:T(8,128)(2,1)S(1)} %pad_maximum_fusion.4), channel_id=1, source_target_pairs={{0,4},{1,5},{2,6},{3,7},{4,0},{5,1},{6,2},{7,3},{8,12},{9,13},{10,... | collective-permute-start | bytes 737288 | tf_op jit(solution)/shard_map/ppermute | solution.py:43
  22.5 20.7 %collective-permute-start.3 = (bf16[4,80,768]{2,1,0:T(8,128)(2,1)S(1)}, bf16[4,80,768]{2,1,0:T(8,128)(2,1)S(1)}, u32[]{:S(2)}, u32[]{:S(2)}) collective-permute-start(bf16[4,80,768]{2,1,0:T(8,128)(2,1)S(1)} %pad_maximum_fusion.3), channel_id=1, source_target_pairs={{0,2},{1,3},{2,0},{3,1},{4,6},{5,7},{6,4},{7,5},{8,10},{9,11},{10,... | collective-permute-start | bytes 1474568 | tf_op jit(solution)/shard_map/ppermute | solution.py:43
  23.8 19.4 %collective-permute-start.5 = (bf16[256,768]{1,0:T(8,128)(2,1)S(1)}, bf16[256,768]{1,0:T(8,128)(2,1)}, u32[]{:S(2)}, u32[]{:S(2)}) collective-permute-start(bf16[256,768]{1,0:T(8,128)(2,1)S(1)} %get-tuple-element.112), channel_id=1, source_target_pairs={{0,1},{1,2},{2,3},{3,4},{4,5},{5,6},{6,7},{7,8},{8,9},{9,10},{10,1... | collective-permute-start | bytes 1179656 | tf_op jit(solution)/shard_map/ppermute | solution.py:1404
  31.4 11.8 %collective-permute-start.4 = (bf16[1,224,768]{2,1,0:T(8,128)(2,1)S(1)}, bf16[1,224,768]{2,1,0:T(8,128)(2,1)S(1)}, u32[]{:S(2)}, u32[]{:S(2)}) collective-permute-start(bf16[1,224,768]{2,1,0:T(8,128)(2,1)S(1)} %slice.154), channel_id=1, source_target_pairs={{0,8},{1,9},{2,10},{3,11},{4,12},{5,13},{6,14},{7,15},{8,0},{9,1},... | collective-permute-start | bytes 1032200 | tf_op jit(solution)/shard_map/ppermute | solution.py:43
  43.3 26.5 %copy-start.2 = (bf16[8,80,768]{2,1,0:T(8,128)(2,1)}, bf16[8,80,768]{2,1,0:T(8,128)(2,1)S(1)}, u32[]{:S(2)}) copy-start(bf16[8,80,768]{2,1,0:T(8,128)(2,1)S(1)} %pad_maximum_fusion.1.low) | copy-start | bytes 2949124
  43.4 22.7 %collective-permute-start.7 = (bf16[8,80,768]{2,1,0:T(8,128)(2,1)S(1)}, bf16[8,80,768]{2,1,0:T(8,128)(2,1)S(1)}, u32[]{:S(2)}, u32[]{:S(2)}) collective-permute-start(bf16[8,80,768]{2,1,0:T(8,128)(2,1)S(1)} %pad_maximum_fusion.1.low), channel_id=1, source_target_pairs={{0,16},{16,0},{1,17},{17,1},{2,18},{18,2},{3,19},{19,3},{4,20},{20... | collective-permute-start | bytes 2949128 | tf_op jit(solution)/shard_map/ppermute | solution.py:47
  43.4 22.6 %collective-permute-start.6 = (bf16[8,80,768]{2,1,0:T(8,128)(2,1)S(1)}, bf16[8,80,768]{2,1,0:T(8,128)(2,1)S(1)}, u32[]{:S(2)}, u32[]{:S(2)}) collective-permute-start(bf16[8,80,768]{2,1,0:T(8,128)(2,1)S(1)} %pad_maximum_fusion.1.low), channel_id=1, source_target_pairs={{0,1},{1,0},{2,3},{3,2},{4,5},{5,4},{6,7},{7,6},{8,9},{9,8},{10,11... | collective-permute-start | bytes 2949128 | tf_op jit(solution)/shard_map/ppermute | solution.py:43
  44.8 21.2 %collective-permute-start.8 = (bf16[2,224,768]{2,1,0:T(8,128)(2,1)S(1)}, bf16[2,224,768]{2,1,0:T(8,128)(2,1)S(1)}, u32[]{:S(2)}, u32[]{:S(2)}) collective-permute-start(bf16[2,224,768]{2,1,0:T(8,128)(2,1)S(1)} %pad_maximum_fusion.2), channel_id=1, source_target_pairs={{0,4},{1,5},{2,6},{3,7},{4,0},{5,1},{6,2},{7,3},{8,12},{9,13},{10,... | collective-permute-start | bytes 2064392 | tf_op jit(solution)/shard_map/ppermute | solution.py:43
  45.6 20.4 %collective-permute-start.9 = (bf16[256,768]{1,0:T(8,128)(2,1)S(1)}, bf16[256,768]{1,0:T(8,128)(2,1)S(1)}, u32[]{:S(2)}, u32[]{:S(2)}) collective-permute-start(bf16[256,768]{1,0:T(8,128)(2,1)S(1)} %get-tuple-element.115), channel_id=1, source_target_pairs={{1,0},{2,1},{3,2},{4,3},{5,4},{6,5},{7,6},{8,7},{9,8},{10,9},{11,1... | collective-permute-start | bytes 1179656 | tf_op jit(solution)/shard_map/ppermute | solution.py:1413
  66.0 2.3 copy-start.16
  66.0 6.6 %copy-start.12 = (bf16[8,80,768]{2,1,0:T(8,128)(2,1)}, bf16[8,80,768]{2,1,0:T(8,128)(2,1)S(1)}, u32[]{:S(2)}) copy-start(bf16[8,80,768]{2,1,0:T(8,128)(2,1)S(1)} %collective-permute-done.7.olow) | copy-start | bytes 2949124
  66.1 6.6 %copy-start.13 = (bf16[8,80,768]{2,1,0:T(8,128)(2,1)}, bf16[8,80,768]{2,1,0:T(8,128)(2,1)S(1)}, u32[]{:S(2)}) copy-start(bf16[8,80,768]{2,1,0:T(8,128)(2,1)S(1)} %collective-permute-done.6.high) | copy-start | bytes 2949124
  66.1 8.1 %collective-permute-start.10 = (bf16[8,80,768]{2,1,0:T(8,128)(2,1)S(1)}, bf16[8,80,768]{2,1,0:T(8,128)(2,1)}, u32[]{:S(2)}, u32[]{:S(2)}) collective-permute-start(bf16[8,80,768]{2,1,0:T(8,128)(2,1)S(1)} %collective-permute-done.6.high), channel_id=1, source_target_pairs={{0,16},{16,0},{1,17},{17,1},{2,18},{18,2},{3,19},{19,3},{4,20},{20... | collective-permute-start | bytes 2949128 | tf_op jit(solution)/shard_map/ppermute | solution.py:47
  68.4 16.2 %collective-permute-start.11 = (bf16[256,768]{1,0:T(8,128)(2,1)S(1)}, bf16[256,768]{1,0:T(8,128)(2,1)}, u32[]{:S(2)}, u32[]{:S(2)}) collective-permute-start(bf16[256,768]{1,0:T(8,128)(2,1)S(1)} %get-tuple-element.124), channel_id=1, source_target_pairs={{1,0},{2,1},{3,2},{4,3},{5,4},{6,5},{7,6},{8,7},{9,8},{10,9},{11,1... | collective-permute-start | bytes 1179656 | tf_op jit(solution)/shard_map/ppermute | solution.py:1419
  69.8 21.8 %collective-permute-start.12 = (bf16[4,224,768]{2,1,0:T(8,128)(2,1)S(1)}, bf16[4,224,768]{2,1,0:T(8,128)(2,1)S(1)}, u32[]{:S(2)}, u32[]{:S(2)}) collective-permute-start(bf16[4,224,768]{2,1,0:T(8,128)(2,1)S(1)} %pad_maximum_fusion), channel_id=1, source_target_pairs={{0,2},{1,3},{2,0},{3,1},{4,6},{5,7},{6,4},{7,5},{8,10},{9,11},{10,... | collective-permute-start | bytes 4128776 | tf_op jit(solution)/shard_map/ppermute | solution.py:43
  72.6 1.5 copy-start.7
  92.8 41.6 %collective-permute-start.14 = (bf16[8,224,768]{2,1,0:T(8,128)(2,1)}, bf16[8,224,768]{2,1,0:T(8,128)(2,1)S(1)}, u32[]{:S(2)}, u32[]{:S(2)}) collective-permute-start(bf16[8,224,768]{2,1,0:T(8,128)(2,1)} %constant_dynamic-update-slice_fusion.low), channel_id=1, source_target_pairs={{0,16},{16,0},{1,17},{17,1},{2,18},{18,2},{3,19},{19,3},{4,20},{20... | collective-permute-start | bytes 8257544 | tf_op jit(solution)/shard_map/ppermute | solution.py:47
  100.7 33.7 %collective-permute-start.13 = (bf16[8,224,768]{2,1,0:T(8,128)(2,1)}, bf16[8,224,768]{2,1,0:T(8,128)(2,1)S(1)}, u32[]{:S(2)}, u32[]{:S(2)}) collective-permute-start(bf16[8,224,768]{2,1,0:T(8,128)(2,1)} %constant_dynamic-update-slice_fusion.low), channel_id=1, source_target_pairs={{0,1},{1,0},{2,3},{3,2},{4,5},{5,4},{6,7},{7,6},{8,9},{9,8},{10,11... | collective-permute-start | bytes 8257544 | tf_op jit(solution)/shard_map/ppermute | solution.py:43
  134.4 6.6 %copy-start.10 = (bf16[8,224,768]{2,1,0:T(8,128)(2,1)}, bf16[8,224,768]{2,1,0:T(8,128)(2,1)S(1)}, u32[]{:S(2)}) copy-start(bf16[8,224,768]{2,1,0:T(8,128)(2,1)S(1)} %collective-permute-done.13.high) | copy-start | bytes 8257540
  134.4 5.1 %collective-permute-start.15 = (bf16[8,224,768]{2,1,0:T(8,128)(2,1)S(1)}, bf16[8,224,768]{2,1,0:T(8,128)(2,1)S(1)}, u32[]{:S(2)}, u32[]{:S(2)}) collective-permute-start(bf16[8,224,768]{2,1,0:T(8,128)(2,1)S(1)} %collective-permute-done.13.high), channel_id=1, source_target_pairs={{0,16},{16,0},{1,17},{17,1},{2,18},{18,2},{3,19},{19,3},{4,20},{20... | collective-permute-start | bytes 8257544 | tf_op jit(solution)/shard_map/ppermute | solution.py:47
  134.4 6.6 %copy-start.9 = (bf16[8,224,768]{2,1,0:T(8,128)(2,1)}, bf16[8,224,768]{2,1,0:T(8,128)(2,1)S(1)}, u32[]{:S(2)}) copy-start(bf16[8,224,768]{2,1,0:T(8,128)(2,1)S(1)} %collective-permute-done.14.olow) | copy-start | bytes 8257540
  176.5 9.3 %collective-permute-start.16 = (bf16[16,224,768]{2,1,0:T(8,128)(2,1)}, bf16[16,224,768]{2,1,0:T(8,128)(2,1)S(1)}, u32[]{:S(2)}, u32[]{:S(2)}) collective-permute-start(bf16[16,224,768]{2,1,0:T(8,128)(2,1)} %get-tuple-element.148), channel_id=1, source_target_pairs={{0,16},{16,0},{1,17},{17,1},{2,18},{18,2},{3,19},{19,3},{4,20},{20... | collective-permute-start | bytes 16515080 | tf_op jit(solution)/shard_map/ppermute | solution.py:47
  176.7 42.7 %collective-permute-start.18 = (bf16[256,896]{1,0:T(8,128)(2,1)}, bf16[256,896]{1,0:T(8,128)(2,1)S(1)}, u32[]{:S(2)}, u32[]{:S(2)}) collective-permute-start(bf16[256,896]{1,0:T(8,128)(2,1)} %get-tuple-element.156), channel_id=1, source_target_pairs={{0,1},{1,2},{2,3},{3,4},{4,5},{5,6},{6,7},{7,8},{8,9},{9,10},{10,1... | collective-permute-start | bytes 1376264 | tf_op jit(solution)/shard_map/ppermute | solution.py:1474
  180.7 38.8 %collective-permute-start.19 = (bf16[256,896]{1,0:T(8,128)(2,1)}, bf16[256,896]{1,0:T(8,128)(2,1)}, u32[]{:S(2)}, u32[]{:S(2)}) collective-permute-start(bf16[256,896]{1,0:T(8,128)(2,1)} %get-tuple-element.157), channel_id=1, source_target_pairs={{1,0},{2,1},{3,2},{4,3},{5,4},{6,5},{7,6},{8,7},{9,8},{10,9},{11,1... | collective-permute-start | bytes 1376264 | tf_op jit(solution)/shard_map/ppermute | solution.py:1475
  185.8 4.5 %copy-start = (bf16[16,224,768]{2,1,0:T(8,128)(2,1)}, bf16[16,224,768]{2,1,0:T(8,128)(2,1)S(1)}, u32[]{:S(2)}) copy-start(bf16[16,224,768]{2,1,0:T(8,128)(2,1)S(1)} %collective-permute-done.16) | copy-start | bytes 16515076
  190.3 42.5 %collective-permute-start.17 = (bf16[8,224,768]{2,1,0:T(8,128)(2,1)S(1)}, bf16[8,224,768]{2,1,0:T(8,128)(2,1)S(1)}, u32[]{:S(2)}, u32[]{:S(2)}) collective-permute-start(bf16[8,224,768]{2,1,0:T(8,128)(2,1)S(1)} %add_convert_fusion), channel_id=1, source_target_pairs={{0,1},{1,0},{2,3},{3,2},{4,5},{5,4},{6,7},{7,6},{8,9},{9,8},{10,11... | collective-permute-start | bytes 8257544 | tf_op jit(solution)/shard_map/ppermute | solution.py:43
  237.4 18.5 %collective-permute-start.21 = (bf16[4,224,768]{2,1,0:T(8,128)(2,1)}, bf16[4,224,768]{2,1,0:T(8,128)(2,1)S(1)}, u32[]{:S(2)}, u32[]{:S(2)}) collective-permute-start(bf16[4,224,768]{2,1,0:T(8,128)(2,1)} %get-tuple-element.208), channel_id=1, source_target_pairs={{0,2},{1,3},{2,0},{3,1},{4,6},{5,7},{6,4},{7,5},{8,10},{9,11},{10,... | collective-permute-start | bytes 4128776 | tf_op jit(solution)/shard_map/ppermute | solution.py:43
  247.3 4.4 %collective-permute-start.20 = (bf16[8,80,768]{2,1,0:T(8,128)(2,1)}, bf16[8,80,768]{2,1,0:T(8,128)(2,1)S(1)}, u32[]{:S(2)}, u32[]{:S(2)}) collective-permute-start(bf16[8,80,768]{2,1,0:T(8,128)(2,1)} %get-tuple-element.172), channel_id=1, source_target_pairs={{0,16},{16,0},{1,17},{17,1},{2,18},{18,2},{3,19},{19,3},{4,20},{20... | collective-permute-start | bytes 2949128 | tf_op jit(solution)/shard_map/ppermute | solution.py:47
  248.7 25.2 %collective-permute-start.24 = (bf16[8,80,768]{2,1,0:T(8,128)(2,1)}, bf16[8,80,768]{2,1,0:T(8,128)(2,1)}, u32[]{:S(2)}, u32[]{:S(2)}) collective-permute-start(bf16[8,80,768]{2,1,0:T(8,128)(2,1)} %get-tuple-element.179), channel_id=1, source_target_pairs={{0,16},{16,0},{1,17},{17,1},{2,18},{18,2},{3,19},{19,3},{4,20},{20... | collective-permute-start | bytes 2949128 | tf_op jit(solution)/shard_map/ppermute | solution.py:47
  256.0 17.9 %collective-permute-start.23 = (bf16[8,80,768]{2,1,0:T(8,128)(2,1)}, bf16[8,80,768]{2,1,0:T(8,128)(2,1)}, u32[]{:S(2)}, u32[]{:S(2)}) collective-permute-start(bf16[8,80,768]{2,1,0:T(8,128)(2,1)} %add_convert_fusion.2), channel_id=1, source_target_pairs={{0,1},{1,0},{2,3},{3,2},{4,5},{5,4},{6,7},{7,6},{8,9},{9,8},{10,11... | collective-permute-start | bytes 2949128 | tf_op jit(solution)/shard_map/ppermute | solution.py:43
  256.8 17.0 %collective-permute-start.22 = (bf16[2,224,768]{2,1,0:T(8,128)(2,1)S(1)}, bf16[2,224,768]{2,1,0:T(8,128)(2,1)S(1)}, u32[]{:S(2)}, u32[]{:S(2)}) collective-permute-start(bf16[2,224,768]{2,1,0:T(8,128)(2,1)S(1)} %get-tuple-element.211), channel_id=1, source_target_pairs={{0,4},{1,5},{2,6},{3,7},{4,0},{5,1},{6,2},{7,3},{8,12},{9,13},{10,... | collective-permute-start | bytes 2064392 | tf_op jit(solution)/shard_map/ppermute | solution.py:43
  258.5 15.3 %copy-start.3 = (bf16[8,80,768]{2,1,0:T(8,128)(2,1)S(1)}, bf16[8,80,768]{2,1,0:T(8,128)(2,1)}, u32[]{:S(2)}) copy-start(bf16[8,80,768]{2,1,0:T(8,128)(2,1)} %get-tuple-element.178) | copy-start | bytes 2949124
  275.7 15.3 %collective-permute-start.26 = (bf16[4,80,768]{2,1,0:T(8,128)(2,1)S(1)}, bf16[4,80,768]{2,1,0:T(8,128)(2,1)S(1)}, u32[]{:S(2)}, u32[]{:S(2)}) collective-permute-start(bf16[4,80,768]{2,1,0:T(8,128)(2,1)S(1)} %get-tuple-element.212), channel_id=1, source_target_pairs={{0,2},{1,3},{2,0},{3,1},{4,6},{5,7},{6,4},{7,5},{8,10},{9,11},{10,... | collective-permute-start | bytes 1474568 | tf_op jit(solution)/shard_map/ppermute | solution.py:43
  279.1 11.9 %collective-permute-start.25 = (bf16[1,224,768]{2,1,0:T(8,128)(2,1)S(1)}, bf16[1,224,768]{2,1,0:T(8,128)(2,1)S(1)}, u32[]{:S(2)}, u32[]{:S(2)}) collective-permute-start(bf16[1,224,768]{2,1,0:T(8,128)(2,1)S(1)} %fusion.5), channel_id=1, source_target_pairs={{0,8},{1,9},{2,10},{3,11},{4,12},{5,13},{6,14},{7,15},{8,0},{9,1},... | collective-permute-start | bytes 1032200 | tf_op jit(solution)/shard_map/ppermute | solution.py:43
  291.1 11.8 %copy-start.4 = (f32[224,768]{1,0:T(8,128)}, f32[224,768]{1,0:T(8,128)S(1)}, u32[]{:S(2)}) copy-start(f32[224,768]{1,0:T(8,128)S(1)} %fusion.4.mine) | copy-start | bytes 2064388
  291.1 8.6 %collective-permute-start.28 = (f32[224,768]{1,0:T(8,128)S(1)}, f32[224,768]{1,0:T(8,128)S(1)}, u32[]{:S(2)}, u32[]{:S(2)}) collective-permute-start(f32[224,768]{1,0:T(8,128)S(1)} %fusion.4.mine), channel_id=1, source_target_pairs={{0,16},{16,0},{1,17},{17,1},{2,18},{18,2},{3,19},{19,3},{4,20},{20... | collective-permute-start | bytes 2064392 | tf_op jit(solution)/shard_map/ppermute | solution.py:47
  291.3 8.5 %collective-permute-start.27 = (bf16[2,80,768]{2,1,0:T(8,128)(2,1)S(1)}, bf16[2,80,768]{2,1,0:T(8,128)(2,1)S(1)}, u32[]{:S(2)}, u32[]{:S(2)}) collective-permute-start(bf16[2,80,768]{2,1,0:T(8,128)(2,1)S(1)} %get-tuple-element.218), channel_id=1, source_target_pairs={{0,4},{1,5},{2,6},{3,7},{4,0},{5,1},{6,2},{7,3},{8,12},{9,13},{10,... | collective-permute-start | bytes 737288 | tf_op jit(solution)/shard_map/ppermute | solution.py:43
  299.7 3.2 %copy-start.14 = (f32[224,768]{1,0:T(8,128)}, f32[224,768]{1,0:T(8,128)S(1)}, u32[]{:S(2)}) copy-start(f32[224,768]{1,0:T(8,128)S(1)} %collective-permute-done.28.other) | copy-start | bytes 2064388
  299.8 6.2 %copy-start.6 = (f32[1,80,768]{2,1,0:T(8,128)}, f32[1,80,768]{2,1,0:T(8,128)S(1)}, u32[]{:S(2)}) copy-start(f32[1,80,768]{2,1,0:T(8,128)S(1)} %get-tuple-element.221) | copy-start | bytes 737284
  299.8 9.7 %collective-permute-start.30 = (f32[1,80,768]{2,1,0:T(8,128)S(1)}, f32[1,80,768]{2,1,0:T(8,128)S(1)}, u32[]{:S(2)}, u32[]{:S(2)}) collective-permute-start(f32[1,80,768]{2,1,0:T(8,128)S(1)} %get-tuple-element.221), channel_id=1, source_target_pairs={{0,16},{16,0},{1,17},{17,1},{2,18},{18,2},{3,19},{19,3},{4,20},{20... | collective-permute-start | bytes 737288 | tf_op jit(solution)/shard_map/ppermute | solution.py:47
  300.1 5.9 %collective-permute-start.31 = (bf16[1,80,768]{2,1,0:T(8,128)(2,1)S(1)}, bf16[1,80,768]{2,1,0:T(8,128)(2,1)S(1)}, u32[]{:S(2)}, u32[]{:S(2)}) collective-permute-start(bf16[1,80,768]{2,1,0:T(8,128)(2,1)S(1)} %get-tuple-element.220), channel_id=1, source_target_pairs={{0,24},{1,25},{2,26},{3,27},{4,28},{5,29},{6,30},{7,31},{8,16},{9,... | collective-permute-start | bytes 368648 | tf_op jit(solution)/shard_map/ppermute | solution.py:1513
  300.7 8.8 %collective-permute-start.29 = (bf16[1,80,768]{2,1,0:T(8,128)(2,1)S(1)}, bf16[1,80,768]{2,1,0:T(8,128)(2,1)S(1)}, u32[]{:S(2)}, u32[]{:S(2)}) collective-permute-start(bf16[1,80,768]{2,1,0:T(8,128)(2,1)S(1)} %get-tuple-element.220), channel_id=1, source_target_pairs={{0,8},{1,9},{2,10},{3,11},{4,12},{5,13},{6,14},{7,15},{8,0},{9,1},... | collective-permute-start | bytes 368648 | tf_op jit(solution)/shard_map/ppermute | solution.py:43
  306.0 3.5 %copy-start.18 = (bf16[1,80,768]{2,1,0:T(8,128)(2,1)}, bf16[1,80,768]{2,1,0:T(8,128)(2,1)S(1)}, u32[]{:S(2)}) copy-start(bf16[1,80,768]{2,1,0:T(8,128)(2,1)S(1)} %collective-permute-done.31) | copy-start | bytes 368644
  (4 other events, 3.7 us)
